TPU v7x, 256 devices: a whole 4x4x8 slice. The times are simulated.
256 devices in a mesh: ctx: 64 (over x, z, core), head: 4 (over y).
Axes of the slice: x: 4, y: 4, z: 8, core: 2. Of those that a mesh axis runs over, the one named last changes fastest.
Arguments:
- queries: bfloat16 [16384, 4096], P('ctx', 'head'), may hold values from -13 to 13
- key_rows: bfloat16 [16384, 4096], P('ctx', 'head'), may hold values from -4 to 4
- value_rows: bfloat16 [16384, 4096], P('ctx', 'head'), may hold values from -14 to 14
- grad_out: bfloat16 [16384, 4096], P('ctx', 'head'), may hold values from -55 to 55
- doc_ids: int32 [16384], P('ctx'), may hold values from 0 to 31, never falling along the last dimension, each value on 1 to 1024 neighbouring positions
- out_gain: float32 [4096], P('head'), may hold values from 0.1 to 1.9
Outputs:
- normed_out: bfloat16 [16384, 4096], P('ctx', 'head')
- grad_query: bfloat16 [16384, 4096], P('ctx', 'head')
- grad_key: bfloat16 [16384, 4096], P('ctx', 'head')
- grad_value: bfloat16 [16384, 4096], P('ctx', 'head')
Inputs may be any that keep to these rules, and one draw needn't show every extreme that they name: Along the tokens doc_ids never falls; each of the 32 documents has 1 to 1024 tokens, and one has exactly 1024.
All inputs are finite; a program needn't handle non-finite values.
Results may differ from a plain program's by a relative error of at most 0.0085.
Values sent between devices are 32-bit elements; how exact they have to be, the bound alone decides.
No kernel may reach another device: no remote copies, remote signals or barrier semaphores. Data moves between devices by JAX's collectives and lax.ppermute only.
A program may use at most 192 MiB of HBM per device.

v0:
```python
import jax
import jax.numpy as jnp
from jax import lax
from jax.sharding import PartitionSpec as P

HEADS = 32
HD = 128


def entering(value, axis, join, neutral, backward):
    count, mine = (lax.axis_size(axis), lax.axis_index(axis))
    pieces = jax.tree.map(lambda part: lax.all_gather(part, axis), value)
    if backward:
        pieces = jax.tree.map(lambda part: part[::-1], pieces)
        mine = count - 1 - mine
    subtotal = jax.tree.map(
        lambda part, zero: jnp.full_like(part, 0) + jnp.asarray(zero, part.dtype), value, neutral
    )

    def step(position, subtotal):
        longer = join(subtotal, jax.tree.map(lambda part: part[position], pieces))
        return jax.tree.map(lambda new, old: jnp.where(position < mine, new, old), longer, subtotal)

    return lax.fori_loop(0, count - 1, step, subtotal)


def join_runs(early, late):
    early_state, early_doc = early
    late_state, late_doc = late
    absent = late_doc < 0
    merged = jnp.where(early_doc == late_doc, early_state + late_state, late_state)
    state = jnp.where(absent, early_state, merged)
    return (state, jnp.where(absent, early_doc, late_doc))


def carried_runs(state, doc, step):
    identity = (jnp.zeros_like(state), jnp.full((), -1, jnp.int32))
    return entering((state, doc), "ctx", join_runs, identity, step < 0)


def local(queries, key_rows, value_rows, grad_out, doc_ids, out_gain):
    rows = queries.shape[0]
    local_heads = queries.shape[1] // HD
    feats = HEADS * HD
    q3 = queries.reshape(rows, local_heads, HD)
    k3 = key_rows.reshape(rows, local_heads, HD)
    v3 = value_rows.reshape(rows, local_heads, HD)
    first_doc = doc_ids[0]
    last_doc = doc_ids[rows - 1]
    in_first = (doc_ids == first_doc)[:, None, None]
    in_last = (doc_ids == last_doc)[:, None, None]
    position = lax.iota(jnp.int32, rows)
    visible = (doc_ids[:, None] == doc_ids[None, :]) & (position[:, None] >= position[None, :])
    zero_half = jnp.zeros((), jnp.bfloat16)
    last_keys = jnp.where(in_last, k3, zero_half)
    block_state = jnp.einsum("shd,she->hde", last_keys, v3, preferred_element_type=jnp.float32)
    carried, prev_doc = carried_runs(block_state, last_doc, 1)
    carried = jnp.where(prev_doc == first_doc, carried, 0.0).astype(jnp.bfloat16)
    scores = jnp.einsum("thd,shd->hts", q3, k3, preferred_element_type=jnp.float32)
    scores = jnp.where(visible[None], scores, 0.0).astype(jnp.bfloat16)
    local_part = jnp.einsum("hts,she->the", scores, v3, preferred_element_type=jnp.float32)
    carried_part = jnp.einsum("thd,hde->the", q3, carried, preferred_element_type=jnp.float32)
    attended = (local_part + jnp.where(in_first, carried_part, 0.0)).astype(jnp.bfloat16)
    att32 = attended.reshape(rows, local_heads * HD).astype(jnp.float32)
    weighted = out_gain * grad_out.astype(jnp.float32)
    square_sum, dot_sum = lax.psum(
        (jnp.sum(att32 * att32, axis=1), jnp.sum(weighted * att32, axis=1)), "head"
    )
    inv_rms = lax.rsqrt(square_sum / feats + 1e-06)
    inner = dot_sum / feats
    normed = (out_gain * att32 * inv_rms[:, None]).astype(jnp.bfloat16)
    grad_att = (
        inv_rms[:, None] * weighted - att32 * (inv_rms * inv_rms * inv_rms * inner)[:, None]
    ).astype(jnp.bfloat16)
    grad3 = grad_att.reshape(rows, local_heads, HD)
    first_queries = jnp.where(in_first, q3, zero_half)
    block_grad = jnp.einsum(
        "thd,the->hde", first_queries, grad3, preferred_element_type=jnp.float32
    )
    later, next_doc = carried_runs(block_grad, first_doc, -1)
    later = jnp.where(next_doc == last_doc, later, 0.0).astype(jnp.bfloat16)
    grad_sc = jnp.einsum("the,she->hts", grad3, v3, preferred_element_type=jnp.float32)
    grad_sc = jnp.where(visible[None], grad_sc, 0.0).astype(jnp.bfloat16)
    grad_q = jnp.einsum("hts,shd->thd", grad_sc, k3, preferred_element_type=jnp.float32)
    grad_q = grad_q + jnp.where(
        in_first,
        jnp.einsum("the,hde->thd", grad3, carried, preferred_element_type=jnp.float32),
        0.0,
    )
    grad_k = jnp.einsum("hts,thd->shd", grad_sc, q3, preferred_element_type=jnp.float32)
    grad_k = grad_k + jnp.where(
        in_last, jnp.einsum("she,hde->shd", v3, later, preferred_element_type=jnp.float32), 0.0
    )
    grad_v = jnp.einsum("hts,the->she", scores, grad3, preferred_element_type=jnp.float32)
    grad_v = grad_v + jnp.where(
        in_last, jnp.einsum("shd,hde->she", k3, later, preferred_element_type=jnp.float32), 0.0
    )
    width = local_heads * HD
    return (
        normed,
        grad_q.reshape(rows, width).astype(jnp.bfloat16),
        grad_k.reshape(rows, width).astype(jnp.bfloat16),
        grad_v.reshape(rows, width).astype(jnp.bfloat16),
    )


def solution(mesh):
    placed = (
        P("ctx", "head"),
        P("ctx", "head"),
        P("ctx", "head"),
        P("ctx", "head"),
        P("ctx"),
        P("head"),
    )
    return jax.shard_map(
        local,
        mesh=mesh,
        in_specs=placed,
        out_specs=(P("ctx", "head"), P("ctx", "head"), P("ctx", "head"), P("ctx", "head")),
        check_vma=False,
    )
```

profile of v0, /device:TPU:1, one launch (start us, length us, event | category | flops | bytes accessed | tf_op | source)
XLA Modules:
  0.0 837.6 jit_solution(5185550907148817818)
XLA Ops:
  15.2 20.9 %all-reduce.2 = (s32[64]{0:T(128)S(1)}, s32[64]{0:T(128)S(1)}) all-reduce(s32[64]{0:T(128)S(1)} %slice_dynamic-update-slice_fusion, s32[64]{0:T(128)S(1)} %get-tuple-element.313), channel_id=1, replica_groups=mesh['ctx'=64,'head'=4] {'ctx'}, use_global_device_ids=true, to_apply=%add | all-reduce | flops 128 | bytes 1024
  38.2 120.8 %all-gather.5.cloned.1.call-done = f32[512,128,128]{2,1,0:T(8,128)} async-done(((f32[8,128,128]{2,1,0:T(8,128)}), f32[512,128,128]{2,1,0:T(8,128)}) %all-gather.5.cloned.1.call-update) | async-done | bytes 33554448 | tf_op jit(solution)/shard_map/all_gather | solution.py:12
  159.0 242.9 %while.32 = (s32[]{:T(128)}, f32[8,128,128]{2,1,0:T(8,128)S(1)}, s32[]{:T(128)}, s32[]{:T(128)}, s32[64]{0:T(128)S(1)}, /*index=5*/f32[64,8,128,128]{3,2,1,0:T(8,128)}, s32[]{:T(128)}, s32[]{:T(128)}) while((s32[]{:T(128)}, f32[8,128,128]{2,1,0:T(8,128)S(1)}, s32[]{:T(128)}, s32[]{:T(128)}, s32[64]{0:T(128)S(1)}, ...), condition=%wide.region_1.2_spmd.clone, body=%wide.region_0.1_spmd.clone.sunk | while | flops 655368 | bytes 1573031 | solution.py:24
  160.9 1.3 select_select_fusion.4
  164.7 1.3 select_select_fusion.4
  168.6 1.3 select_select_fusion.4
  172.4 1.3 select_select_fusion.4
  176.3 1.3 select_select_fusion.4
  180.2 1.3 select_select_fusion.4
  184.0 1.3 select_select_fusion.4
  187.9 1.3 select_select_fusion.4
  191.7 1.3 select_select_fusion.4
  195.6 1.3 select_select_fusion.4
  199.4 1.3 select_select_fusion.4
  203.3 1.3 select_select_fusion.4
  207.1 1.3 select_select_fusion.4
  211.0 1.3 select_select_fusion.4
  214.9 1.3 select_select_fusion.4
  218.7 1.3 select_select_fusion.4
  222.6 1.3 select_select_fusion.4
  226.4 1.3 select_select_fusion.4
  230.3 1.3 select_select_fusion.4
  238.0 1.3 select_select_fusion.4
  257.3 1.3 select_select_fusion.4
  272.7 1.3 select_select_fusion.4
  276.6 1.3 select_select_fusion.4
  292.0 1.3 select_select_fusion.4
  295.8 1.3 select_select_fusion.4
  311.3 1.3 select_select_fusion.4
  330.5 1.3 select_select_fusion.4
  346.0 1.3 select_select_fusion.4
  349.8 1.3 select_select_fusion.4
  365.3 1.3 select_select_fusion.4
  369.1 1.3 select_select_fusion.4
  384.5 1.3 select_select_fusion.4
  402.6 1.3 multiply_reduce_fusion.1
  403.9 1.6 copy.41
  406.7 8.5 %all-reduce.3 = (f32[256]{0:T(256)S(1)}, f32[256]{0:T(256)S(1)}) all-reduce(f32[256]{0:T(256)S(1)} %get-tuple-element.315, f32[256]{0:T(256)S(1)} %multiply_reduce_fusion), channel_id=1, replica_groups=mesh['ctx'=64,'head'=4] {'head'}, use_global_device_ids=true, to_apply=%region_3.4 | all-reduce | flops 512 | bytes 4096 | tf_op jit(solution)/shard_map/psum | solution.py:66
  415.2 2.3 subtract_convert_fusion
  422.4 2.6 fusion.41
  425.3 133.2 %all-gather.7.cloned.1.call-done = f32[512,128,128]{2,1,0:T(8,128)} async-done(((f32[8,128,128]{2,1,0:T(8,128)}), f32[512,128,128]{2,1,0:T(8,128)}) %all-gather.7.cloned.1.call-update) | async-done | bytes 33554448 | tf_op jit(solution)/shard_map/all_gather | solution.py:12
  558.6 23.0 %rev.7 = f32[64,8,128,128]{3,2,1,0:T(8,128)} reverse(f32[64,8,128,128]{3,2,1,0:T(8,128)} %bitcast.101), dimensions={0} | reverse | bytes 67108864 | tf_op jit(solution)/shard_map/rev | solution.py:14
  581.6 243.0 %while.33 = (s32[]{:T(128)}, f32[8,128,128]{2,1,0:T(8,128)S(1)}, s32[]{:T(128)}, s32[]{:T(128)}, s32[64]{0:T(128)S(1)}, /*index=5*/f32[64,8,128,128]{3,2,1,0:T(8,128)}, s32[]{:T(128)}, s32[]{:T(128)}) while((s32[]{:T(128)}, f32[8,128,128]{2,1,0:T(8,128)S(1)}, s32[]{:T(128)}, s32[]{:T(128)}, s32[64]{0:T(128)S(1)}, ...), condition=%wide.region_7.8_spmd.clone, body=%wide.region_6.7_spmd.clone.sunk | while | flops 655368 | bytes 1573031 | solution.py:24
  602.8 1.3 select_select_fusion.5
  606.6 1.3 select_select_fusion.5
  610.5 1.3 select_select_fusion.5
  637.5 1.3 select_select_fusion.5
  641.3 1.3 select_select_fusion.5
  645.2 1.3 select_select_fusion.5
  676.0 1.3 select_select_fusion.5
  679.9 1.3 select_select_fusion.5
  683.8 1.3 select_select_fusion.5
  710.8 1.3 select_select_fusion.5
  714.6 1.3 select_select_fusion.5
  718.5 1.3 select_select_fusion.5
  749.3 1.3 select_select_fusion.5
  753.2 1.3 select_select_fusion.5
  757.0 1.3 select_select_fusion.5
  784.0 1.3 select_select_fusion.5
  787.9 1.3 select_select_fusion.5
  791.8 1.3 select_select_fusion.5
  822.6 1.3 select_select_fusion.5
  825.2 2.2 fusion.7
  827.4 2.0 copy.57
  (250 shorter events, 188.4 us)
Async XLA Ops:
  7.2 4.8 copy-start
  7.2 1.6 copy-start.8
  7.2 2.2 copy-start.7
  7.2 151.8 %all-gather.5.cloned.1.call-start = ((), (), s32[]{:S(2)}) async-start(), calls=%async_computation | async-start | bytes 34078720 | tf_op jit(solution)/shard_map/all_gather | solution.py:12
  8.4 27.8 %copy-start.5 = (bf16[256,1024]{1,0:T(8,128)(2,1)S(1)}, bf16[256,1024]{1,0:T(8,128)(2,1)}, u32[]{:S(2)}) copy-start(bf16[256,1024]{1,0:T(8,128)(2,1)} %param.11) | copy-start | bytes 1572868
  13.1 545.5 %all-gather.7.cloned.1.call-start = ((), (), s32[]{:S(2)}) async-start(), calls=%async_computation.1 | async-start | bytes 34078720 | tf_op jit(solution)/shard_map/all_gather | solution.py:12
  36.7 1.0 copy-start.2
  402.5 2.9 copy-start.6
  420.5 1.0 copy-start.3
  422.4 2.6 copy-start.4
  581.6 243.6 %copy-start.1 = (f32[8,128,256]{2,1,0:T(8,128)S(1)}, f32[8,128,256]{2,1,0:T(8,128)}, u32[]{:S(2)}) copy-start(f32[8,128,256]{2,1,0:T(8,128)} %fusion.41) | copy-start | bytes 3145732
Sparse Core Ops, SparseCore 0:
  13.2 145.7 all-gather.4
  420.0 138.5 all-gather.6
where the time goes:
time: 848 us; the launch traced here: 838 us
  waiting for transfers between devices  254 us (30%)
  loops' own time  249 us (29%)
  other arithmetic  168 us (20%)
  local copies, waits for them, and re-layouts  110 us (13%)
  blocking collectives  29.4 us (3%)
  between operations  15.6 us (2%)
  matrix products  11.1 us (1%)
    all_gather x2, waiting for transfers between devices, entering(): pieces = jax.tree.map(lambda part: lax.all_gather(part, axis), value)  254 us
    another operation x2, loops' own time, entering(): return lax.fori_loop(0, count - 1, step, subtotal)  249 us
    select_n x126, other arithmetic, step(): jnp.where(position < mine, new, old)  163 us
    dynamic_slice x126, local copies, waits for them, and re-layouts, step(): longer = join(subtotal, jax.tree.map(lambda part: part[position], pieces))  73.9 us
    rev x2, local copies, waits for them, and re-layouts, entering(): pieces = jax.tree.map(lambda part: part[::-1], pieces)  23.1 us
    unnamed x1, blocking collectives  20.9 us
  transfers between devices with their start and end apart: 2, of which 2 were waited for; matrix products, arithmetic and copies ran while one was open for 1% of the time, Pallas kernels for 0%

commit v1 on v0

v1 whole, which is shorter than its diff:
```python
import jax
import jax.numpy as jnp
from jax import lax
from jax.experimental import pallas as pl
from jax.experimental.pallas import tpu as pltpu
from jax.sharding import PartitionSpec as P

HEADS = 32
HD = 128
TAG = 8
F32 = jnp.float32
BF16 = jnp.bfloat16


def dot(a, b, dims):
    return lax.dot_general(a, b, (dims, ((), ())), preferred_element_type=F32)


NN = ((1,), (0,))
NT = ((1,), (1,))
TN = ((0,), (0,))


def as_column(row):
    return jnp.transpose(jnp.broadcast_to(row, (HD, row.shape[1])))


def head(h):
    return slice(h * HD, (h + 1) * HD)


def in_doc(row_ref, which):
    return (as_column(row_ref[...].astype(F32)) == which.astype(F32)).astype(F32)


def visible(row_ref):
    rows = row_ref.shape[1]
    row = row_ref[...].astype(F32)
    column = as_column(row)
    column = jnp.concatenate([column] * (rows // HD), axis=1)
    t = lax.broadcasted_iota(jnp.int32, (rows, rows), 0)
    s = lax.broadcasted_iota(jnp.int32, (rows, rows), 1)
    return (column == jnp.broadcast_to(row, (rows, rows))) & (t >= s)


def state_kernel(ids, row, k, v, out):
    rows = k.shape[0]
    last = ids[rows - 1]
    keep = in_doc(row, last).astype(BF16)
    for h in range(k.shape[1] // HD):
        out[head(h), :] = dot(k[:, head(h)] * keep, v[:, head(h)], TN)
    out[k.shape[1]:, :] = jnp.full((TAG, HD), last.astype(F32))


def local_kernel(row, q, k, v, after, scores, part):
    del after
    seen = visible(row)
    for h in range(q.shape[1] // HD):
        sc = dot(q[:, head(h)], k[:, head(h)], NT)
        sc = jnp.where(seen, sc, 0.0).astype(BF16)
        scores[h] = sc
        part[:, head(h)] = dot(sc, v[:, head(h)], NN)


def attend_kernel(ids, row, q, part, came, grad, gain, attended, carried, stats):
    rows, width = q.shape
    first = ids[0]
    keep = in_doc(row, first)
    same = came[width:width + 1, :] == first.astype(F32)
    square = jnp.zeros((rows, HD), F32)
    inner = jnp.zeros((rows, HD), F32)
    for h in range(width // HD):
        state = jnp.where(same, came[head(h), :], 0.0).astype(BF16)
        carried[head(h), :] = state
        att = (part[:, head(h)] + keep * dot(q[:, head(h)], state, NN)).astype(BF16)
        attended[:, head(h)] = att
        att = att.astype(F32)
        square = square + att * att
        inner = inner + gain[:, head(h)] * grad[:, head(h)].astype(F32) * att
    ones = jnp.ones((TAG, HD), F32)
    upper = lax.broadcasted_iota(jnp.int32, (TAG, rows), 0) < TAG // 2
    exact = lax.Precision.HIGHEST
    sums = [
        lax.dot_general(ones, x, (NT, ((), ())), precision=exact, preferred_element_type=F32)
        for x in (square, inner)
    ]
    stats[...] = jnp.where(upper, sums[0], sums[1])


def norm_scales(stats):
    feats = HEADS * HD
    inv = lax.rsqrt(stats[0:1, :] / feats + 1e-06)
    back = inv * inv * inv * (stats[TAG - 1:TAG, :] / feats)
    return as_column(inv), as_column(back)


def grad_kernel(ids, row, q, attended, grad, gain, stats, g_out, out):
    rows, width = q.shape
    first = ids[0]
    keep = in_doc(row, first).astype(BF16)
    inv, back = norm_scales(stats[...])
    for h in range(width // HD):
        weighted = gain[:, head(h)] * grad[:, head(h)].astype(F32)
        g = (inv * weighted - attended[:, head(h)].astype(F32) * back).astype(BF16)
        g_out[:, head(h)] = g
        out[head(h), :] = dot(q[:, head(h)] * keep, g, TN)
    out[width:, :] = jnp.full((TAG, HD), first.astype(F32))


def back_kernel(ids, row, q, k, v, g, scores, attended, carried, gain, stats, after,
                normed, grad_q, part_k, part_v):
    del after
    rows, width = q.shape
    keep = in_doc(row, ids[0])
    seen = visible(row)
    inv, _ = norm_scales(stats[...])
    for h in range(width // HD):
        gh = g[:, head(h)]
        normed[:, head(h)] = (gain[:, head(h)] * attended[:, head(h)].astype(F32) * inv).astype(BF16)
        gs = dot(gh, v[:, head(h)], NT)
        gs = jnp.where(seen, gs, 0.0).astype(BF16)
        whole = dot(gs, k[:, head(h)], NN) + keep * dot(gh, carried[head(h), :], NT)
        grad_q[:, head(h)] = whole.astype(BF16)
        part_k[:, head(h)] = dot(gs, q[:, head(h)], TN)
        part_v[:, head(h)] = dot(scores[h], gh, TN)


def last_kernel(ids, row, k, v, part_k, part_v, came, grad_k, grad_v):
    rows, width = k.shape
    last = ids[rows - 1]
    keep = in_doc(row, last)
    same = came[width:width + 1, :] == last.astype(F32)
    for h in range(width // HD):
        later = jnp.where(same, came[head(h), :], 0.0).astype(BF16)
        grad_k[:, head(h)] = (part_k[:, head(h)] + keep * dot(v[:, head(h)], later, NT)).astype(BF16)
        grad_v[:, head(h)] = (part_v[:, head(h)] + keep * dot(k[:, head(h)], later, NN)).astype(BF16)


def call(kernel, outs, *args, smem=0):
    specs = [pl.BlockSpec(memory_space=pltpu.SMEM)] * smem
    specs += [pl.BlockSpec(memory_space=pltpu.VMEM)] * (len(args) - smem)
    out_specs = [pl.BlockSpec(memory_space=pltpu.VMEM)] * len(outs)
    return pl.pallas_call(
        kernel,
        out_shape=[jax.ShapeDtypeStruct(shape, kind) for shape, kind in outs],
        in_specs=specs,
        out_specs=out_specs,
        compiler_params=pltpu.CompilerParams(vmem_limit_bytes=40 * 1024 * 1024),
        name=kernel.__name__,
    )(*args)


def joined(mine, came):
    width = mine.shape[0] - TAG
    same = mine[width, 0] == came[width, 0]
    inside = lax.broadcasted_iota(jnp.int32, mine.shape, 0) < width
    return mine + jnp.where(same & inside, came, 0.0)


def carry(states, blocks, backward):
    chips = blocks // 2

    def hop(value, source, target, apart):
        pairs = [
            (2 * c + source, 2 * (c + apart) + target) for c in range(chips) if c + apart < chips
        ]
        if backward:
            pairs = [(blocks - 1 - a, blocks - 1 - b) for a, b in pairs]
        return lax.ppermute(value, "ctx", pairs)

    both = joined(states, hop(states, 0, 1, 0))
    window = joined(both, hop(both, 1, 1, 1))
    entering = hop(window, 1, 0, 1)
    passed = hop(joined(states, entering), 0, 1, 0)
    return entering + passed, both


def local(queries, key_rows, value_rows, grad_out, doc_ids, out_gain):
    rows, width = queries.shape
    heads = width // HD
    blocks = lax.axis_size("ctx")
    ranks = lax.axis_size("head")
    row = doc_ids.reshape(1, rows)
    gain = out_gain.reshape(1, width)
    wide, half, state = ((rows, width), F32), ((rows, width), BF16), ((width + TAG, HD), F32)

    (states,) = call(state_kernel, [state], doc_ids, row, key_rows, value_rows, smem=1)
    came, both = carry(states, blocks, False)
    scores, part = call(
        local_kernel, [((heads, rows, rows), BF16), wide],
        row, queries, key_rows, value_rows, both[width:],
    )
    attended, carried, stats = call(
        attend_kernel, [half, ((width, HD), BF16), ((TAG, rows), F32)],
        doc_ids, row, queries, part, came, grad_out, gain, smem=1,
    )
    total = stats
    for apart in range(1, ranks):
        total = total + lax.ppermute(
            stats, "head", [(i, (i + apart) % ranks) for i in range(ranks)]
        )
    g, grads = call(
        grad_kernel, [half, state],
        doc_ids, row, queries, attended, grad_out, gain, total, smem=1,
    )
    came, both = carry(grads, blocks, True)
    normed, grad_q, part_k, part_v = call(
        back_kernel, [half, half, wide, wide],
        doc_ids, row, queries, key_rows, value_rows, g, scores, attended, carried, gain, total,
        both[width:], smem=1,
    )
    grad_k, grad_v = call(
        last_kernel, [half, half],
        doc_ids, row, key_rows, value_rows, part_k, part_v, came, smem=1,
    )
    return normed, grad_q, grad_k, grad_v


def solution(mesh):
    cut = P("ctx", "head")
    return jax.shard_map(
        local,
        mesh=mesh,
        in_specs=(cut, cut, cut, cut, P("ctx"), P("head")),
        out_specs=(cut, cut, cut, cut),
        check_vma=False,
    )
```

time: 848 us -> 91 us (0.11)
  the two profiles are of different devices: /device:TPU:1 before, /device:TPU:7 now
where the time goes in v1:
time: 91 us; the launch traced here: 90.5 us
  waiting for transfers between devices  42.5 us (47%)
  starting transfers between devices  18.9 us (21%)
  Pallas kernels  10.5 us (12%)
  between operations  8.68 us (10%)
  local copies, waits for them, and re-layouts  8.51 us (9%)
  other arithmetic  1.44 us (2%)
    ppermute x8, waiting for transfers between devices, hop(): return lax.ppermute(value, 'ctx', pairs)  39.4 us
    ppermute x8, starting transfers between devices, hop(): return lax.ppermute(value, 'ctx', pairs)  15.1 us
    pallas_call x6, Pallas kernels, call(): pl.pallas_call(kernel, out_shape=[jax.ShapeDtypeStruct(shape, kind) for s...  10.5 us
    slice x10, local copies, waits for them, and re-layouts, joined(): same = mine[width, 0] == came[width, 0]  5.12 us
    ppermute x3, starting transfers between devices, local(): lax.ppermute(stats, 'head', [(i, (i + apart) % ranks) for i in range(rank...  3.8 us
    unnamed x14, local copies, waits for them, and re-layouts  3.38 us
    ppermute x3, waiting for transfers between devices, local(): lax.ppermute(stats, 'head', [(i, (i + apart) % ranks) for i in range(rank...  3.05 us
  transfers between devices with their start and end apart: 11, of which 8 were waited for; matrix products, arithmetic and copies ran while one was open for 2% of the time, Pallas kernels for 5%

profile of v1, /device:TPU:7, one launch (start us, length us, event | category | flops | bytes accessed | tf_op | source)
XLA Modules:
  0.0 90.5 jit_solution(2730084904590722565)
XLA Ops:
  0.6 0.0 copy-start.5
  0.6 0.7 copy-done.5
  1.3 0.0 copy-start.1
  1.3 1.0 %copy-done.1 = bf16[256,1024]{1,0:T(8,128)(2,1)S(1)} copy-done((bf16[256,1024]{1,0:T(8,128)(2,1)S(1)}, bf16[256,1024]{1,0:T(8,128)(2,1)}, u32[]{:S(2)}) %copy-start.1) | copy-done | bytes 524312
  2.4 0.0 copy-start.2
  2.4 1.0 %copy-done.2 = bf16[256,1024]{1,0:T(8,128)(2,1)S(1)} copy-done((bf16[256,1024]{1,0:T(8,128)(2,1)S(1)}, bf16[256,1024]{1,0:T(8,128)(2,1)}, u32[]{:S(2)}) %copy-start.2) | copy-done | bytes 524312
  3.4 1.0 %state_kernel.1 = f32[1032,128]{1,0:T(8,128)S(1)} custom-call(s32[256]{0:T(256)S(1)} %copy-done.5, s32[1,256]{1,0:T(1,128)S(1)} %bitcast.8, bf16[256,1024]{1,0:T(8,128)(2,1)S(1)} %copy-done.1, bf16[256,1024]{1,0:T(8,128)(2,1)S(1)} %copy-done.2), custom_call_target="tpu_custom_call" | custom-call | tf_op jit(solution)/shard_map/state_kernel/pallas_call | solution.py:143
  4.4 1.3 %collective-permute-start = (f32[1032,128]{1,0:T(8,128)S(1)}, f32[1032,128]{1,0:T(8,128)S(1)}, u32[]{:S(2)}, u32[]{:S(2)}) collective-permute-start(f32[1032,128]{1,0:T(8,128)S(1)} %state_kernel.1), channel_id=1, source_target_pairs={{0,4},{8,12},{16,20},{24,28},{32,36},{40,44},{48,52},{56,60},{64,6... | collective-permute-start | bytes 1585160 | tf_op jit(solution)/shard_map/ppermute | solution.py:169
  5.7 0.5 slice.50
  6.2 2.0 %collective-permute-done = f32[1032,128]{1,0:T(8,128)S(1)} collective-permute-done((f32[1032,128]{1,0:T(8,128)S(1)}, f32[1032,128]{1,0:T(8,128)S(1)}, u32[]{:S(2)}, u32[]{:S(2)}) %collective-permute-start) | collective-permute-done | bytes 528416 | tf_op jit(solution)/shard_map/ppermute | solution.py:169
  8.2 0.5 slice.51
  10.0 0.2 select_add_fusion.5
  10.2 3.5 %collective-permute-start.1 = (f32[1032,128]{1,0:T(8,128)S(1)}, f32[1032,128]{1,0:T(8,128)S(1)}, u32[]{:S(2)}, u32[]{:S(2)}) collective-permute-start(f32[1032,128]{1,0:T(8,128)S(1)} %select_add_fusion.5), channel_id=1, source_target_pairs={{4,12},{12,20},{20,28},{28,36},{36,44},{44,52},{52,60},{60,68},{68... | collective-permute-start | bytes 1585160 | tf_op jit(solution)/shard_map/ppermute | solution.py:169
  13.8 0.5 slice.53
  14.3 10.3 %collective-permute-done.1 = f32[1032,128]{1,0:T(8,128)S(1)} collective-permute-done((f32[1032,128]{1,0:T(8,128)S(1)}, f32[1032,128]{1,0:T(8,128)S(1)}, u32[]{:S(2)}, u32[]{:S(2)}) %collective-permute-start.1) | collective-permute-done | bytes 528416 | tf_op jit(solution)/shard_map/ppermute | solution.py:169
  24.6 0.5 slice.54
  26.4 0.2 select_add_fusion.4
  26.6 1.3 %collective-permute-start.2 = (f32[1032,128]{1,0:T(8,128)S(1)}, f32[1032,128]{1,0:T(8,128)S(1)}, u32[]{:S(2)}, u32[]{:S(2)}) collective-permute-start(f32[1032,128]{1,0:T(8,128)S(1)} %select_add_fusion.4), channel_id=1, source_target_pairs={{4,8},{12,16},{20,24},{28,32},{36,40},{44,48},{52,56},{60,64},{68,... | collective-permute-start | bytes 1585160 | tf_op jit(solution)/shard_map/ppermute | solution.py:169
  28.0 6.1 %collective-permute-done.2 = f32[1032,128]{1,0:T(8,128)S(1)} collective-permute-done((f32[1032,128]{1,0:T(8,128)S(1)}, f32[1032,128]{1,0:T(8,128)S(1)}, u32[]{:S(2)}, u32[]{:S(2)}) %collective-permute-start.2) | collective-permute-done | bytes 528416 | tf_op jit(solution)/shard_map/ppermute | solution.py:169
  34.1 0.5 slice.55
  35.9 0.0 copy-start
  35.9 0.2 select_add_fusion.3
  36.1 1.3 %collective-permute-start.3 = (f32[1032,128]{1,0:T(8,128)S(1)}, f32[1032,128]{1,0:T(8,128)S(1)}, u32[]{:S(2)}, u32[]{:S(2)}) collective-permute-start(f32[1032,128]{1,0:T(8,128)S(1)} %select_add_fusion.3), channel_id=1, source_target_pairs={{0,4},{8,12},{16,20},{24,28},{32,36},{40,44},{48,52},{56,60},{64,6... | collective-permute-start | bytes 1585160 | tf_op jit(solution)/shard_map/ppermute | solution.py:169
  37.4 0.0 copy-done
  37.5 0.9 %local_kernel.1 = (bf16[8,256,256]{2,1,0:T(8,128)(2,1)S(1)}, f32[256,1024]{1,0:T(8,128)S(1)}) custom-call(s32[1,256]{1,0:T(1,128)S(1)} %bitcast.9, bf16[256,1024]{1,0:T(8,128)(2,1)S(1)} %copy-done, bf16[256,1024]{1,0:T(8,128)(2,1)S(1)} %copy-done.1, bf16[256,1024]{1,0:T(8,128)(2,1)S(1)} %copy-done.2, f32[8,128]{1,0:T(8,128)S(1)} %slice.52.after), custom_call_target="tpu_custom_call" | custom-call | tf_op jit(solution)/shard_map/local_kernel/pallas_call | solution.py:143
  38.4 0.0 copy-start.4
  38.4 3.0 %collective-permute-done.3 = f32[1032,128]{1,0:T(8,128)S(1)} collective-permute-done((f32[1032,128]{1,0:T(8,128)S(1)}, f32[1032,128]{1,0:T(8,128)S(1)}, u32[]{:S(2)}, u32[]{:S(2)}) %collective-permute-start.3) | collective-permute-done | bytes 528416 | tf_op jit(solution)/shard_map/ppermute | solution.py:169
  41.4 0.0 copy-start.6
  41.4 0.1 add.36.came
  41.5 0.0 copy-done.4
  41.5 0.6 copy-done.6
  42.1 1.4 %attend_kernel.1 = (bf16[256,1024]{1,0:T(8,128)(2,1)S(1)}, bf16[1024,128]{1,0:T(8,128)(2,1)S(1)}, f32[8,256]{1,0:T(8,128)S(1)}) custom-call(s32[256]{0:T(256)S(1)} %copy-done.5, s32[1,256]{1,0:T(1,128)S(1)} %bitcast.10, bf16[256,1024]{1,0:T(8,128)(2,1)S(1)} %copy-done, f32[256,1024]{1,0:T(8,128)S(1)} %get-tuple-element.17.part, f32[1032,128]{1,0:T(8,128)S(1)} %add.36.came, ...), custom_call_target="tpu_custom_call" | custom-call | tf_op jit(solution)/shard_map/attend_kernel/pallas_call | solution.py:143
  43.5 2.8 %collective-permute-start.6 = (f32[8,256]{1,0:T(8,128)S(1)}, f32[8,256]{1,0:T(8,128)S(1)}, u32[]{:S(2)}, u32[]{:S(2)}) collective-permute-start(f32[8,256]{1,0:T(8,128)S(1)} %get-tuple-element.19), channel_id=1, source_target_pairs={{0,3},{1,0},{2,1},{3,2},{4,7},{5,4},{6,5},{7,6},{8,11},{9,8},{10,9... | collective-permute-start | bytes 24584 | tf_op jit(solution)/shard_map/ppermute | solution.py:199
  46.2 0.3 collective-permute-start.5
  46.6 0.7 collective-permute-start.4
  47.3 0.0 collective-permute-done.6
  47.3 3.0 %collective-permute-done.5 = f32[8,256]{1,0:T(8,128)S(1)} collective-permute-done((f32[8,256]{1,0:T(8,128)S(1)}, f32[8,256]{1,0:T(8,128)S(1)}, u32[]{:S(2)}, u32[]{:S(2)}) %collective-permute-start.5) | collective-permute-done | bytes 8224 | tf_op jit(solution)/shard_map/ppermute | solution.py:199
  50.2 0.1 collective-permute-done.4
  50.3 1.2 %grad_kernel.1 = (bf16[256,1024]{1,0:T(8,128)(2,1)S(1)}, f32[1032,128]{1,0:T(8,128)S(1)}) custom-call(s32[256]{0:T(256)S(1)} %copy-done.5, s32[1,256]{1,0:T(1,128)S(1)} %bitcast.11, bf16[256,1024]{1,0:T(8,128)(2,1)S(1)} %copy-done, bf16[256,1024]{1,0:T(8,128)(2,1)S(1)} %get-tuple-element.18.attended, bf16[256,1024]{1,0:T(8,128)(2,1)S(1)} %copy-done.4, ...), custom_call_target="tpu_custom_call" | custom-call | tf_op jit(solution)/shard_map/grad_kernel/pallas_call | solution.py:143
  51.5 3.8 %collective-permute-start.7 = (f32[1032,128]{1,0:T(8,128)S(1)}, f32[1032,128]{1,0:T(8,128)S(1)}, u32[]{:S(2)}, u32[]{:S(2)}) collective-permute-start(f32[1032,128]{1,0:T(8,128)S(1)} %get-tuple-element.23), channel_id=1, source_target_pairs={{252,248},{244,240},{236,232},{228,224},{220,216},{212,208},{204,2... | collective-permute-start | bytes 1585160 | tf_op jit(solution)/shard_map/ppermute | solution.py:169
  55.3 0.5 slice.44
  55.8 1.0 %collective-permute-done.7 = f32[1032,128]{1,0:T(8,128)S(1)} collective-permute-done((f32[1032,128]{1,0:T(8,128)S(1)}, f32[1032,128]{1,0:T(8,128)S(1)}, u32[]{:S(2)}, u32[]{:S(2)}) %collective-permute-start.7) | collective-permute-done | bytes 528416 | tf_op jit(solution)/shard_map/ppermute | solution.py:169
  56.8 0.5 slice.56
  58.6 0.2 select_add_fusion.2
  58.9 0.7 collective-permute-start.8
  59.6 0.5 slice.58
  60.1 0.0 collective-permute-done.8
  60.1 0.5 slice.59
  61.9 0.2 select_add_fusion.1
  62.1 1.3 %collective-permute-start.9 = (f32[1032,128]{1,0:T(8,128)S(1)}, f32[1032,128]{1,0:T(8,128)S(1)}, u32[]{:S(2)}, u32[]{:S(2)}) collective-permute-start(f32[1032,128]{1,0:T(8,128)S(1)} %select_add_fusion.1), channel_id=1, source_target_pairs={{248,244},{240,236},{232,228},{224,220},{216,212},{208,204},{200,1... | collective-permute-start | bytes 1585160 | tf_op jit(solution)/shard_map/ppermute | solution.py:169
  63.4 17.1 %collective-permute-done.9 = f32[1032,128]{1,0:T(8,128)S(1)} collective-permute-done((f32[1032,128]{1,0:T(8,128)S(1)}, f32[1032,128]{1,0:T(8,128)S(1)}, u32[]{:S(2)}, u32[]{:S(2)}) %collective-permute-start.9) | collective-permute-done | bytes 528416 | tf_op jit(solution)/shard_map/ppermute | solution.py:169
  80.5 0.5 slice.60
  82.3 0.0 copy-start.3
  82.3 0.2 select_add_fusion
  82.5 1.9 %collective-permute-start.10 = (f32[1032,128]{1,0:T(8,128)S(1)}, f32[1032,128]{1,0:T(8,128)S(1)}, u32[]{:S(2)}, u32[]{:S(2)}) collective-permute-start(f32[1032,128]{1,0:T(8,128)S(1)} %select_add_fusion), channel_id=1, source_target_pairs={{252,248},{244,240},{236,232},{228,224},{220,216},{212,208},{204,2... | collective-permute-start | bytes 1585160 | tf_op jit(solution)/shard_map/ppermute | solution.py:169
  84.4 0.0 copy-done.3
  84.4 4.0 %back_kernel.1 = (bf16[256,1024]{1,0:T(8,128)(2,1)}, bf16[256,1024]{1,0:T(8,128)(2,1)}, f32[256,1024]{1,0:T(8,128)S(1)}, f32[256,1024]{1,0:T(8,128)S(1)}) custom-call(s32[256]{0:T(256)S(1)} %copy-done.5, s32[1,256]{1,0:T(1,128)S(1)} %bitcast.12, bf16[256,1024]{1,0:T(8,128)(2,1)S(1)} %copy-done, bf16[256,1024]{1,0:T(8,128)(2,1)S(1)} %copy-done.1, ...), custom_call_target="tpu_custom_call" | custom-call | tf_op jit(solution)/shard_map/back_kernel/pallas_call | solution.py:143
  88.4 0.0 collective-permute-done.10
  88.4 0.1 add.43.came
  88.5 2.0 %last_kernel.1 = (bf16[256,1024]{1,0:T(8,128)(2,1)}, bf16[256,1024]{1,0:T(8,128)(2,1)}) custom-call(s32[256]{0:T(256)S(1)} %copy-done.5, s32[1,256]{1,0:T(1,128)S(1)} %bitcast.13, bf16[256,1024]{1,0:T(8,128)(2,1)S(1)} %copy-done.1, bf16[256,1024]{1,0:T(8,128)(2,1)S(1)} %copy-done.3, f32[256,1024]{1,0:T(8,128)S(1)} %get-tuple-element.26.part_k, ...), custom_call_target="tpu_custom_call" | custom-call | tf_op jit(solution)/shard_map/last_kernel/pallas_call | solution.py:143
  (9 shorter events, 0.1 us)
Async XLA Ops:
  0.6 0.7 copy-start.5
  1.3 1.0 %copy-start.1 = (bf16[256,1024]{1,0:T(8,128)(2,1)S(1)}, bf16[256,1024]{1,0:T(8,128)(2,1)}, u32[]{:S(2)}) copy-start(bf16[256,1024]{1,0:T(8,128)(2,1)} %k.7) | copy-start | bytes 1572868
  2.4 1.0 %copy-start.2 = (bf16[256,1024]{1,0:T(8,128)(2,1)S(1)}, bf16[256,1024]{1,0:T(8,128)(2,1)}, u32[]{:S(2)}) copy-start(bf16[256,1024]{1,0:T(8,128)(2,1)} %v.7) | copy-start | bytes 1572868
  4.4 3.8 %collective-permute-start = (f32[1032,128]{1,0:T(8,128)S(1)}, f32[1032,128]{1,0:T(8,128)S(1)}, u32[]{:S(2)}, u32[]{:S(2)}) collective-permute-start(f32[1032,128]{1,0:T(8,128)S(1)} %state_kernel.1), channel_id=1, source_target_pairs={{0,4},{8,12},{16,20},{24,28},{32,36},{40,44},{48,52},{56,60},{64,6... | collective-permute-start | bytes 1585160 | tf_op jit(solution)/shard_map/ppermute | solution.py:169
  10.2 14.3 %collective-permute-start.1 = (f32[1032,128]{1,0:T(8,128)S(1)}, f32[1032,128]{1,0:T(8,128)S(1)}, u32[]{:S(2)}, u32[]{:S(2)}) collective-permute-start(f32[1032,128]{1,0:T(8,128)S(1)} %select_add_fusion.5), channel_id=1, source_target_pairs={{4,12},{12,20},{20,28},{28,36},{36,44},{44,52},{52,60},{60,68},{68... | collective-permute-start | bytes 1585160 | tf_op jit(solution)/shard_map/ppermute | solution.py:169
  26.6 7.5 %collective-permute-start.2 = (f32[1032,128]{1,0:T(8,128)S(1)}, f32[1032,128]{1,0:T(8,128)S(1)}, u32[]{:S(2)}, u32[]{:S(2)}) collective-permute-start(f32[1032,128]{1,0:T(8,128)S(1)} %select_add_fusion.4), channel_id=1, source_target_pairs={{4,8},{12,16},{20,24},{28,32},{36,40},{44,48},{52,56},{60,64},{68,... | collective-permute-start | bytes 1585160 | tf_op jit(solution)/shard_map/ppermute | solution.py:169
  35.9 1.5 %copy-start = (bf16[256,1024]{1,0:T(8,128)(2,1)S(1)}, bf16[256,1024]{1,0:T(8,128)(2,1)}, u32[]{:S(2)}) copy-start(bf16[256,1024]{1,0:T(8,128)(2,1)} %q.7) | copy-start | bytes 1572868
  36.1 5.3 %collective-permute-start.3 = (f32[1032,128]{1,0:T(8,128)S(1)}, f32[1032,128]{1,0:T(8,128)S(1)}, u32[]{:S(2)}, u32[]{:S(2)}) collective-permute-start(f32[1032,128]{1,0:T(8,128)S(1)} %select_add_fusion.3), channel_id=1, source_target_pairs={{0,4},{8,12},{16,20},{24,28},{32,36},{40,44},{48,52},{56,60},{64,6... | collective-permute-start | bytes 1585160 | tf_op jit(solution)/shard_map/ppermute | solution.py:169
  38.4 3.1 %copy-start.4 = (bf16[256,1024]{1,0:T(8,128)(2,1)S(1)}, bf16[256,1024]{1,0:T(8,128)(2,1)}, u32[]{:S(2)}) copy-start(bf16[256,1024]{1,0:T(8,128)(2,1)} %grad.3) | copy-start | bytes 1572868
  41.4 0.7 copy-start.6
  43.5 3.8 %collective-permute-start.6 = (f32[8,256]{1,0:T(8,128)S(1)}, f32[8,256]{1,0:T(8,128)S(1)}, u32[]{:S(2)}, u32[]{:S(2)}) collective-permute-start(f32[8,256]{1,0:T(8,128)S(1)} %get-tuple-element.19), channel_id=1, source_target_pairs={{0,3},{1,0},{2,1},{3,2},{4,7},{5,4},{6,5},{7,6},{8,11},{9,8},{10,9... | collective-permute-start | bytes 24584 | tf_op jit(solution)/shard_map/ppermute | solution.py:199
  46.2 4.0 %collective-permute-start.5 = (f32[8,256]{1,0:T(8,128)S(1)}, f32[8,256]{1,0:T(8,128)S(1)}, u32[]{:S(2)}, u32[]{:S(2)}) collective-permute-start(f32[8,256]{1,0:T(8,128)S(1)} %get-tuple-element.19), channel_id=1, source_target_pairs={{0,2},{1,3},{2,0},{3,1},{4,6},{5,7},{6,4},{7,5},{8,10},{9,11},{10,... | collective-permute-start | bytes 24584 | tf_op jit(solution)/shard_map/ppermute | solution.py:199
  46.6 3.7 %collective-permute-start.4 = (f32[8,256]{1,0:T(8,128)S(1)}, f32[8,256]{1,0:T(8,128)S(1)}, u32[]{:S(2)}, u32[]{:S(2)}) collective-permute-start(f32[8,256]{1,0:T(8,128)S(1)} %get-tuple-element.19), channel_id=1, source_target_pairs={{0,1},{1,2},{2,3},{3,0},{4,5},{5,6},{6,7},{7,4},{8,9},{9,10},{10,1... | collective-permute-start | bytes 24584 | tf_op jit(solution)/shard_map/ppermute | solution.py:199
  51.5 5.3 %collective-permute-start.7 = (f32[1032,128]{1,0:T(8,128)S(1)}, f32[1032,128]{1,0:T(8,128)S(1)}, u32[]{:S(2)}, u32[]{:S(2)}) collective-permute-start(f32[1032,128]{1,0:T(8,128)S(1)} %get-tuple-element.23), channel_id=1, source_target_pairs={{252,248},{244,240},{236,232},{228,224},{220,216},{212,208},{204,2... | collective-permute-start | bytes 1585160 | tf_op jit(solution)/shard_map/ppermute | solution.py:169
  58.9 1.2 %collective-permute-start.8 = (f32[1032,128]{1,0:T(8,128)S(1)}, f32[1032,128]{1,0:T(8,128)S(1)}, u32[]{:S(2)}, u32[]{:S(2)}) collective-permute-start(f32[1032,128]{1,0:T(8,128)S(1)} %select_add_fusion.2), channel_id=1, source_target_pairs={{248,240},{240,232},{232,224},{224,216},{216,208},{208,200},{200,1... | collective-permute-start | bytes 1585160 | tf_op jit(solution)/shard_map/ppermute | solution.py:169
  62.1 18.4 %collective-permute-start.9 = (f32[1032,128]{1,0:T(8,128)S(1)}, f32[1032,128]{1,0:T(8,128)S(1)}, u32[]{:S(2)}, u32[]{:S(2)}) collective-permute-start(f32[1032,128]{1,0:T(8,128)S(1)} %select_add_fusion.1), channel_id=1, source_target_pairs={{248,244},{240,236},{232,228},{224,220},{216,212},{208,204},{200,1... | collective-permute-start | bytes 1585160 | tf_op jit(solution)/shard_map/ppermute | solution.py:169
  82.3 2.1 %copy-start.3 = (bf16[256,1024]{1,0:T(8,128)(2,1)S(1)}, bf16[256,1024]{1,0:T(8,128)(2,1)}, u32[]{:S(2)}) copy-start(bf16[256,1024]{1,0:T(8,128)(2,1)} %v.7) | copy-start | bytes 1572868
  82.5 5.9 %collective-permute-start.10 = (f32[1032,128]{1,0:T(8,128)S(1)}, f32[1032,128]{1,0:T(8,128)S(1)}, u32[]{:S(2)}, u32[]{:S(2)}) collective-permute-start(f32[1032,128]{1,0:T(8,128)S(1)} %select_add_fusion), channel_id=1, source_target_pairs={{252,248},{244,240},{236,232},{228,224},{220,216},{212,208},{204,2... | collective-permute-start | bytes 1585160 | tf_op jit(solution)/shard_map/ppermute | solution.py:169

commit v2 on v1

v2 whole, which is shorter than its diff:
```python
import jax
import jax.numpy as jnp
from jax import lax
from jax.experimental import pallas as pl
from jax.experimental.pallas import tpu as pltpu
from jax.sharding import PartitionSpec as P

HEADS = 32
HD = 128
TAG = 8
F32 = jnp.float32
BF16 = jnp.bfloat16


def dot(a, b, dims):
    return lax.dot_general(a, b, (dims, ((), ())), preferred_element_type=F32)


NN = ((1,), (0,))
NT = ((1,), (1,))
TN = ((0,), (0,))


def as_column(row):
    return jnp.transpose(jnp.broadcast_to(row, (HD, row.shape[1])))


def head(h):
    return slice(h * HD, (h + 1) * HD)


def in_doc(row_ref, at):
    row = row_ref[...].astype(F32)
    which = jnp.broadcast_to(row[:, at:at + 1], (row.shape[1], HD))
    return (as_column(row) == which).astype(F32)


def tag(row_ref, at):
    return jnp.broadcast_to(row_ref[:, at:at + 1].astype(F32), (1, HD))


def visible(row_ref):
    rows = row_ref.shape[1]
    row = row_ref[...].astype(F32)
    column = as_column(row)
    column = jnp.concatenate([column] * (rows // HD), axis=1)
    t = lax.broadcasted_iota(jnp.int32, (rows, rows), 0)
    s = lax.broadcasted_iota(jnp.int32, (rows, rows), 1)
    return (column == jnp.broadcast_to(row, (rows, rows))) & (t >= s)


def state_kernel(lo, hi, row_hbm, k_hbm, v_hbm, out, row, k, v, sems):
    rows = k.shape[0]
    width = (hi - lo) * HD
    span = slice(lo * HD, hi * HD)
    copies = [
        pltpu.make_async_copy(row_hbm, row, sems.at[0]),
        pltpu.make_async_copy(k_hbm.at[:, span], k, sems.at[1]),
        pltpu.make_async_copy(v_hbm.at[:, span], v, sems.at[2]),
    ]
    for copy in copies:
        copy.start()
    copies[0].wait()
    keep = in_doc(row, rows - 1).astype(BF16)
    out[width:, :] = jnp.broadcast_to(tag(row, rows - 1), (TAG, HD))
    copies[1].wait()
    copies[2].wait()
    for h in range(hi - lo):
        out[head(h), :] = dot(k[:, head(h)] * keep, v[:, head(h)], TN)


def merge_kernel(mine, came, *rest):
    out = rest[-1]
    width = mine.shape[0] - TAG
    same = mine[width:width + 1, :] == came[width:width + 1, :]
    out[:width, :] = mine[:width, :] + jnp.where(same, came[:width, :], 0.0)
    out[width:, :] = mine[width:, :]


def local_kernel(row, q, k, v, after, scores, part):
    del after
    seen = visible(row)
    for h in range(q.shape[1] // HD):
        sc = dot(q[:, head(h)], k[:, head(h)], NT)
        sc = jnp.where(seen, sc, 0.0).astype(BF16)
        scores[h] = sc
        part[:, head(h)] = dot(sc, v[:, head(h)], NN)


def attend_kernel(lo, hi, row, q, part, entering, passed, grad, gain, *rest):
    attended, carried, stats = rest[-3:]
    rows = q.shape[0]
    width = (hi - lo) * HD
    keep = in_doc(row, 0)
    came = entering[width:width + 1, :] + passed[width:width + 1, :]
    same = came == tag(row, 0)
    square = jnp.zeros((rows, HD), F32)
    inner = jnp.zeros((rows, HD), F32)
    for h in range(hi - lo):
        at = head(lo + h)
        state = jnp.where(same, entering[head(h), :] + passed[head(h), :], 0.0).astype(BF16)
        carried[head(h), :] = state
        att = (part[:, at] + keep * dot(q[:, at], state, NN)).astype(BF16)
        attended[:, head(h)] = att
        att = att.astype(F32)
        square = square + att * att
        inner = inner + gain[:, at] * grad[:, at].astype(F32) * att
    ones = jnp.ones((TAG, HD), F32)
    upper = lax.broadcasted_iota(jnp.int32, (TAG, rows), 0) < TAG // 2
    exact = lax.Precision.HIGHEST
    sums = [
        lax.dot_general(ones, x, (NT, ((), ())), precision=exact, preferred_element_type=F32)
        for x in (square, inner)
    ]
    sums = jnp.where(upper, sums[0], sums[1])
    stats[...] = sums + rest[0][...] if len(rest) > 3 else sums


def norm_scales(parts):
    feats = HEADS * HD
    total = parts[0][...]
    for x in parts[1:]:
        total = total + x[...]
    inv = lax.rsqrt(total[0:1, :] / feats + 1e-06)
    back = inv * inv * inv * (total[TAG - 1:TAG, :] / feats)
    return as_column(inv), as_column(back)


def grad_kernel(lo, hi, ranks, row, q, attended, grad, gain, *rest):
    g_out, out = rest[-2:]
    rows = q.shape[0]
    width = (hi - lo) * HD
    keep = in_doc(row, 0).astype(BF16)
    inv, back = norm_scales(rest[:ranks])
    for h in range(hi - lo):
        at = head(lo + h)
        weighted = gain[:, at] * grad[:, at].astype(F32)
        g = (inv * weighted - attended[:, head(h)].astype(F32) * back).astype(BF16)
        g_out[:, head(h)] = g
        out[head(h), :] = dot(q[:, at] * keep, g, TN)
    out[width:, :] = jnp.broadcast_to(tag(row, 0), (TAG, HD))


def back_kernel(cuts, ranks, row, q, k, v, scores, gain, *rest):
    normed, grad_q, part_k, part_v = rest[-4:]
    n = len(cuts)
    inv, _ = norm_scales(rest[3 * n:3 * n + ranks])
    keep = in_doc(row, 0)
    seen = visible(row)
    for c, (lo, hi) in enumerate(cuts):
        g, attended, carried = rest[c], rest[n + c], rest[2 * n + c]
        for h in range(hi - lo):
            at = head(lo + h)
            gh = g[:, head(h)]
            att = attended[:, head(h)].astype(F32)
            normed[:, at] = (gain[:, at] * att * inv).astype(BF16)
            gs = dot(gh, v[:, at], NT)
            gs = jnp.where(seen, gs, 0.0).astype(BF16)
            whole = dot(gs, k[:, at], NN) + keep * dot(gh, carried[head(h), :], NT)
            grad_q[:, at] = whole.astype(BF16)
            part_k[:, at] = dot(gs, q[:, at], TN)
            part_v[:, at] = dot(scores[lo + h], gh, TN)


def last_kernel(lo, hi, row, k, v, part_k, part_v, entering, passed, *rest):
    k_hbm, v_hbm, grad_k, grad_v, sems = rest[-5:]
    rows = k.shape[0]
    width = (hi - lo) * HD
    keep = in_doc(row, rows - 1)
    came = entering[width:width + 1, :] + passed[width:width + 1, :]
    same = came == tag(row, rows - 1)
    copies = []
    for h in range(hi - lo):
        at = head(lo + h)
        later = jnp.where(same, entering[head(h), :] + passed[head(h), :], 0.0).astype(BF16)
        grad_k[:, head(h)] = (part_k[:, at] + keep * dot(v[:, at], later, NT)).astype(BF16)
        grad_v[:, head(h)] = (part_v[:, at] + keep * dot(k[:, at], later, NN)).astype(BF16)
        for i, (held, out) in enumerate(((grad_k, k_hbm), (grad_v, v_hbm))):
            copies.append(pltpu.make_async_copy(held.at[:, head(h)], out.at[:, at], sems.at[2 * h + i]))
            copies[-1].start()
    for copy in copies:
        copy.wait()


VMEM, HBM, ANY = pltpu.VMEM, pltpu.HBM, pl.ANY


def call(kernel, name, outs, args, spaces=(), after=(), out_space=VMEM, scratch=(), aliases={}):
    spaces = list(spaces) + [VMEM] * (len(args) - len(spaces)) + [ANY] * len(after)
    return pl.pallas_call(
        kernel,
        out_shape=[jax.ShapeDtypeStruct(shape, kind) for shape, kind in outs],
        in_specs=[pl.BlockSpec(memory_space=space) for space in spaces],
        out_specs=[pl.BlockSpec(memory_space=out_space)] * len(outs),
        scratch_shapes=scratch,
        input_output_aliases=aliases,
        compiler_params=pltpu.CompilerParams(vmem_limit_bytes=40 * 1024 * 1024),
        name=name,
    )(*args, *after)


def merge(mine, came, after=()):
    return call(merge_kernel, "merge", [(mine.shape, F32)], [mine, came], after=after)[0]


def carry(states, blocks, backward, beside):
    chips = blocks // 2

    def hop(value, source, target, apart):
        pairs = [
            (2 * c + source, 2 * (c + apart) + target) for c in range(chips) if c + apart < chips
        ]
        if backward:
            pairs = [(blocks - 1 - a, blocks - 1 - b) for a, b in pairs]
        return lax.ppermute(value, "ctx", pairs)

    both = [merge(s, hop(s, 0, 1, 0)) for s in states]
    once = [hop(b, 1, 1, 1) for b in both]
    work, token = beside(both[-1])
    window = [merge(b, o, [token]) for b, o in zip(both, once)]
    entering = [hop(w, 1, 0, 1) for w in window]
    passed = [hop(merge(s, e), 0, 1, 0) for s, e in zip(states, entering)]
    return list(zip(entering, passed)), work


CUTS = ((0, 4), (4, 8))


def local(queries, key_rows, value_rows, grad_out, doc_ids, out_gain):
    rows, width = queries.shape
    heads = width // HD
    blocks = lax.axis_size("ctx")
    ranks = lax.axis_size("head")
    row = doc_ids.reshape(1, rows)
    gain = out_gain.reshape(1, width)
    wide, half, sums = ((rows, width), F32), ((rows, width), BF16), ((TAG, rows), F32)

    def of(cut, *rest):
        return ((cut[1] - cut[0]) * HD, *rest)

    def bind(kernel, *fixed):
        return lambda *refs: kernel(*fixed, *refs)

    states = [
        call(
            bind(state_kernel, *cut), "state", [((of(cut)[0] + TAG, HD), F32)],
            [pltpu.with_memory_space_constraint(x, HBM) for x in (row, key_rows, value_rows)],
            spaces=[HBM] * 3,
            scratch=[VMEM((1, rows), jnp.int32), VMEM((rows, *of(cut)), BF16),
                     VMEM((rows, *of(cut)), BF16), pltpu.SemaphoreType.DMA((3,))],
        )[0]
        for cut in CUTS
    ]

    def local_work(held):
        scores, part = call(
            local_kernel, "local", [((heads, rows, rows), BF16), wide],
            [row, queries, key_rows, value_rows], after=[held],
        )
        return (scores, part), part

    came, (scores, part) = carry(states, blocks, False, local_work)
    attended, carried, stats = [], [], []
    for cut, pair in zip(CUTS, came):
        out = call(
            bind(attend_kernel, *cut), "attend",
            [((rows, *of(cut)), BF16), (of(cut, HD), BF16), sums],
            [row, queries, part, *pair, grad_out, gain, *stats[-1:]],
        )
        for held, new in zip((attended, carried, stats), out):
            held.append(new)
    stats = stats[-1:]
    stats += [
        lax.ppermute(stats[0], "head", [(i, (i + apart) % ranks) for i in range(ranks)])
        for apart in range(1, ranks)
    ]
    g, grads = [], []
    for cut, att in zip(CUTS, attended):
        out = call(
            bind(grad_kernel, *cut, ranks), "grad",
            [((rows, *of(cut)), BF16), ((of(cut)[0] + TAG, HD), F32)],
            [row, queries, att, grad_out, gain, *stats],
        )
        g.append(out[0])
        grads.append(out[1])

    def back_work(held):
        out = call(
            bind(back_kernel, CUTS, ranks), "back", [half, half, wide, wide],
            [row, queries, key_rows, value_rows, scores, gain, *g, *attended, *carried, *stats],
            after=[held],
        )
        return out, out[2]

    came, (normed, grad_q, part_k, part_v) = carry(grads, blocks, True, back_work)
    done = ()
    for cut, pair in zip(CUTS, came):
        n = 7
        done = call(
            bind(last_kernel, *cut), "last", [half, half],
            [row, key_rows, value_rows, part_k, part_v, *pair], after=done, out_space=HBM,
            scratch=[VMEM((rows, *of(cut)), BF16), VMEM((rows, *of(cut)), BF16),
                     pltpu.SemaphoreType.DMA((2 * (cut[1] - cut[0]),))],
            aliases={n: 0, n + 1: 1} if done else {},
        )
    return normed, grad_q, *done


def solution(mesh):
    cut = P("ctx", "head")
    return jax.shard_map(
        local,
        mesh=mesh,
        in_specs=(cut, cut, cut, cut, P("ctx"), P("head")),
        out_specs=(cut, cut, cut, cut),
        check_vma=False,
    )
```

time: 91 us -> 65.6 us (0.72)
  waiting for transfers between devices: 42.5 us -> 20.2 us
  starting transfers between devices: 18.9 us -> 31.7 us
  local copies, waits for them, and re-layouts: 8.51 us -> 0.03 us
  between operations: 8.68 us -> 0.96 us
  Pallas kernels: 10.5 us -> 12.2 us
  other arithmetic: 1.44 us -> 0 us
    ppermute x8 -> x16, waiting for transfers between devices: 39.4 us -> 18.7 us  [hop(): return lax.ppermute(value, 'ctx', pairs)]
    ppermute x8 -> x16, starting transfers between devices: 15.1 us -> 26.7 us  [hop(): return lax.ppermute(value, 'ctx', pairs)]
    slice x12 -> x0, local copies, waits for them, and re-layouts: 5.13 us -> none  [the longest x10 5.12 us: joined(): same = mine[width, 0] == came[width, 0]]
    unnamed x14 -> x12, local copies, waits for them, and re-layouts: 3.38 us -> 0.03 us
    pallas_call x6 -> x22, Pallas kernels: 10.5 us -> 12.2 us  [call(): pl.pallas_call(kernel, out_shape=[jax.ShapeDtypeStruct(shape, kind) for s...]
    ppermute x3, waiting for transfers between devices: 3.05 us -> 1.48 us  [local(): lax.ppermute(stats[0], 'head', [(i, (i + apart) % ranks) for i in range(r...]
    add x9 -> x0, other arithmetic: 1.4 us -> none  [the longest x6 1.24 us: joined(): return mine + jnp.where(same & inside, came, 0.0)]
    ppermute x3, starting transfers between devices: 3.8 us -> 5.01 us  [local(): lax.ppermute(stats[0], 'head', [(i, (i + apart) % ranks) for i in range(r...]
  transfers between devices with their start and end apart: 11 -> 19, of which waited for: 8 -> 11; matrix products, arithmetic and copies ran while one was open for 2% -> 0% of each run, Pallas kernels for 5% -> 13%
where the time goes in v2:
time: 65.6 us; the launch traced here: 65.1 us
  starting transfers between devices  31.7 us (48%)
  waiting for transfers between devices  20.2 us (31%)
  Pallas kernels  12.2 us (19%)
  between operations  0.96 us (1%)
    ppermute x16, starting transfers between devices, hop(): return lax.ppermute(value, 'ctx', pairs)  26.7 us
    ppermute x16, waiting for transfers between devices, hop(): return lax.ppermute(value, 'ctx', pairs)  18.7 us
    pallas_call x22, Pallas kernels, call(): pl.pallas_call(kernel, out_shape=[jax.ShapeDtypeStruct(shape, kind) for s...  12.2 us
    ppermute x3, starting transfers between devices, local(): lax.ppermute(stats[0], 'head', [(i, (i + apart) % ranks) for i in range(r...  5.01 us
    ppermute x3, waiting for transfers between devices, local(): lax.ppermute(stats[0], 'head', [(i, (i + apart) % ranks) for i in range(r...  1.48 us
  transfers between devices with their start and end apart: 19, of which 11 were waited for; matrix products, arithmetic and copies ran while one was open for 0% of the time, Pallas kernels for 13%

profile of v2, /device:TPU:7, one launch (start us, length us, event | category | flops | bytes accessed | tf_op | source)
XLA Modules:
  0.0 65.1 jit_solution(7640879192220990500)
XLA Ops:
  0.6 1.3 %state.3.mine = f32[520,128]{1,0:T(8,128)S(1)} custom-call(s32[1,256]{1,0:T(1,128)} %bitcast.7, bf16[256,1024]{1,0:T(8,128)(2,1)} %refs_1_.17, bf16[256,1024]{1,0:T(8,128)(2,1)} %refs_2_.9), custom_call_target="tpu_custom_call" | custom-call | tf_op jit(solution)/shard_map/state/pallas_call | solution.py:190
  2.0 1.3 %collective-permute-start.1 = (f32[520,128]{1,0:T(8,128)S(1)}, f32[520,128]{1,0:T(8,128)S(1)}, u32[]{:S(2)}, u32[]{:S(2)}) collective-permute-start(f32[520,128]{1,0:T(8,128)S(1)} %state.3.mine), channel_id=1, source_target_pairs={{0,4},{8,12},{16,20},{24,28},{32,36},{40,44},{48,52},{56,60},{64,6... | collective-permute-start | bytes 798728 | tf_op jit(solution)/shard_map/ppermute | solution.py:215
  3.3 1.4 %state.2.mine = f32[520,128]{1,0:T(8,128)S(1)} custom-call(s32[1,256]{1,0:T(1,128)} %bitcast.8, bf16[256,1024]{1,0:T(8,128)(2,1)} %refs_1_.17, bf16[256,1024]{1,0:T(8,128)(2,1)} %refs_2_.9), custom_call_target="tpu_custom_call" | custom-call | tf_op jit(solution)/shard_map/state/pallas_call | solution.py:190
  4.6 1.3 %collective-permute-start = (f32[520,128]{1,0:T(8,128)S(1)}, f32[520,128]{1,0:T(8,128)S(1)}, u32[]{:S(2)}, u32[]{:S(2)}) collective-permute-start(f32[520,128]{1,0:T(8,128)S(1)} %state.2.mine), channel_id=1, source_target_pairs={{0,4},{8,12},{16,20},{24,28},{32,36},{40,44},{48,52},{56,60},{64,6... | collective-permute-start | bytes 798728 | tf_op jit(solution)/shard_map/ppermute | solution.py:215
  5.9 0.0 collective-permute-done.1.came
  6.0 0.0 copy-start.1
  6.0 0.0 copy-start.2
  6.0 0.0 copy-start
  6.0 0.0 copy-start.5
  6.0 3.7 %collective-permute-start.2 = (f32[520,128]{1,0:T(8,128)S(1)}, f32[520,128]{1,0:T(8,128)S(1)}, u32[]{:S(2)}, u32[]{:S(2)}) collective-permute-start(f32[520,128]{1,0:T(8,128)S(1)} %merge.13.mine), channel_id=1, source_target_pairs={{4,12},{12,20},{20,28},{28,36},{36,44},{44,52},{52,60},{60,68},{68... | collective-permute-start | bytes 798728 | tf_op jit(solution)/shard_map/ppermute | solution.py:215
  9.7 0.0 collective-permute-done.came
  9.8 3.5 %collective-permute-start.5 = (f32[520,128]{1,0:T(8,128)S(1)}, f32[520,128]{1,0:T(8,128)S(1)}, u32[]{:S(2)}, u32[]{:S(2)}) collective-permute-start(f32[520,128]{1,0:T(8,128)S(1)} %merge.12.after.mine), channel_id=1, source_target_pairs={{4,12},{12,20},{20,28},{28,36},{36,44},{44,52},{52,60},{60,68},{68... | collective-permute-start | bytes 798728 | tf_op jit(solution)/shard_map/ppermute | solution.py:215
  13.3 0.0 copy-done.1
  13.3 0.0 copy-done.2
  13.4 0.0 copy-done
  13.4 0.0 copy-done.5
  13.4 0.9 %local.1 = (bf16[8,256,256]{2,1,0:T(8,128)(2,1)S(1)}, f32[256,1024]{1,0:T(8,128)S(1)}) custom-call(s32[1,256]{1,0:T(1,128)S(1)} %bitcast.9, bf16[256,1024]{1,0:T(8,128)(2,1)S(1)} %copy-done, bf16[256,1024]{1,0:T(8,128)(2,1)S(1)} %copy-done.1, bf16[256,1024]{1,0:T(8,128)(2,1)S(1)} %copy-done.2, f32[520,128]{1,0:T(8,128)S(1)} %merge.12.after.mine), custom_call_target="tpu_custom_call" | custom-call | tf_op jit(solution)/shard_map/local/pallas_call | solution.py:190
  14.3 3.4 %collective-permute-done.2.came = f32[520,128]{1,0:T(8,128)S(1)} collective-permute-done((f32[520,128]{1,0:T(8,128)S(1)}, f32[520,128]{1,0:T(8,128)S(1)}, u32[]{:S(2)}, u32[]{:S(2)}) %collective-permute-start.2) | collective-permute-done | bytes 266272 | tf_op jit(solution)/shard_map/ppermute | solution.py:215
  17.8 1.3 %collective-permute-start.3 = (f32[520,128]{1,0:T(8,128)S(1)}, f32[520,128]{1,0:T(8,128)S(1)}, u32[]{:S(2)}, u32[]{:S(2)}) collective-permute-start(f32[520,128]{1,0:T(8,128)S(1)} %merge.14), channel_id=1, source_target_pairs={{4,8},{12,16},{20,24},{28,32},{36,40},{44,48},{52,56},{60,64},{68,... | collective-permute-start | bytes 798728 | tf_op jit(solution)/shard_map/ppermute | solution.py:215
  19.1 1.5 %collective-permute-done.5.came = f32[520,128]{1,0:T(8,128)S(1)} collective-permute-done((f32[520,128]{1,0:T(8,128)S(1)}, f32[520,128]{1,0:T(8,128)S(1)}, u32[]{:S(2)}, u32[]{:S(2)}) %collective-permute-start.5) | collective-permute-done | bytes 266272 | tf_op jit(solution)/shard_map/ppermute | solution.py:215
  20.6 0.1 merge.16
  20.6 1.3 %collective-permute-start.6 = (f32[520,128]{1,0:T(8,128)S(1)}, f32[520,128]{1,0:T(8,128)S(1)}, u32[]{:S(2)}, u32[]{:S(2)}) collective-permute-start(f32[520,128]{1,0:T(8,128)S(1)} %merge.16), channel_id=1, source_target_pairs={{4,8},{12,16},{20,24},{28,32},{36,40},{44,48},{52,56},{60,64},{68,... | collective-permute-start | bytes 798728 | tf_op jit(solution)/shard_map/ppermute | solution.py:215
  21.9 0.5 collective-permute-done.3.came.refs_3_
  22.4 0.0 copy-start.3
  22.5 1.4 %collective-permute-start.4 = (f32[520,128]{1,0:T(8,128)S(1)}, f32[520,128]{1,0:T(8,128)S(1)}, u32[]{:S(2)}, u32[]{:S(2)}) collective-permute-start(f32[520,128]{1,0:T(8,128)S(1)} %merge.15), channel_id=1, source_target_pairs={{0,4},{8,12},{16,20},{24,28},{32,36},{40,44},{48,52},{56,60},{64,6... | collective-permute-start | bytes 798728 | tf_op jit(solution)/shard_map/ppermute | solution.py:215
  23.9 1.4 %collective-permute-done.6.came.refs_3_ = f32[520,128]{1,0:T(8,128)S(1)} collective-permute-done((f32[520,128]{1,0:T(8,128)S(1)}, f32[520,128]{1,0:T(8,128)S(1)}, u32[]{:S(2)}, u32[]{:S(2)}) %collective-permute-start.6) | collective-permute-done | bytes 266272 | tf_op jit(solution)/shard_map/ppermute | solution.py:215
  25.3 0.0 copy-start.4
  25.3 1.3 %collective-permute-start.7 = (f32[520,128]{1,0:T(8,128)S(1)}, f32[520,128]{1,0:T(8,128)S(1)}, u32[]{:S(2)}, u32[]{:S(2)}) collective-permute-start(f32[520,128]{1,0:T(8,128)S(1)} %merge.17), channel_id=1, source_target_pairs={{0,4},{8,12},{16,20},{24,28},{32,36},{40,44},{48,52},{56,60},{64,6... | collective-permute-start | bytes 798728 | tf_op jit(solution)/shard_map/ppermute | solution.py:215
  26.6 0.9 %collective-permute-done.4.refs_4_ = f32[520,128]{1,0:T(8,128)S(1)} collective-permute-done((f32[520,128]{1,0:T(8,128)S(1)}, f32[520,128]{1,0:T(8,128)S(1)}, u32[]{:S(2)}, u32[]{:S(2)}) %collective-permute-start.4) | collective-permute-done | bytes 266272 | tf_op jit(solution)/shard_map/ppermute | solution.py:215
  27.5 0.0 copy-done.3
  27.5 0.0 copy-done.4
  27.5 0.7 %attend.2 = (bf16[256,512]{1,0:T(8,128)(2,1)S(1)}, bf16[512,128]{1,0:T(8,128)(2,1)S(1)}, f32[8,256]{1,0:T(8,128)S(1)}) custom-call(s32[1,256]{1,0:T(1,128)S(1)} %bitcast.10, bf16[256,1024]{1,0:T(8,128)(2,1)S(1)} %copy-done, f32[256,1024]{1,0:T(8,128)S(1)} %get-tuple-element.25.rest_0_.refs_2_, f32[520,128]{1,0:T(8,128)S(1)} %collective-permute-done.3.came.refs_3_, ...), custom_call_target="tpu_custom_call" | custom-call | tf_op jit(solution)/shard_map/attend/pallas_call | solution.py:190
  28.2 2.0 %collective-permute-done.7.refs_4_ = f32[520,128]{1,0:T(8,128)S(1)} collective-permute-done((f32[520,128]{1,0:T(8,128)S(1)}, f32[520,128]{1,0:T(8,128)S(1)}, u32[]{:S(2)}, u32[]{:S(2)}) %collective-permute-start.7) | collective-permute-done | bytes 266272 | tf_op jit(solution)/shard_map/ppermute | solution.py:215
  30.2 0.7 %attend.3 = (bf16[256,512]{1,0:T(8,128)(2,1)S(1)}, bf16[512,128]{1,0:T(8,128)(2,1)S(1)}, f32[8,256]{1,0:T(8,128)S(1)}) custom-call(s32[1,256]{1,0:T(1,128)S(1)} %bitcast.11, bf16[256,1024]{1,0:T(8,128)(2,1)S(1)} %copy-done, f32[256,1024]{1,0:T(8,128)S(1)} %get-tuple-element.25.rest_0_.refs_2_, f32[520,128]{1,0:T(8,128)S(1)} %collective-permute-done.6.came.refs_3_, ...), custom_call_target="tpu_custom_call" | custom-call | tf_op jit(solution)/shard_map/attend/pallas_call | solution.py:190
  30.9 1.3 %collective-permute-start.8 = (f32[8,256]{1,0:T(8,128)S(1)}, f32[8,256]{1,0:T(8,128)S(1)}, u32[]{:S(2)}, u32[]{:S(2)}) collective-permute-start(f32[8,256]{1,0:T(8,128)S(1)} %get-tuple-element.28.refs_5_.refs_12_), channel_id=1, source_target_pairs={{0,1},{1,2},{2,3},{3,0},{4,5},{5,6},{6,7},{7,4},{8,9},{9,10},{10,1... | collective-permute-start | bytes 24584 | tf_op jit(solution)/shard_map/ppermute | solution.py:274
  32.2 2.6 %collective-permute-start.9 = (f32[8,256]{1,0:T(8,128)S(1)}, f32[8,256]{1,0:T(8,128)S(1)}, u32[]{:S(2)}, u32[]{:S(2)}) collective-permute-start(f32[8,256]{1,0:T(8,128)S(1)} %get-tuple-element.28.refs_5_.refs_12_), channel_id=1, source_target_pairs={{0,2},{1,3},{2,0},{3,1},{4,6},{5,7},{6,4},{7,5},{8,10},{9,11},{10,... | collective-permute-start | bytes 24584 | tf_op jit(solution)/shard_map/ppermute | solution.py:274
  34.8 1.1 %collective-permute-start.10 = (f32[8,256]{1,0:T(8,128)S(1)}, f32[8,256]{1,0:T(8,128)S(1)}, u32[]{:S(2)}, u32[]{:S(2)}) collective-permute-start(f32[8,256]{1,0:T(8,128)S(1)} %get-tuple-element.28.refs_5_.refs_12_), channel_id=1, source_target_pairs={{0,3},{1,0},{2,1},{3,2},{4,7},{5,4},{6,5},{7,6},{8,11},{9,8},{10,9... | collective-permute-start | bytes 24584 | tf_op jit(solution)/shard_map/ppermute | solution.py:274
  35.9 0.0 collective-permute-done.8.refs_6_.refs_13_
  35.9 0.3 collective-permute-done.9.refs_7_.refs_14_
  36.2 1.2 %collective-permute-done.10.refs_8_.refs_15_ = f32[8,256]{1,0:T(8,128)S(1)} collective-permute-done((f32[8,256]{1,0:T(8,128)S(1)}, f32[8,256]{1,0:T(8,128)S(1)}, u32[]{:S(2)}, u32[]{:S(2)}) %collective-permute-start.10) | collective-permute-done | bytes 8224 | tf_op jit(solution)/shard_map/ppermute | solution.py:274
  37.4 0.4 grad.2
  37.8 3.7 %collective-permute-start.15 = (f32[520,128]{1,0:T(8,128)S(1)}, f32[520,128]{1,0:T(8,128)S(1)}, u32[]{:S(2)}, u32[]{:S(2)}) collective-permute-start(f32[520,128]{1,0:T(8,128)S(1)} %get-tuple-element.39.mine), channel_id=1, source_target_pairs={{252,248},{244,240},{236,232},{228,224},{220,216},{212,208},{204,2... | collective-permute-start | bytes 798728 | tf_op jit(solution)/shard_map/ppermute | solution.py:215
  41.6 0.4 grad.3
  42.0 1.3 %collective-permute-start.11 = (f32[520,128]{1,0:T(8,128)S(1)}, f32[520,128]{1,0:T(8,128)S(1)}, u32[]{:S(2)}, u32[]{:S(2)}) collective-permute-start(f32[520,128]{1,0:T(8,128)S(1)} %get-tuple-element.34.mine), channel_id=1, source_target_pairs={{252,248},{244,240},{236,232},{228,224},{220,216},{212,208},{204,2... | collective-permute-start | bytes 798728 | tf_op jit(solution)/shard_map/ppermute | solution.py:215
  43.3 0.0 collective-permute-done.15.came
  43.4 0.7 %collective-permute-start.16 = (f32[520,128]{1,0:T(8,128)S(1)}, f32[520,128]{1,0:T(8,128)S(1)}, u32[]{:S(2)}, u32[]{:S(2)}) collective-permute-start(f32[520,128]{1,0:T(8,128)S(1)} %merge.21.mine), channel_id=1, source_target_pairs={{248,240},{240,232},{232,224},{224,216},{216,208},{208,200},{200,1... | collective-permute-start | bytes 798728 | tf_op jit(solution)/shard_map/ppermute | solution.py:215
  44.1 0.4 collective-permute-done.11.came
  44.5 0.7 %collective-permute-start.12 = (f32[520,128]{1,0:T(8,128)S(1)}, f32[520,128]{1,0:T(8,128)S(1)}, u32[]{:S(2)}, u32[]{:S(2)}) collective-permute-start(f32[520,128]{1,0:T(8,128)S(1)} %merge.18.refs_16_.mine), channel_id=1, source_target_pairs={{248,240},{240,232},{232,224},{224,216},{216,208},{208,200},{200,1... | collective-permute-start | bytes 798728 | tf_op jit(solution)/shard_map/ppermute | solution.py:215
  45.2 3.6 %back.1 = (bf16[256,1024]{1,0:T(8,128)(2,1)}, bf16[256,1024]{1,0:T(8,128)(2,1)}, f32[256,1024]{1,0:T(8,128)S(1)}, f32[256,1024]{1,0:T(8,128)S(1)}) custom-call(s32[1,256]{1,0:T(1,128)S(1)} %bitcast.14, bf16[256,1024]{1,0:T(8,128)(2,1)S(1)} %copy-done, bf16[256,1024]{1,0:T(8,128)(2,1)S(1)} %copy-done.1, bf16[256,1024]{1,0:T(8,128)(2,1)S(1)} %copy-done.2, ...), custom_call_target="tpu_custom_call" | custom-call | tf_op jit(solution)/shard_map/back/pallas_call | solution.py:190
  48.8 0.0 collective-permute-done.16.came
  48.8 0.1 merge.22
  48.9 1.3 %collective-permute-start.17 = (f32[520,128]{1,0:T(8,128)S(1)}, f32[520,128]{1,0:T(8,128)S(1)}, u32[]{:S(2)}, u32[]{:S(2)}) collective-permute-start(f32[520,128]{1,0:T(8,128)S(1)} %merge.22), channel_id=1, source_target_pairs={{248,244},{240,236},{232,228},{224,220},{216,212},{208,204},{200,1... | collective-permute-start | bytes 798728 | tf_op jit(solution)/shard_map/ppermute | solution.py:215
  50.1 0.0 collective-permute-done.12.came
  50.2 1.3 %collective-permute-start.13 = (f32[520,128]{1,0:T(8,128)S(1)}, f32[520,128]{1,0:T(8,128)S(1)}, u32[]{:S(2)}, u32[]{:S(2)}) collective-permute-start(f32[520,128]{1,0:T(8,128)S(1)} %merge.19), channel_id=1, source_target_pairs={{248,244},{240,236},{232,228},{224,220},{216,212},{208,204},{200,1... | collective-permute-start | bytes 798728 | tf_op jit(solution)/shard_map/ppermute | solution.py:215
  51.5 7.2 %collective-permute-done.17.came.refs_5_ = f32[520,128]{1,0:T(8,128)S(1)} collective-permute-done((f32[520,128]{1,0:T(8,128)S(1)}, f32[520,128]{1,0:T(8,128)S(1)}, u32[]{:S(2)}, u32[]{:S(2)}) %collective-permute-start.17) | collective-permute-done | bytes 266272 | tf_op jit(solution)/shard_map/ppermute | solution.py:215
  58.7 1.3 %collective-permute-start.18 = (f32[520,128]{1,0:T(8,128)S(1)}, f32[520,128]{1,0:T(8,128)S(1)}, u32[]{:S(2)}, u32[]{:S(2)}) collective-permute-start(f32[520,128]{1,0:T(8,128)S(1)} %merge.23), channel_id=1, source_target_pairs={{252,248},{244,240},{236,232},{228,224},{220,216},{212,208},{204,2... | collective-permute-start | bytes 798728 | tf_op jit(solution)/shard_map/ppermute | solution.py:215
  60.0 1.5 %collective-permute-done.13.came.refs_5_ = f32[520,128]{1,0:T(8,128)S(1)} collective-permute-done((f32[520,128]{1,0:T(8,128)S(1)}, f32[520,128]{1,0:T(8,128)S(1)}, u32[]{:S(2)}, u32[]{:S(2)}) %collective-permute-start.13) | collective-permute-done | bytes 266272 | tf_op jit(solution)/shard_map/ppermute | solution.py:215
  61.6 1.3 %collective-permute-start.14 = (f32[520,128]{1,0:T(8,128)S(1)}, f32[520,128]{1,0:T(8,128)S(1)}, u32[]{:S(2)}, u32[]{:S(2)}) collective-permute-start(f32[520,128]{1,0:T(8,128)S(1)} %merge.20), channel_id=1, source_target_pairs={{252,248},{244,240},{236,232},{228,224},{220,216},{212,208},{204,2... | collective-permute-start | bytes 798728 | tf_op jit(solution)/shard_map/ppermute | solution.py:215
  62.9 0.0 collective-permute-done.18.refs_6_
  62.9 1.1 %last.2 = (bf16[256,1024]{1,0:T(8,128)(2,1)}, bf16[256,1024]{1,0:T(8,128)(2,1)}) custom-call(s32[1,256]{1,0:T(1,128)S(1)} %bitcast.15, bf16[256,1024]{1,0:T(8,128)(2,1)S(1)} %copy-done.1, bf16[256,1024]{1,0:T(8,128)(2,1)S(1)} %copy-done.2, f32[256,1024]{1,0:T(8,128)S(1)} %get-tuple-element.37.rest_0_.refs_3_, f32[256,1024]{1,0:T(8,128)S(1)} %get-tuple-element.38.refs_4_, ...), custom_call_target="tpu_custom_call" | custom-call | tf_op jit(solution)/shard_map/last/pallas_call | solution.py:190
  64.0 0.0 collective-permute-done.14.refs_6_
  64.0 1.1 %last.3 = (bf16[256,1024]{1,0:T(8,128)(2,1)}, bf16[256,1024]{1,0:T(8,128)(2,1)}) custom-call(s32[1,256]{1,0:T(1,128)S(1)} %bitcast.16, bf16[256,1024]{1,0:T(8,128)(2,1)S(1)} %copy-done.1, bf16[256,1024]{1,0:T(8,128)(2,1)S(1)} %copy-done.2, f32[256,1024]{1,0:T(8,128)S(1)} %get-tuple-element.37.rest_0_.refs_3_, ...), custom_call_target="tpu_custom_call", output_to_operand_aliasing={{0}: (7, {}), {1}: (8, {})} | custom-call | tf_op jit(solution)/shard_map/last/pallas_call | solution.py:190
  (10 shorter events, 0.4 us)
Async XLA Ops:
  2.0 4.0 %collective-permute-start.1 = (f32[520,128]{1,0:T(8,128)S(1)}, f32[520,128]{1,0:T(8,128)S(1)}, u32[]{:S(2)}, u32[]{:S(2)}) collective-permute-start(f32[520,128]{1,0:T(8,128)S(1)} %state.3.mine), channel_id=1, source_target_pairs={{0,4},{8,12},{16,20},{24,28},{32,36},{40,44},{48,52},{56,60},{64,6... | collective-permute-start | bytes 798728 | tf_op jit(solution)/shard_map/ppermute | solution.py:215
  4.6 5.1 %collective-permute-start = (f32[520,128]{1,0:T(8,128)S(1)}, f32[520,128]{1,0:T(8,128)S(1)}, u32[]{:S(2)}, u32[]{:S(2)}) collective-permute-start(f32[520,128]{1,0:T(8,128)S(1)} %state.2.mine), channel_id=1, source_target_pairs={{0,4},{8,12},{16,20},{24,28},{32,36},{40,44},{48,52},{56,60},{64,6... | collective-permute-start | bytes 798728 | tf_op jit(solution)/shard_map/ppermute | solution.py:215
  6.0 7.4 %copy-start.1 = (bf16[256,1024]{1,0:T(8,128)(2,1)S(1)}, bf16[256,1024]{1,0:T(8,128)(2,1)}, u32[]{:S(2)}) copy-start(bf16[256,1024]{1,0:T(8,128)(2,1)} %refs_1_.17) | copy-start | bytes 1572868
  6.0 7.4 %copy-start.2 = (bf16[256,1024]{1,0:T(8,128)(2,1)S(1)}, bf16[256,1024]{1,0:T(8,128)(2,1)}, u32[]{:S(2)}) copy-start(bf16[256,1024]{1,0:T(8,128)(2,1)} %refs_2_.9) | copy-start | bytes 1572868
  6.0 7.3 %copy-start = (bf16[256,1024]{1,0:T(8,128)(2,1)S(1)}, bf16[256,1024]{1,0:T(8,128)(2,1)}, u32[]{:S(2)}) copy-start(bf16[256,1024]{1,0:T(8,128)(2,1)} %refs_1_.15) | copy-start | bytes 1572868
  6.0 7.3 %copy-start.5 = (s32[256]{0:T(256)S(1)}, s32[256]{0:T(256)}, u32[]{:S(2)}) copy-start(s32[256]{0:T(256)} %param.10) | copy-start | bytes 3076
  6.0 11.7 %collective-permute-start.2 = (f32[520,128]{1,0:T(8,128)S(1)}, f32[520,128]{1,0:T(8,128)S(1)}, u32[]{:S(2)}, u32[]{:S(2)}) collective-permute-start(f32[520,128]{1,0:T(8,128)S(1)} %merge.13.mine), channel_id=1, source_target_pairs={{4,12},{12,20},{20,28},{28,36},{36,44},{44,52},{52,60},{60,68},{68... | collective-permute-start | bytes 798728 | tf_op jit(solution)/shard_map/ppermute | solution.py:215
  9.8 10.8 %collective-permute-start.5 = (f32[520,128]{1,0:T(8,128)S(1)}, f32[520,128]{1,0:T(8,128)S(1)}, u32[]{:S(2)}, u32[]{:S(2)}) collective-permute-start(f32[520,128]{1,0:T(8,128)S(1)} %merge.12.after.mine), channel_id=1, source_target_pairs={{4,12},{12,20},{20,28},{28,36},{36,44},{44,52},{52,60},{60,68},{68... | collective-permute-start | bytes 798728 | tf_op jit(solution)/shard_map/ppermute | solution.py:215
  17.8 4.6 %collective-permute-start.3 = (f32[520,128]{1,0:T(8,128)S(1)}, f32[520,128]{1,0:T(8,128)S(1)}, u32[]{:S(2)}, u32[]{:S(2)}) collective-permute-start(f32[520,128]{1,0:T(8,128)S(1)} %merge.14), channel_id=1, source_target_pairs={{4,8},{12,16},{20,24},{28,32},{36,40},{44,48},{52,56},{60,64},{68,... | collective-permute-start | bytes 798728 | tf_op jit(solution)/shard_map/ppermute | solution.py:215
  20.6 4.6 %collective-permute-start.6 = (f32[520,128]{1,0:T(8,128)S(1)}, f32[520,128]{1,0:T(8,128)S(1)}, u32[]{:S(2)}, u32[]{:S(2)}) collective-permute-start(f32[520,128]{1,0:T(8,128)S(1)} %merge.16), channel_id=1, source_target_pairs={{4,8},{12,16},{20,24},{28,32},{36,40},{44,48},{52,56},{60,64},{68,... | collective-permute-start | bytes 798728 | tf_op jit(solution)/shard_map/ppermute | solution.py:215
  22.4 5.0 %copy-start.3 = (bf16[256,1024]{1,0:T(8,128)(2,1)S(1)}, bf16[256,1024]{1,0:T(8,128)(2,1)}, u32[]{:S(2)}) copy-start(bf16[256,1024]{1,0:T(8,128)(2,1)} %refs_3_.4) | copy-start | bytes 1572868
  22.5 5.0 %collective-permute-start.4 = (f32[520,128]{1,0:T(8,128)S(1)}, f32[520,128]{1,0:T(8,128)S(1)}, u32[]{:S(2)}, u32[]{:S(2)}) collective-permute-start(f32[520,128]{1,0:T(8,128)S(1)} %merge.15), channel_id=1, source_target_pairs={{0,4},{8,12},{16,20},{24,28},{32,36},{40,44},{48,52},{56,60},{64,6... | collective-permute-start | bytes 798728 | tf_op jit(solution)/shard_map/ppermute | solution.py:215
  25.3 2.2 %copy-start.4 = (f32[1024]{0:T(1024)S(1)}, f32[1024]{0:T(1024)}, u32[]{:S(2)}) copy-start(f32[1024]{0:T(1024)} %param.11) | copy-start | bytes 12292
  25.3 4.9 %collective-permute-start.7 = (f32[520,128]{1,0:T(8,128)S(1)}, f32[520,128]{1,0:T(8,128)S(1)}, u32[]{:S(2)}, u32[]{:S(2)}) collective-permute-start(f32[520,128]{1,0:T(8,128)S(1)} %merge.17), channel_id=1, source_target_pairs={{0,4},{8,12},{16,20},{24,28},{32,36},{40,44},{48,52},{56,60},{64,6... | collective-permute-start | bytes 798728 | tf_op jit(solution)/shard_map/ppermute | solution.py:215
  30.9 5.0 %collective-permute-start.8 = (f32[8,256]{1,0:T(8,128)S(1)}, f32[8,256]{1,0:T(8,128)S(1)}, u32[]{:S(2)}, u32[]{:S(2)}) collective-permute-start(f32[8,256]{1,0:T(8,128)S(1)} %get-tuple-element.28.refs_5_.refs_12_), channel_id=1, source_target_pairs={{0,1},{1,2},{2,3},{3,0},{4,5},{5,6},{6,7},{7,4},{8,9},{9,10},{10,1... | collective-permute-start | bytes 24584 | tf_op jit(solution)/shard_map/ppermute | solution.py:274
  32.2 4.0 %collective-permute-start.9 = (f32[8,256]{1,0:T(8,128)S(1)}, f32[8,256]{1,0:T(8,128)S(1)}, u32[]{:S(2)}, u32[]{:S(2)}) collective-permute-start(f32[8,256]{1,0:T(8,128)S(1)} %get-tuple-element.28.refs_5_.refs_12_), channel_id=1, source_target_pairs={{0,2},{1,3},{2,0},{3,1},{4,6},{5,7},{6,4},{7,5},{8,10},{9,11},{10,... | collective-permute-start | bytes 24584 | tf_op jit(solution)/shard_map/ppermute | solution.py:274
  34.8 2.6 %collective-permute-start.10 = (f32[8,256]{1,0:T(8,128)S(1)}, f32[8,256]{1,0:T(8,128)S(1)}, u32[]{:S(2)}, u32[]{:S(2)}) collective-permute-start(f32[8,256]{1,0:T(8,128)S(1)} %get-tuple-element.28.refs_5_.refs_12_), channel_id=1, source_target_pairs={{0,3},{1,0},{2,1},{3,2},{4,7},{5,4},{6,5},{7,6},{8,11},{9,8},{10,9... | collective-permute-start | bytes 24584 | tf_op jit(solution)/shard_map/ppermute | solution.py:274
  37.8 5.5 %collective-permute-start.15 = (f32[520,128]{1,0:T(8,128)S(1)}, f32[520,128]{1,0:T(8,128)S(1)}, u32[]{:S(2)}, u32[]{:S(2)}) collective-permute-start(f32[520,128]{1,0:T(8,128)S(1)} %get-tuple-element.39.mine), channel_id=1, source_target_pairs={{252,248},{244,240},{236,232},{228,224},{220,216},{212,208},{204,2... | collective-permute-start | bytes 798728 | tf_op jit(solution)/shard_map/ppermute | solution.py:215
  42.0 2.4 %collective-permute-start.11 = (f32[520,128]{1,0:T(8,128)S(1)}, f32[520,128]{1,0:T(8,128)S(1)}, u32[]{:S(2)}, u32[]{:S(2)}) collective-permute-start(f32[520,128]{1,0:T(8,128)S(1)} %get-tuple-element.34.mine), channel_id=1, source_target_pairs={{252,248},{244,240},{236,232},{228,224},{220,216},{212,208},{204,2... | collective-permute-start | bytes 798728 | tf_op jit(solution)/shard_map/ppermute | solution.py:215
  43.4 5.4 %collective-permute-start.16 = (f32[520,128]{1,0:T(8,128)S(1)}, f32[520,128]{1,0:T(8,128)S(1)}, u32[]{:S(2)}, u32[]{:S(2)}) collective-permute-start(f32[520,128]{1,0:T(8,128)S(1)} %merge.21.mine), channel_id=1, source_target_pairs={{248,240},{240,232},{232,224},{224,216},{216,208},{208,200},{200,1... | collective-permute-start | bytes 798728 | tf_op jit(solution)/shard_map/ppermute | solution.py:215
  44.5 5.7 %collective-permute-start.12 = (f32[520,128]{1,0:T(8,128)S(1)}, f32[520,128]{1,0:T(8,128)S(1)}, u32[]{:S(2)}, u32[]{:S(2)}) collective-permute-start(f32[520,128]{1,0:T(8,128)S(1)} %merge.18.refs_16_.mine), channel_id=1, source_target_pairs={{248,240},{240,232},{232,224},{224,216},{216,208},{208,200},{200,1... | collective-permute-start | bytes 798728 | tf_op jit(solution)/shard_map/ppermute | solution.py:215
  48.9 9.8 %collective-permute-start.17 = (f32[520,128]{1,0:T(8,128)S(1)}, f32[520,128]{1,0:T(8,128)S(1)}, u32[]{:S(2)}, u32[]{:S(2)}) collective-permute-start(f32[520,128]{1,0:T(8,128)S(1)} %merge.22), channel_id=1, source_target_pairs={{248,244},{240,236},{232,228},{224,220},{216,212},{208,204},{200,1... | collective-permute-start | bytes 798728 | tf_op jit(solution)/shard_map/ppermute | solution.py:215
  50.2 11.3 %collective-permute-start.13 = (f32[520,128]{1,0:T(8,128)S(1)}, f32[520,128]{1,0:T(8,128)S(1)}, u32[]{:S(2)}, u32[]{:S(2)}) collective-permute-start(f32[520,128]{1,0:T(8,128)S(1)} %merge.19), channel_id=1, source_target_pairs={{248,244},{240,236},{232,228},{224,220},{216,212},{208,204},{200,1... | collective-permute-start | bytes 798728 | tf_op jit(solution)/shard_map/ppermute | solution.py:215
  58.7 4.2 %collective-permute-start.18 = (f32[520,128]{1,0:T(8,128)S(1)}, f32[520,128]{1,0:T(8,128)S(1)}, u32[]{:S(2)}, u32[]{:S(2)}) collective-permute-start(f32[520,128]{1,0:T(8,128)S(1)} %merge.23), channel_id=1, source_target_pairs={{252,248},{244,240},{236,232},{228,224},{220,216},{212,208},{204,2... | collective-permute-start | bytes 798728 | tf_op jit(solution)/shard_map/ppermute | solution.py:215
  61.6 2.5 %collective-permute-start.14 = (f32[520,128]{1,0:T(8,128)S(1)}, f32[520,128]{1,0:T(8,128)S(1)}, u32[]{:S(2)}, u32[]{:S(2)}) collective-permute-start(f32[520,128]{1,0:T(8,128)S(1)} %merge.20), channel_id=1, source_target_pairs={{252,248},{244,240},{236,232},{228,224},{220,216},{212,208},{204,2... | collective-permute-start | bytes 798728 | tf_op jit(solution)/shard_map/ppermute | solution.py:215

commit v3 on v2

v3 whole, which is shorter than its diff:
```python
import jax
import jax.numpy as jnp
from jax import lax
from jax.experimental import pallas as pl
from jax.experimental.pallas import tpu as pltpu
from jax.sharding import PartitionSpec as P

HEADS = 32
HD = 128
TAG = 8
F32 = jnp.float32
BF16 = jnp.bfloat16
VMEM, HBM, ANY = pltpu.VMEM, pltpu.HBM, pl.ANY
DMA = pltpu.SemaphoreType.DMA
NN = ((1,), (0,))
NT = ((1,), (1,))
TN = ((0,), (0,))


def dot(a, b, dims):
    return lax.dot_general(a, b, (dims, ((), ())), preferred_element_type=F32)


def head(h):
    return slice(h * HD, (h + 1) * HD)


def core():
    return lax.rem(lax.axis_index("ctx"), 2)


def columns(half, width):
    at = core() if half == 0 else 1 - core()
    return pl.ds(pl.multiple_of(at * width, width), width)


def as_column(row):
    return jnp.transpose(jnp.broadcast_to(row, (HD, row.shape[1])))


def in_doc(row_ref, at):
    row = row_ref[...].astype(F32)
    which = jnp.broadcast_to(row[:, at:at + 1], (row.shape[1], HD))
    return (as_column(row) == which).astype(F32)


def tag(row_ref, at):
    return jnp.broadcast_to(row_ref[:, at:at + 1].astype(F32), (1, HD))


def visible(row_ref):
    rows = row_ref.shape[1]
    row = row_ref[...].astype(F32)
    column = as_column(row)
    column = jnp.concatenate([column] * (rows // HD), axis=1)
    t = lax.broadcasted_iota(jnp.int32, (rows, rows), 0)
    s = lax.broadcasted_iota(jnp.int32, (rows, rows), 1)
    return (column == jnp.broadcast_to(row, (rows, rows))) & (t >= s)


def state_kernel(half, row_hbm, k_hbm, v_hbm, *rest):
    out, k, v, row, sems = rest[-5:]
    rows, width = k.shape
    span = columns(half, width)
    copies = [
        pltpu.make_async_copy(row_hbm, row, sems.at[0]),
        pltpu.make_async_copy(k_hbm.at[:, span], k, sems.at[1]),
        pltpu.make_async_copy(v_hbm.at[:, span], v, sems.at[2]),
    ]
    for copy in copies:
        copy.start()
    copies[0].wait()
    keep = in_doc(row, rows - 1).astype(BF16)
    out[width:, :] = jnp.broadcast_to(tag(row, rows - 1), (TAG, HD))
    copies[1].wait()
    copies[2].wait()
    for h in range(width // HD):
        out[head(h), :] = dot(k[:, head(h)] * keep, v[:, head(h)], TN)


def add_into(out, near, far, near_lo, far_lo):
    size = out.shape[0] - TAG
    near_tag = near[near.shape[0] - TAG:, :]
    same = near_tag[0:1, :] == far[far.shape[0] - TAG:far.shape[0] - TAG + 1, :]
    here = far[far_lo:far_lo + size, :]
    out[:size, :] = near[near_lo:near_lo + size, :] + jnp.where(same, here, 0.0)
    out[size:, :] = near_tag


def pair_kernel(backward, mine, came, *outs):
    size = outs[0].shape[0] - TAG
    upstream = core() == int(backward)

    def fill(down, up):
        for i, out in enumerate(outs):
            add_into(out, down, up, i * size, i * size)

    pl.when(upstream)(lambda: fill(came, mine))
    pl.when(jnp.logical_not(upstream))(lambda: fill(mine, came))


def merge_kernel(near, far, *rest):
    add_into(rest[-1], near, far, 0, 0)


def split_kernel(backward, part, entering, mine, came, keep, send):
    size = entering.shape[0] - TAG
    upstream = core() == int(backward)

    def fill(to_up, to_down, up):
        to_up[...] = entering[...]
        add_into(to_down, up, entering, part * size, 0)

    pl.when(upstream)(lambda: fill(keep, send, mine))
    pl.when(jnp.logical_not(upstream))(lambda: fill(send, keep, came))


def local_kernel(row, k0, k1, v0, v1, q_hbm, grad_hbm, gain_hbm, *rest):
    scores, part, q, weighted, gain, grad, sems = rest[-7:]
    rows, width = k0.shape
    copies = []
    for i, (hbm, held) in enumerate(((q_hbm, q), (gain_hbm, gain), (grad_hbm, grad))):
        for half in range(2):
            at = slice(half * width, (half + 1) * width)
            copies.append(
                pltpu.make_async_copy(
                    hbm.at[:, columns(half, width)], held.at[:, at], sems.at[2 * i + half]
                )
            )
            copies[-1].start()
    seen = visible(row)
    copies[0].wait()
    copies[1].wait()
    n = width // HD
    for h in range(2 * n):
        k, v = (k0, v0) if h < n else (k1, v1)
        sc = dot(q[:, head(h)], k[:, head(h % n)], NT)
        sc = jnp.where(seen, sc, 0.0).astype(BF16)
        scores[h] = sc
        part[:, head(h)] = dot(sc, v[:, head(h % n)], NN)
    for copy in copies[2:]:
        copy.wait()
    for h in range(2 * n):
        weighted[:, head(h)] = gain[:, head(h)] * grad[:, head(h)].astype(F32)


def pieces(refs):
    for ref in refs:
        size = ref.shape[0] - TAG
        for h in range(size // HD):
            yield ref[head(h), :], ref[size:size + 1, :]


def attend_kernel(half, chunks, row, q, part, weighted, *rest):
    came, rest = rest[:chunks], rest[chunks:]
    attended, carried, stats = rest[-3:]
    rows, width = attended.shape
    keep = in_doc(row, 0)
    first = tag(row, 0)
    square = jnp.zeros((rows, HD), F32)
    inner = jnp.zeros((rows, HD), F32)
    for h, (state, its) in enumerate(pieces(came)):
        at = head(half * (width // HD) + h)
        state = jnp.where(its == first, state, 0.0).astype(BF16)
        carried[head(h), :] = state
        att = (part[:, at] + keep * dot(q[:, at], state, NN)).astype(BF16)
        attended[:, head(h)] = att
        att = att.astype(F32)
        square = square + att * att
        inner = inner + weighted[:, at] * att
    ones = jnp.ones((TAG, HD), F32)
    upper = lax.broadcasted_iota(jnp.int32, (TAG, rows), 0) < TAG // 2
    exact = lax.Precision.HIGHEST
    sums = [
        lax.dot_general(ones, x, (NT, ((), ())), precision=exact, preferred_element_type=F32)
        for x in (square, inner)
    ]
    sums = jnp.where(upper, sums[0], sums[1])
    stats[...] = sums + rest[0][...] if len(rest) > 3 else sums


def norm_scales(parts):
    feats = HEADS * HD
    total = parts[0][...]
    for x in parts[1:]:
        total = total + x[...]
    inv = lax.rsqrt(total[0:1, :] / feats + 1e-06)
    back = inv * inv * inv * (total[TAG - 1:TAG, :] / feats)
    return as_column(inv), as_column(back)


def grad_kernel(half, ranks, row, q, weighted, attended, *rest):
    g_out, out = rest[-2:]
    rows, width = attended.shape
    keep = in_doc(row, 0).astype(BF16)
    inv, back = norm_scales(rest[:ranks])
    for h in range(width // HD):
        at = head(half * (width // HD) + h)
        g = (inv * weighted[:, at] - attended[:, head(h)].astype(F32) * back).astype(BF16)
        g_out[:, head(h)] = g
        out[head(h), :] = dot(q[:, at] * keep, g, TN)
    out[width:, :] = jnp.broadcast_to(tag(row, 0), (TAG, HD))


def back_kernel(ranks, row, q, scores, gain, k0, k1, v0, v1, g0, g1, a0, a1, c0, c1, *rest):
    normed_hbm, grad_q_hbm, part_k, part_v, normed, grad_q, sems = rest[-7:]
    rows, width = k0.shape
    inv, _ = norm_scales(rest[:ranks])
    keep = in_doc(row, 0)
    seen = visible(row)
    n = width // HD
    copies = []
    for half, (k, v, g, attended, carried) in enumerate(((k0, v0, g0, a0, c0), (k1, v1, g1, a1, c1))):
        for h in range(n):
            at = head(half * n + h)
            gh = g[:, head(h)]
            normed[:, at] = (gain[:, at] * attended[:, head(h)].astype(F32) * inv).astype(BF16)
            gs = dot(gh, v[:, head(h)], NT)
            gs = jnp.where(seen, gs, 0.0).astype(BF16)
            whole = dot(gs, k[:, head(h)], NN) + keep * dot(gh, carried[head(h), :], NT)
            grad_q[:, at] = whole.astype(BF16)
            part_k[:, at] = dot(gs, q[:, at], TN)
            part_v[:, at] = dot(scores[half * n + h], gh, TN)
        span = slice(half * width, (half + 1) * width)
        for i, (held, out) in enumerate(((normed, normed_hbm), (grad_q, grad_q_hbm))):
            copies.append(
                pltpu.make_async_copy(
                    held.at[:, span], out.at[:, columns(half, width)], sems.at[2 * half + i]
                )
            )
            copies[-1].start()
    for copy in copies:
        copy.wait()


def last_kernel(half, chunks, row, k, v, part_k, part_v, *rest):
    came = rest[:chunks]
    k_hbm, v_hbm, grad_k, grad_v, sems = rest[-5:]
    rows, width = k.shape
    keep = in_doc(row, rows - 1)
    last = tag(row, rows - 1)
    at_core = core() if half == 0 else 1 - core()
    copies = []
    for h, (state, its) in enumerate(pieces(came)):
        at = head(half * (width // HD) + h)
        later = jnp.where(its == last, state, 0.0).astype(BF16)
        grad_k[:, head(h)] = (part_k[:, at] + keep * dot(v[:, head(h)], later, NT)).astype(BF16)
        grad_v[:, head(h)] = (part_v[:, at] + keep * dot(k[:, head(h)], later, NN)).astype(BF16)
        span = pl.ds(pl.multiple_of(at_core * width + h * HD, HD), HD)
        for i, (held, out) in enumerate(((grad_k, k_hbm), (grad_v, v_hbm))):
            copies.append(
                pltpu.make_async_copy(held.at[:, head(h)], out.at[:, span], sems.at[2 * h + i])
            )
            copies[-1].start()
    for copy in copies:
        copy.wait()


def call(kernel, fixed, outs, args, after=(), scratch=(), aliases={}):
    spaces = [HBM if isinstance(x, list) else VMEM for x in args] + [ANY] * len(after)
    args = [
        pltpu.with_memory_space_constraint(x[0], HBM) if isinstance(x, list) else x for x in args
    ]
    return pl.pallas_call(
        lambda *refs: kernel(*fixed, *refs),
        out_shape=[jax.ShapeDtypeStruct(*out[:2]) for out in outs],
        in_specs=[pl.BlockSpec(memory_space=space) for space in spaces],
        out_specs=[pl.BlockSpec(memory_space=(*out, VMEM)[2]) for out in outs],
        scratch_shapes=scratch,
        input_output_aliases=aliases,
        compiler_params=pltpu.CompilerParams(vmem_limit_bytes=40 * 1024 * 1024),
        name=kernel.__name__[:-7],
    )(*args, *after)


def carry(mine, other, chunks, backward, beside):
    blocks = lax.axis_size("ctx")
    step = -2 if backward else 2

    def swap(value):
        return lax.ppermute(value, "ctx", [(i, i ^ 1) for i in range(blocks)])

    def hop(value):
        return lax.ppermute(value, "ctx", [(i, (i + step) % blocks) for i in range(blocks)])

    sent = other()
    came = swap(sent)
    mine = mine(sent)
    size = (mine.shape[0] - TAG) // chunks
    chunk = ((size + TAG, HD), F32)
    both = call(pair_kernel, [backward], [chunk] * chunks, [mine, came])
    once = [hop(b) for b in both]
    work, token = beside(both[-1])
    window = [call(merge_kernel, [], [chunk], [b, o], [token])[0] for b, o in zip(both, once)]
    entering = [hop(w) for w in window]
    keep, back = [], []
    for i, e in enumerate(entering):
        kept, send = call(split_kernel, [backward, i], [chunk] * 2, [e, mine, came])
        keep.append(kept)
        back.append(swap(send))
    return keep, back, work


CHUNKS = 2


def local(queries, key_rows, value_rows, grad_out, doc_ids, out_gain):
    rows, width = queries.shape
    heads = width // HD
    part_width = width // 2
    ranks = lax.axis_size("head")
    row = doc_ids.reshape(1, rows)
    gain = out_gain.reshape(1, width)
    wide, half, sums = ((rows, width), F32), ((rows, part_width), BF16), ((TAG, rows), F32)
    state = ((part_width + TAG, HD), F32)

    held = {}

    def make_state(which, after=()):
        out, held["k", which], held["v", which] = call(
            state_kernel, [which], [state, half, half], [[row], [key_rows], [value_rows]],
            after=after, scratch=[VMEM((1, rows), jnp.int32), DMA((3,))],
        )
        return out

    def local_work(token):
        out = call(
            local_kernel, [],
            [((heads, rows, rows), BF16), wide, ((rows, width), BF16), wide, ((1, width), F32)],
            [row, *k, *v, [queries], [grad_out], [gain]],
            after=[token], scratch=[VMEM((rows, width), BF16), DMA((6,))],
        )
        return out, out[1]

    k, v = [], []

    def own_state(sent):
        out = make_state(0, [sent])
        k.extend(held["k", i] for i in range(2))
        v.extend(held["v", i] for i in range(2))
        return out

    own, other, work = carry(own_state, lambda: make_state(1), CHUNKS, False, local_work)
    scores, part, q, weighted, gain = work
    attended, carried, stats = [], [], []
    for which, came in enumerate((own, other)):
        out = call(
            attend_kernel, [which, CHUNKS], [half, ((part_width, HD), BF16), sums],
            [row, q, part, weighted, *came, *stats[-1:]],
        )
        for kept, new in zip((attended, carried, stats), out):
            kept.append(new)
    stats = stats[-1:]
    stats += [
        lax.ppermute(stats[0], "head", [(i, (i + apart) % ranks) for i in range(ranks)])
        for apart in range(1, ranks)
    ]

    def make_grad(which, after=()):
        held["g", which], out = call(
            grad_kernel, [which, ranks], [half, state],
            [row, q, weighted, attended[which], *stats], after=after,
        )
        return out

    def back_work(token):
        out = call(
            back_kernel, [ranks], [((rows, width), BF16, HBM)] * 2 + [wide, wide],
            [row, q, scores, gain, *k, *v, held["g", 0], held["g", 1], *attended, *carried, *stats],
            after=[token],
            scratch=[VMEM((rows, width), BF16), VMEM((rows, width), BF16), DMA((4,))],
        )
        return out, out[2]

    own, other, work = carry(
        lambda sent: make_grad(0, [sent]), lambda: make_grad(1), CHUNKS, True, back_work
    )
    normed, grad_q, part_k, part_v = work
    done = ()
    for which, came in enumerate((own, other)):
        n = 5 + CHUNKS
        done = call(
            last_kernel, [which, CHUNKS], [((rows, width), BF16, HBM)] * 2,
            [row, k[which], v[which], part_k, part_v, *came], after=done,
            scratch=[VMEM(*half), VMEM(*half), DMA((heads,))],
            aliases={n: 0, n + 1: 1} if done else {},
        )
    return normed, grad_q, *done


def solution(mesh):
    cut = P("ctx", "head")
    return jax.shard_map(
        local,
        mesh=mesh,
        in_specs=(cut, cut, cut, cut, P("ctx"), P("head")),
        out_specs=(cut, cut, cut, cut),
        check_vma=False,
    )
```

time: 65.6 us -> 59.6 us (0.909)
  the two profiles are of different devices: /device:TPU:7 before, /device:TPU:1 now
where the time goes in v3:
time: 59.6 us; the launch traced here: 59.4 us
  starting transfers between devices  26.3 us (44%)
  waiting for transfers between devices  18.1 us (30%)
  Pallas kernels  13.3 us (22%)
  between operations  0.97 us (2%)
  local copies, waits for them, and re-layouts  0.68 us (1%)
    ppermute x8, waiting for transfers between devices, hop(): lax.ppermute(value, 'ctx', [(i, (i + step) % blocks) for i in range(block...  15.4 us
    pallas_call x20, Pallas kernels, call(): pl.pallas_call(lambda *refs: kernel(*fixed, *refs), out_shape=[jax.ShapeD...  13.3 us
    ppermute x6, starting transfers between devices, swap(): return lax.ppermute(value, 'ctx', [(i, i ^ 1) for i in range(blocks)])  12.6 us
    ppermute x8, starting transfers between devices, hop(): lax.ppermute(value, 'ctx', [(i, (i + step) % blocks) for i in range(block...  8.7 us
    ppermute x3, starting transfers between devices, local(): lax.ppermute(stats[0], 'head', [(i, (i + apart) % ranks) for i in range(r...  5 us
    ppermute x3, waiting for transfers between devices, local(): lax.ppermute(stats[0], 'head', [(i, (i + apart) % ranks) for i in range(r...  1.71 us
  transfers between devices with their start and end apart: 17, of which 10 were waited for; matrix products, arithmetic and copies ran while one was open for 0% of the time, Pallas kernels for 16%

profile of v3, /device:TPU:1, one launch (start us, length us, event | category | flops | bytes accessed | tf_op | source)
XLA Modules:
  0.0 59.4 jit_solution(13752448544609626488)
XLA Ops:
  0.6 1.3 %state.2 = (f32[520,128]{1,0:T(8,128)S(1)}, bf16[256,512]{1,0:T(8,128)(2,1)S(1)}, bf16[256,512]{1,0:T(8,128)(2,1)S(1)}) custom-call(s32[1,256]{1,0:T(1,128)} %bitcast.2, bf16[256,1024]{1,0:T(8,128)(2,1)} %refs_1_.3, bf16[256,1024]{1,0:T(8,128)(2,1)} %refs_2_.3), custom_call_target="tpu_custom_call" | custom-call | tf_op jit(solution)/shard_map/state/pallas_call | solution.py:264
  2.0 3.3 %collective-permute-start = (f32[520,128]{1,0:T(8,128)S(1)}, f32[520,128]{1,0:T(8,128)S(1)}, u32[]{:S(2)}, u32[]{:S(2)}) collective-permute-start(f32[520,128]{1,0:T(8,128)S(1)} %get-tuple-element.45.refs_3_), channel_id=1, source_target_pairs={{0,4},{4,0},{8,12},{12,8},{16,20},{20,16},{24,28},{28,24},{32,36},... | collective-permute-start | bytes 798728 | tf_op jit(solution)/shard_map/ppermute | solution.py:281
  5.3 1.3 %state.3 = (f32[520,128]{1,0:T(8,128)S(1)}, bf16[256,512]{1,0:T(8,128)(2,1)S(1)}, bf16[256,512]{1,0:T(8,128)(2,1)S(1)}) custom-call(s32[1,256]{1,0:T(1,128)} %bitcast.3, bf16[256,1024]{1,0:T(8,128)(2,1)} %refs_1_.3, bf16[256,1024]{1,0:T(8,128)(2,1)} %refs_2_.3, f32[520,128]{1,0:T(8,128)S(1)} %get-tuple-element.45.refs_3_), custom_call_target="tpu_custom_call" | custom-call | tf_op jit(solution)/shard_map/state/pallas_call | solution.py:264
  6.6 0.0 collective-permute-done.refs_1_.refs_2_
  6.6 0.1 pair.2
  6.7 0.1 collective-permute-start.3
  6.8 1.6 %collective-permute-start.1 = (f32[264,128]{1,0:T(8,128)S(1)}, f32[264,128]{1,0:T(8,128)S(1)}, u32[]{:S(2)}, u32[]{:S(2)}) collective-permute-start(f32[264,128]{1,0:T(8,128)S(1)} %get-tuple-element.57.refs_0_), channel_id=1, source_target_pairs={{0,8},{4,12},{8,16},{12,20},{16,24},{20,28},{24,32},{28,36},{32,40... | collective-permute-start | bytes 405512 | tf_op jit(solution)/shard_map/ppermute | solution.py:284
  8.3 0.0 copy-start
  8.3 0.7 %copy-done = s32[256]{0:T(256)S(1)} copy-done((s32[256]{0:T(256)S(1)}, s32[256]{0:T(256)}, u32[]{:S(2)}) %copy-start) | copy-done | bytes 1048
  9.0 2.2 %local.1 = (bf16[8,256,256]{2,1,0:T(8,128)(2,1)S(1)}, f32[256,1024]{1,0:T(8,128)S(1)}, bf16[256,1024]{1,0:T(8,128)(2,1)S(1)}, f32[256,1024]{1,0:T(8,128)S(1)}, f32[1,1024]{1,0:T(1,128)S(1)}) custom-call(s32[1,256]{1,0:T(1,128)S(1)} %bitcast.4, bf16[256,512]{1,0:T(8,128)(2,1)S(1)} %get-tuple-element.46.refs_1_.refs_4_, ...), custom_call_target="tpu_custom_call" | custom-call | tf_op jit(solution)/shard_map/local/pallas_call | solution.py:264
  11.2 5.4 %collective-permute-done.3.refs_1_ = f32[264,128]{1,0:T(8,128)S(1)} collective-permute-done((f32[264,128]{1,0:T(8,128)S(1)}, f32[264,128]{1,0:T(8,128)S(1)}, u32[]{:S(2)}, u32[]{:S(2)}) %collective-permute-start.3) | collective-permute-done | bytes 135200 | tf_op jit(solution)/shard_map/ppermute | solution.py:284
  16.7 0.1 collective-permute-start.4
  16.7 2.8 %collective-permute-done.1.refs_1_ = f32[264,128]{1,0:T(8,128)S(1)} collective-permute-done((f32[264,128]{1,0:T(8,128)S(1)}, f32[264,128]{1,0:T(8,128)S(1)}, u32[]{:S(2)}, u32[]{:S(2)}) %collective-permute-start.1) | collective-permute-done | bytes 135200 | tf_op jit(solution)/shard_map/ppermute | solution.py:284
  19.5 0.1 collective-permute-start.2
  19.6 4.3 %collective-permute-done.4.refs_0_ = f32[264,128]{1,0:T(8,128)S(1)} collective-permute-done((f32[264,128]{1,0:T(8,128)S(1)}, f32[264,128]{1,0:T(8,128)S(1)}, u32[]{:S(2)}, u32[]{:S(2)}) %collective-permute-start.4) | collective-permute-done | bytes 135200 | tf_op jit(solution)/shard_map/ppermute | solution.py:284
  23.9 2.4 %collective-permute-start.6 = (f32[264,128]{1,0:T(8,128)S(1)}, f32[264,128]{1,0:T(8,128)S(1)}, u32[]{:S(2)}, u32[]{:S(2)}) collective-permute-start(f32[264,128]{1,0:T(8,128)S(1)} %get-tuple-element.62), channel_id=1, source_target_pairs={{0,4},{4,0},{8,12},{12,8},{16,20},{20,16},{24,28},{28,24},{32,36},... | collective-permute-start | bytes 405512 | tf_op jit(solution)/shard_map/ppermute | solution.py:281
  26.4 1.2 %collective-permute-done.2.refs_0_ = f32[264,128]{1,0:T(8,128)S(1)} collective-permute-done((f32[264,128]{1,0:T(8,128)S(1)}, f32[264,128]{1,0:T(8,128)S(1)}, u32[]{:S(2)}, u32[]{:S(2)}) %collective-permute-start.2) | collective-permute-done | bytes 135200 | tf_op jit(solution)/shard_map/ppermute | solution.py:284
  27.6 1.6 %collective-permute-start.5 = (f32[264,128]{1,0:T(8,128)S(1)}, f32[264,128]{1,0:T(8,128)S(1)}, u32[]{:S(2)}, u32[]{:S(2)}) collective-permute-start(f32[264,128]{1,0:T(8,128)S(1)} %get-tuple-element.61), channel_id=1, source_target_pairs={{0,4},{4,0},{8,12},{12,8},{16,20},{20,16},{24,28},{28,24},{32,36},... | collective-permute-start | bytes 405512 | tf_op jit(solution)/shard_map/ppermute | solution.py:281
  29.2 0.7 %attend.2 = (bf16[256,512]{1,0:T(8,128)(2,1)S(1)}, bf16[512,128]{1,0:T(8,128)(2,1)S(1)}, f32[8,256]{1,0:T(8,128)S(1)}) custom-call(s32[1,256]{1,0:T(1,128)S(1)} %bitcast.5, bf16[256,1024]{1,0:T(8,128)(2,1)S(1)} %get-tuple-element.52.refs_1_, f32[256,1024]{1,0:T(8,128)S(1)} %get-tuple-element.56.refs_2_, f32[256,1024]{1,0:T(8,128)S(1)} %get-tuple-element.55.refs_3_.refs_2_, ...), custom_call_target="tpu_custom_call" | custom-call | tf_op jit(solution)/shard_map/attend/pallas_call | solution.py:264
  29.8 0.0 collective-permute-done.6.refs_5_
  29.8 0.3 collective-permute-done.5.refs_4_
  30.2 0.7 %attend.3 = (bf16[256,512]{1,0:T(8,128)(2,1)S(1)}, bf16[512,128]{1,0:T(8,128)(2,1)S(1)}, f32[8,256]{1,0:T(8,128)S(1)}) custom-call(s32[1,256]{1,0:T(1,128)S(1)} %bitcast.6, bf16[256,1024]{1,0:T(8,128)(2,1)S(1)} %get-tuple-element.52.refs_1_, f32[256,1024]{1,0:T(8,128)S(1)} %get-tuple-element.56.refs_2_, f32[256,1024]{1,0:T(8,128)S(1)} %get-tuple-element.55.refs_3_.refs_2_, ...), custom_call_target="tpu_custom_call" | custom-call | tf_op jit(solution)/shard_map/attend/pallas_call | solution.py:264
  30.8 1.3 %collective-permute-start.7 = (f32[8,256]{1,0:T(8,128)S(1)}, f32[8,256]{1,0:T(8,128)S(1)}, u32[]{:S(2)}, u32[]{:S(2)}) collective-permute-start(f32[8,256]{1,0:T(8,128)S(1)} %get-tuple-element.64.refs_4_.refs_14_), channel_id=1, source_target_pairs={{0,1},{1,2},{2,3},{3,0},{4,5},{5,6},{6,7},{7,4},{8,9},{9,10},{10,1... | collective-permute-start | bytes 24584 | tf_op jit(solution)/shard_map/ppermute | solution.py:355
  32.2 2.6 %collective-permute-start.8 = (f32[8,256]{1,0:T(8,128)S(1)}, f32[8,256]{1,0:T(8,128)S(1)}, u32[]{:S(2)}, u32[]{:S(2)}) collective-permute-start(f32[8,256]{1,0:T(8,128)S(1)} %get-tuple-element.64.refs_4_.refs_14_), channel_id=1, source_target_pairs={{0,2},{1,3},{2,0},{3,1},{4,6},{5,7},{6,4},{7,5},{8,10},{9,11},{10,... | collective-permute-start | bytes 24584 | tf_op jit(solution)/shard_map/ppermute | solution.py:355
  34.8 1.1 %collective-permute-start.9 = (f32[8,256]{1,0:T(8,128)S(1)}, f32[8,256]{1,0:T(8,128)S(1)}, u32[]{:S(2)}, u32[]{:S(2)}) collective-permute-start(f32[8,256]{1,0:T(8,128)S(1)} %get-tuple-element.64.refs_4_.refs_14_), channel_id=1, source_target_pairs={{0,3},{1,0},{2,1},{3,2},{4,7},{5,4},{6,5},{7,6},{8,11},{9,8},{10,9... | collective-permute-start | bytes 24584 | tf_op jit(solution)/shard_map/ppermute | solution.py:355
  35.8 0.0 collective-permute-done.7.refs_5_.refs_15_
  35.8 0.3 collective-permute-done.8.refs_6_.refs_16_
  36.2 1.4 %collective-permute-done.9.refs_7_.refs_17_ = f32[8,256]{1,0:T(8,128)S(1)} collective-permute-done((f32[8,256]{1,0:T(8,128)S(1)}, f32[8,256]{1,0:T(8,128)S(1)}, u32[]{:S(2)}, u32[]{:S(2)}) %collective-permute-start.9) | collective-permute-done | bytes 8224 | tf_op jit(solution)/shard_map/ppermute | solution.py:355
  37.6 0.4 grad.2
  38.0 1.9 %collective-permute-start.10 = (f32[520,128]{1,0:T(8,128)S(1)}, f32[520,128]{1,0:T(8,128)S(1)}, u32[]{:S(2)}, u32[]{:S(2)}) collective-permute-start(f32[520,128]{1,0:T(8,128)S(1)} %get-tuple-element.66.refs_8_), channel_id=1, source_target_pairs={{0,4},{4,0},{8,12},{12,8},{16,20},{20,16},{24,28},{28,24},{32,36},... | collective-permute-start | bytes 798728 | tf_op jit(solution)/shard_map/ppermute | solution.py:281
  39.9 0.4 grad.3
  40.3 0.7 %collective-permute-done.10.refs_1_.refs_2_ = f32[520,128]{1,0:T(8,128)S(1)} collective-permute-done((f32[520,128]{1,0:T(8,128)S(1)}, f32[520,128]{1,0:T(8,128)S(1)}, u32[]{:S(2)}, u32[]{:S(2)}) %collective-permute-start.10) | collective-permute-done | bytes 266272 | tf_op jit(solution)/shard_map/ppermute | solution.py:281
  41.1 0.1 collective-permute-start.14
  41.2 0.3 collective-permute-start.11
  41.5 3.7 %back.1 = (bf16[256,1024]{1,0:T(8,128)(2,1)}, bf16[256,1024]{1,0:T(8,128)(2,1)}, f32[256,1024]{1,0:T(8,128)S(1)}, f32[256,1024]{1,0:T(8,128)S(1)}) custom-call(s32[1,256]{1,0:T(1,128)S(1)} %bitcast.9, bf16[256,1024]{1,0:T(8,128)(2,1)S(1)} %get-tuple-element.52.refs_1_, bf16[8,256,256]{2,1,0:T(8,128)(2,1)S(1)} %get-tuple-element.53.refs_2_, ...), custom_call_target="tpu_custom_call" | custom-call | tf_op jit(solution)/shard_map/back/pallas_call | solution.py:264
  45.2 0.8 %collective-permute-done.14.refs_1_ = f32[264,128]{1,0:T(8,128)S(1)} collective-permute-done((f32[264,128]{1,0:T(8,128)S(1)}, f32[264,128]{1,0:T(8,128)S(1)}, u32[]{:S(2)}, u32[]{:S(2)}) %collective-permute-start.14) | collective-permute-done | bytes 135200 | tf_op jit(solution)/shard_map/ppermute | solution.py:284
  46.0 3.7 %collective-permute-start.15 = (f32[264,128]{1,0:T(8,128)S(1)}, f32[264,128]{1,0:T(8,128)S(1)}, u32[]{:S(2)}, u32[]{:S(2)}) collective-permute-start(f32[264,128]{1,0:T(8,128)S(1)} %merge.7), channel_id=1, source_target_pairs={{0,248},{4,252},{8,0},{12,4},{16,8},{20,12},{24,16},{28,20},{32,24... | collective-permute-start | bytes 405512 | tf_op jit(solution)/shard_map/ppermute | solution.py:284
  49.6 0.0 collective-permute-done.11.refs_1_
  49.7 2.9 %collective-permute-start.12 = (f32[264,128]{1,0:T(8,128)S(1)}, f32[264,128]{1,0:T(8,128)S(1)}, u32[]{:S(2)}, u32[]{:S(2)}) collective-permute-start(f32[264,128]{1,0:T(8,128)S(1)} %merge.6), channel_id=1, source_target_pairs={{0,248},{4,252},{8,0},{12,4},{16,8},{20,12},{24,16},{28,20},{32,24... | collective-permute-start | bytes 405512 | tf_op jit(solution)/shard_map/ppermute | solution.py:284
  52.5 0.0 collective-permute-done.15.refs_0_
  52.6 2.0 %collective-permute-start.16 = (f32[264,128]{1,0:T(8,128)S(1)}, f32[264,128]{1,0:T(8,128)S(1)}, u32[]{:S(2)}, u32[]{:S(2)}) collective-permute-start(f32[264,128]{1,0:T(8,128)S(1)} %get-tuple-element.79), channel_id=1, source_target_pairs={{0,4},{4,0},{8,12},{12,8},{16,20},{20,16},{24,28},{28,24},{32,36},... | collective-permute-start | bytes 405512 | tf_op jit(solution)/shard_map/ppermute | solution.py:281
  54.6 1.0 %collective-permute-done.12.refs_0_ = f32[264,128]{1,0:T(8,128)S(1)} collective-permute-done((f32[264,128]{1,0:T(8,128)S(1)}, f32[264,128]{1,0:T(8,128)S(1)}, u32[]{:S(2)}, u32[]{:S(2)}) %collective-permute-start.12) | collective-permute-done | bytes 135200 | tf_op jit(solution)/shard_map/ppermute | solution.py:284
  55.6 1.4 %collective-permute-start.13 = (f32[264,128]{1,0:T(8,128)S(1)}, f32[264,128]{1,0:T(8,128)S(1)}, u32[]{:S(2)}, u32[]{:S(2)}) collective-permute-start(f32[264,128]{1,0:T(8,128)S(1)} %get-tuple-element.78), channel_id=1, source_target_pairs={{0,4},{4,0},{8,12},{12,8},{16,20},{20,16},{24,28},{28,24},{32,36},... | collective-permute-start | bytes 405512 | tf_op jit(solution)/shard_map/ppermute | solution.py:281
  57.0 1.1 %last.2 = (bf16[256,1024]{1,0:T(8,128)(2,1)}, bf16[256,1024]{1,0:T(8,128)(2,1)}) custom-call(s32[1,256]{1,0:T(1,128)S(1)} %bitcast.10, bf16[256,512]{1,0:T(8,128)(2,1)S(1)} %get-tuple-element.46.refs_1_.refs_4_, bf16[256,512]{1,0:T(8,128)(2,1)S(1)} %get-tuple-element.48.refs_3_.refs_6_.refs_2_, f32[256,1024]{1,0:T(8,128)S(1)} %get-tuple-element.75.refs_2_.refs_3_, ...), custom_call_target="tpu_custom_call" | custom-call | tf_op jit(solution)/shard_map/last/pallas_call | solution.py:264
  58.1 0.0 collective-permute-done.16.refs_6_
  58.1 0.0 collective-permute-done.13.refs_5_
  58.1 1.1 %last.3 = (bf16[256,1024]{1,0:T(8,128)(2,1)}, bf16[256,1024]{1,0:T(8,128)(2,1)}) custom-call(s32[1,256]{1,0:T(1,128)S(1)} %bitcast.11, bf16[256,512]{1,0:T(8,128)(2,1)S(1)} %get-tuple-element.47.refs_2_.refs_5_.refs_1_, bf16[256,512]{1,0:T(8,128)(2,1)S(1)} %get-tuple-element.49.refs_4_.refs_7_.refs_2_, ...), custom_call_target="tpu_custom_call", output_to_operand_aliasing={{0}: (7, {}), {1}: (8, {})} | custom-call | tf_op jit(solution)/shard_map/last/pallas_call | solution.py:264
  (9 shorter events, 0.2 us)
Async XLA Ops:
  2.0 4.6 %collective-permute-start = (f32[520,128]{1,0:T(8,128)S(1)}, f32[520,128]{1,0:T(8,128)S(1)}, u32[]{:S(2)}, u32[]{:S(2)}) collective-permute-start(f32[520,128]{1,0:T(8,128)S(1)} %get-tuple-element.45.refs_3_), channel_id=1, source_target_pairs={{0,4},{4,0},{8,12},{12,8},{16,20},{20,16},{24,28},{28,24},{32,36},... | collective-permute-start | bytes 798728 | tf_op jit(solution)/shard_map/ppermute | solution.py:281
  6.7 9.9 %collective-permute-start.3 = (f32[264,128]{1,0:T(8,128)S(1)}, f32[264,128]{1,0:T(8,128)S(1)}, u32[]{:S(2)}, u32[]{:S(2)}) collective-permute-start(f32[264,128]{1,0:T(8,128)S(1)} %get-tuple-element.51.refs_8_.refs_0_), channel_id=1, source_target_pairs={{0,8},{4,12},{8,16},{12,20},{16,24},{20,28},{24,32},{28,36},{32,40... | collective-permute-start | bytes 405512 | tf_op jit(solution)/shard_map/ppermute | solution.py:284
  6.8 12.7 %collective-permute-start.1 = (f32[264,128]{1,0:T(8,128)S(1)}, f32[264,128]{1,0:T(8,128)S(1)}, u32[]{:S(2)}, u32[]{:S(2)}) collective-permute-start(f32[264,128]{1,0:T(8,128)S(1)} %get-tuple-element.57.refs_0_), channel_id=1, source_target_pairs={{0,8},{4,12},{8,16},{12,20},{16,24},{20,28},{24,32},{28,36},{32,40... | collective-permute-start | bytes 405512 | tf_op jit(solution)/shard_map/ppermute | solution.py:284
  8.3 0.7 %copy-start = (s32[256]{0:T(256)S(1)}, s32[256]{0:T(256)}, u32[]{:S(2)}) copy-start(s32[256]{0:T(256)} %param.10) | copy-start | bytes 3076
  16.7 7.3 %collective-permute-start.4 = (f32[264,128]{1,0:T(8,128)S(1)}, f32[264,128]{1,0:T(8,128)S(1)}, u32[]{:S(2)}, u32[]{:S(2)}) collective-permute-start(f32[264,128]{1,0:T(8,128)S(1)} %merge.5), channel_id=1, source_target_pairs={{0,8},{4,12},{8,16},{12,20},{16,24},{20,28},{24,32},{28,36},{32,40... | collective-permute-start | bytes 405512 | tf_op jit(solution)/shard_map/ppermute | solution.py:284
  19.5 8.0 %collective-permute-start.2 = (f32[264,128]{1,0:T(8,128)S(1)}, f32[264,128]{1,0:T(8,128)S(1)}, u32[]{:S(2)}, u32[]{:S(2)}) collective-permute-start(f32[264,128]{1,0:T(8,128)S(1)} %merge.4), channel_id=1, source_target_pairs={{0,8},{4,12},{8,16},{12,20},{16,24},{20,28},{24,32},{28,36},{32,40... | collective-permute-start | bytes 405512 | tf_op jit(solution)/shard_map/ppermute | solution.py:284
  23.9 5.9 %collective-permute-start.6 = (f32[264,128]{1,0:T(8,128)S(1)}, f32[264,128]{1,0:T(8,128)S(1)}, u32[]{:S(2)}, u32[]{:S(2)}) collective-permute-start(f32[264,128]{1,0:T(8,128)S(1)} %get-tuple-element.62), channel_id=1, source_target_pairs={{0,4},{4,0},{8,12},{12,8},{16,20},{20,16},{24,28},{28,24},{32,36},... | collective-permute-start | bytes 405512 | tf_op jit(solution)/shard_map/ppermute | solution.py:281
  27.6 2.6 %collective-permute-start.5 = (f32[264,128]{1,0:T(8,128)S(1)}, f32[264,128]{1,0:T(8,128)S(1)}, u32[]{:S(2)}, u32[]{:S(2)}) collective-permute-start(f32[264,128]{1,0:T(8,128)S(1)} %get-tuple-element.61), channel_id=1, source_target_pairs={{0,4},{4,0},{8,12},{12,8},{16,20},{20,16},{24,28},{28,24},{32,36},... | collective-permute-start | bytes 405512 | tf_op jit(solution)/shard_map/ppermute | solution.py:281
  30.8 5.0 %collective-permute-start.7 = (f32[8,256]{1,0:T(8,128)S(1)}, f32[8,256]{1,0:T(8,128)S(1)}, u32[]{:S(2)}, u32[]{:S(2)}) collective-permute-start(f32[8,256]{1,0:T(8,128)S(1)} %get-tuple-element.64.refs_4_.refs_14_), channel_id=1, source_target_pairs={{0,1},{1,2},{2,3},{3,0},{4,5},{5,6},{6,7},{7,4},{8,9},{9,10},{10,1... | collective-permute-start | bytes 24584 | tf_op jit(solution)/shard_map/ppermute | solution.py:355
  32.2 4.0 %collective-permute-start.8 = (f32[8,256]{1,0:T(8,128)S(1)}, f32[8,256]{1,0:T(8,128)S(1)}, u32[]{:S(2)}, u32[]{:S(2)}) collective-permute-start(f32[8,256]{1,0:T(8,128)S(1)} %get-tuple-element.64.refs_4_.refs_14_), channel_id=1, source_target_pairs={{0,2},{1,3},{2,0},{3,1},{4,6},{5,7},{6,4},{7,5},{8,10},{9,11},{10,... | collective-permute-start | bytes 24584 | tf_op jit(solution)/shard_map/ppermute | solution.py:355
  34.8 2.8 %collective-permute-start.9 = (f32[8,256]{1,0:T(8,128)S(1)}, f32[8,256]{1,0:T(8,128)S(1)}, u32[]{:S(2)}, u32[]{:S(2)}) collective-permute-start(f32[8,256]{1,0:T(8,128)S(1)} %get-tuple-element.64.refs_4_.refs_14_), channel_id=1, source_target_pairs={{0,3},{1,0},{2,1},{3,2},{4,7},{5,4},{6,5},{7,6},{8,11},{9,8},{10,9... | collective-permute-start | bytes 24584 | tf_op jit(solution)/shard_map/ppermute | solution.py:355
  38.0 3.0 %collective-permute-start.10 = (f32[520,128]{1,0:T(8,128)S(1)}, f32[520,128]{1,0:T(8,128)S(1)}, u32[]{:S(2)}, u32[]{:S(2)}) collective-permute-start(f32[520,128]{1,0:T(8,128)S(1)} %get-tuple-element.66.refs_8_), channel_id=1, source_target_pairs={{0,4},{4,0},{8,12},{12,8},{16,20},{20,16},{24,28},{28,24},{32,36},... | collective-permute-start | bytes 798728 | tf_op jit(solution)/shard_map/ppermute | solution.py:281
  41.1 4.8 %collective-permute-start.14 = (f32[264,128]{1,0:T(8,128)S(1)}, f32[264,128]{1,0:T(8,128)S(1)}, u32[]{:S(2)}, u32[]{:S(2)}) collective-permute-start(f32[264,128]{1,0:T(8,128)S(1)} %get-tuple-element.72.refs_18_.refs_0_), channel_id=1, source_target_pairs={{0,248},{4,252},{8,0},{12,4},{16,8},{20,12},{24,16},{28,20},{32,24... | collective-permute-start | bytes 405512 | tf_op jit(solution)/shard_map/ppermute | solution.py:284
  41.2 8.5 %collective-permute-start.11 = (f32[264,128]{1,0:T(8,128)S(1)}, f32[264,128]{1,0:T(8,128)S(1)}, u32[]{:S(2)}, u32[]{:S(2)}) collective-permute-start(f32[264,128]{1,0:T(8,128)S(1)} %get-tuple-element.77.refs_0_), channel_id=1, source_target_pairs={{0,248},{4,252},{8,0},{12,4},{16,8},{20,12},{24,16},{28,20},{32,24... | collective-permute-start | bytes 405512 | tf_op jit(solution)/shard_map/ppermute | solution.py:284
  46.0 6.6 %collective-permute-start.15 = (f32[264,128]{1,0:T(8,128)S(1)}, f32[264,128]{1,0:T(8,128)S(1)}, u32[]{:S(2)}, u32[]{:S(2)}) collective-permute-start(f32[264,128]{1,0:T(8,128)S(1)} %merge.7), channel_id=1, source_target_pairs={{0,248},{4,252},{8,0},{12,4},{16,8},{20,12},{24,16},{28,20},{32,24... | collective-permute-start | bytes 405512 | tf_op jit(solution)/shard_map/ppermute | solution.py:284
  49.7 5.9 %collective-permute-start.12 = (f32[264,128]{1,0:T(8,128)S(1)}, f32[264,128]{1,0:T(8,128)S(1)}, u32[]{:S(2)}, u32[]{:S(2)}) collective-permute-start(f32[264,128]{1,0:T(8,128)S(1)} %merge.6), channel_id=1, source_target_pairs={{0,248},{4,252},{8,0},{12,4},{16,8},{20,12},{24,16},{28,20},{32,24... | collective-permute-start | bytes 405512 | tf_op jit(solution)/shard_map/ppermute | solution.py:284
  52.6 5.5 %collective-permute-start.16 = (f32[264,128]{1,0:T(8,128)S(1)}, f32[264,128]{1,0:T(8,128)S(1)}, u32[]{:S(2)}, u32[]{:S(2)}) collective-permute-start(f32[264,128]{1,0:T(8,128)S(1)} %get-tuple-element.79), channel_id=1, source_target_pairs={{0,4},{4,0},{8,12},{12,8},{16,20},{20,16},{24,28},{28,24},{32,36},... | collective-permute-start | bytes 405512 | tf_op jit(solution)/shard_map/ppermute | solution.py:281
  55.6 2.5 %collective-permute-start.13 = (f32[264,128]{1,0:T(8,128)S(1)}, f32[264,128]{1,0:T(8,128)S(1)}, u32[]{:S(2)}, u32[]{:S(2)}) collective-permute-start(f32[264,128]{1,0:T(8,128)S(1)} %get-tuple-element.78), channel_id=1, source_target_pairs={{0,4},{4,0},{8,12},{12,8},{16,20},{20,16},{24,28},{28,24},{32,36},... | collective-permute-start | bytes 405512 | tf_op jit(solution)/shard_map/ppermute | solution.py:281

commit v4 on v3

--- a/solution.py
+++ b/solution.py
@@ -58,22 +58,28 @@
     return (column == jnp.broadcast_to(row, (rows, rows))) & (t >= s)
 
 
-def state_kernel(half, row_hbm, k_hbm, v_hbm, *rest):
-    out, k, v, row, sems = rest[-5:]
+def state_kernel(half, row, k_hbm, v_hbm, *rest):
+    if half:
+        out, k, v, row_out, sems = rest[-5:]
+    else:
+        out, k, v, sems = rest[-4:]
     rows, width = k.shape
     span = columns(half, width)
     copies = [
-        pltpu.make_async_copy(row_hbm, row, sems.at[0]),
         pltpu.make_async_copy(k_hbm.at[:, span], k, sems.at[1]),
         pltpu.make_async_copy(v_hbm.at[:, span], v, sems.at[2]),
     ]
+    if half:
+        copies.insert(0, pltpu.make_async_copy(row, row_out, sems.at[0]))
+        row = row_out
     for copy in copies:
         copy.start()
-    copies[0].wait()
+    if half:
+        copies.pop(0).wait()
     keep = in_doc(row, rows - 1).astype(BF16)
     out[width:, :] = jnp.broadcast_to(tag(row, rows - 1), (TAG, HD))
-    copies[1].wait()
-    copies[2].wait()
+    for copy in copies:
+        copy.wait()
     for h in range(width // HD):
         out[head(h), :] = dot(k[:, head(h)] * keep, v[:, head(h)], TN)
 
@@ -281,7 +287,8 @@
         return lax.ppermute(value, "ctx", [(i, i ^ 1) for i in range(blocks)])
 
     def hop(value):
-        return lax.ppermute(value, "ctx", [(i, (i + step) % blocks) for i in range(blocks)])
+        pairs = [(i, i + step) for i in range(blocks) if 0 <= i + step < blocks]
+        return lax.ppermute(value, "ctx", pairs)
 
     sent = other()
     came = swap(sent)
@@ -309,7 +316,7 @@
     heads = width // HD
     part_width = width // 2
     ranks = lax.axis_size("head")
-    row = doc_ids.reshape(1, rows)
+    ids = doc_ids.reshape(1, rows)
     gain = out_gain.reshape(1, width)
     wide, half, sums = ((rows, width), F32), ((rows, part_width), BF16), ((TAG, rows), F32)
     state = ((part_width + TAG, HD), F32)
@@ -317,17 +324,20 @@
     held = {}
 
     def make_state(which, after=()):
-        out, held["k", which], held["v", which] = call(
-            state_kernel, [which], [state, half, half], [[row], [key_rows], [value_rows]],
-            after=after, scratch=[VMEM((1, rows), jnp.int32), DMA((3,))],
-        )
+        out, held["k", which], held["v", which], *row = call(
+            state_kernel, [which], [state, half, half] + [((1, rows), jnp.int32)] * which,
+            [[ids] if which else held["row"], [key_rows], [value_rows]],
+            after=after, scratch=[DMA((3,))],
+        )
+        if which:
+            (held["row"],) = row
         return out
 
     def local_work(token):
         out = call(
             local_kernel, [],
             [((heads, rows, rows), BF16), wide, ((rows, width), BF16), wide, ((1, width), F32)],
-            [row, *k, *v, [queries], [grad_out], [gain]],
+            [held["row"], *k, *v, [queries], [grad_out], [gain]],
             after=[token], scratch=[VMEM((rows, width), BF16), DMA((6,))],
         )
         return out, out[1]
@@ -346,7 +356,7 @@
     for which, came in enumerate((own, other)):
         out = call(
             attend_kernel, [which, CHUNKS], [half, ((part_width, HD), BF16), sums],
-            [row, q, part, weighted, *came, *stats[-1:]],
+            [held["row"], q, part, weighted, *came, *stats[-1:]],
         )
         for kept, new in zip((attended, carried, stats), out):
             kept.append(new)
@@ -359,14 +369,14 @@
     def make_grad(which, after=()):
         held["g", which], out = call(
             grad_kernel, [which, ranks], [half, state],
-            [row, q, weighted, attended[which], *stats], after=after,
+            [held["row"], q, weighted, attended[which], *stats], after=after,
         )
         return out
 
     def back_work(token):
         out = call(
             back_kernel, [ranks], [((rows, width), BF16, HBM)] * 2 + [wide, wide],
-            [row, q, scores, gain, *k, *v, held["g", 0], held["g", 1], *attended, *carried, *stats],
+            [held["row"], q, scores, gain, *k, *v, held["g", 0], held["g", 1], *attended, *carried, *stats],
             after=[token],
             scratch=[VMEM((rows, width), BF16), VMEM((rows, width), BF16), DMA((4,))],
         )
@@ -381,7 +391,7 @@
         n = 5 + CHUNKS
         done = call(
             last_kernel, [which, CHUNKS], [((rows, width), BF16, HBM)] * 2,
-            [row, k[which], v[which], part_k, part_v, *came], after=done,
+            [held["row"], k[which], v[which], part_k, part_v, *came], after=done,
             scratch=[VMEM(*half), VMEM(*half), DMA((heads,))],
             aliases={n: 0, n + 1: 1} if done else {},
         )

time: 59.6 us -> 64.3 us (1.079)
  the two profiles are of different devices: /device:TPU:1 before, /device:TPU:7 now
where the time goes in v4:
time: 64.3 us; the launch traced here: 64 us
  starting transfers between devices  40.4 us (63%)
  Pallas kernels  13.3 us (21%)
  waiting for transfers between devices  9.34 us (15%)
  between operations  0.86 us (1%)
    ppermute x8, starting transfers between devices, hop(): return lax.ppermute(value, 'ctx', pairs)  23.7 us
    pallas_call x20, Pallas kernels, call(): pl.pallas_call(lambda *refs: kernel(*fixed, *refs), out_shape=[jax.ShapeD...  13.3 us
    ppermute x6, starting transfers between devices, swap(): return lax.ppermute(value, 'ctx', [(i, i ^ 1) for i in range(blocks)])  11.7 us
    ppermute x8, waiting for transfers between devices, hop(): return lax.ppermute(value, 'ctx', pairs)  6.58 us
    ppermute x3, starting transfers between devices, local(): lax.ppermute(stats[0], 'head', [(i, (i + apart) % ranks) for i in range(r...  5 us
    ppermute x3, waiting for transfers between devices, local(): lax.ppermute(stats[0], 'head', [(i, (i + apart) % ranks) for i in range(r...  1.72 us
  transfers between devices with their start and end apart: 17, of which 9 were waited for; matrix products, arithmetic and copies ran while one was open for 0% of the time, Pallas kernels for 15%

profile of v4, /device:TPU:7, one launch (start us, length us, event | category | flops | bytes accessed | tf_op | source)
XLA Modules:
  0.0 64.0 jit_solution(2816990575814229835)
XLA Ops:
  0.6 1.3 %state.2 = (f32[520,128]{1,0:T(8,128)S(1)}, bf16[256,512]{1,0:T(8,128)(2,1)S(1)}, bf16[256,512]{1,0:T(8,128)(2,1)S(1)}, s32[1,256]{1,0:T(1,128)S(1)}) custom-call(s32[1,256]{1,0:T(1,128)} %bitcast.3, bf16[256,1024]{1,0:T(8,128)(2,1)} %refs_1_.3, bf16[256,1024]{1,0:T(8,128)(2,1)} %refs_2_.3), custom_call_target="tpu_custom_call" | custom-call | tf_op jit(solution)/shard_map/state/pallas_call | solution.py:270
  2.0 0.8 %collective-permute-start = (f32[520,128]{1,0:T(8,128)S(1)}, f32[520,128]{1,0:T(8,128)S(1)}, u32[]{:S(2)}, u32[]{:S(2)}) collective-permute-start(f32[520,128]{1,0:T(8,128)S(1)} %get-tuple-element.47.refs_3_), channel_id=1, source_target_pairs={{0,4},{4,0},{8,12},{12,8},{16,20},{20,16},{24,28},{28,24},{32,36},... | collective-permute-start | bytes 798728 | tf_op jit(solution)/shard_map/ppermute | solution.py:287
  2.7 1.3 %state.3 = (f32[520,128]{1,0:T(8,128)S(1)}, bf16[256,512]{1,0:T(8,128)(2,1)S(1)}, bf16[256,512]{1,0:T(8,128)(2,1)S(1)}) custom-call(s32[1,256]{1,0:T(1,128)S(1)} %get-tuple-element.46.refs_0_, bf16[256,1024]{1,0:T(8,128)(2,1)} %refs_1_.3, bf16[256,1024]{1,0:T(8,128)(2,1)} %refs_2_.3, f32[520,128]{1,0:T(8,128)S(1)} %get-tuple-element.47.refs_3_), custom_call_target="tpu_custom_call" | custom-call | tf_op jit(solution)/shard_map/state/pallas_call | solution.py:270
  4.1 0.0 collective-permute-done.refs_1_.refs_2_
  4.1 0.1 pair.2
  4.2 3.5 %collective-permute-start.3 = (f32[264,128]{1,0:T(8,128)S(1)}, f32[264,128]{1,0:T(8,128)S(1)}, u32[]{:S(2)}, u32[]{:S(2)}) collective-permute-start(f32[264,128]{1,0:T(8,128)S(1)} %get-tuple-element.53.refs_8_.refs_0_), channel_id=1, source_target_pairs={{0,8},{4,12},{8,16},{12,20},{16,24},{20,28},{24,32},{28,36},{32,40... | collective-permute-start | bytes 405512 | tf_op jit(solution)/shard_map/ppermute | solution.py:291
  7.7 3.5 %collective-permute-start.1 = (f32[264,128]{1,0:T(8,128)S(1)}, f32[264,128]{1,0:T(8,128)S(1)}, u32[]{:S(2)}, u32[]{:S(2)}) collective-permute-start(f32[264,128]{1,0:T(8,128)S(1)} %get-tuple-element.59.refs_0_), channel_id=1, source_target_pairs={{0,8},{4,12},{8,16},{12,20},{16,24},{20,28},{24,32},{28,36},{32,40... | collective-permute-start | bytes 405512 | tf_op jit(solution)/shard_map/ppermute | solution.py:291
  11.3 2.2 %local.1 = (bf16[8,256,256]{2,1,0:T(8,128)(2,1)S(1)}, f32[256,1024]{1,0:T(8,128)S(1)}, bf16[256,1024]{1,0:T(8,128)(2,1)S(1)}, f32[256,1024]{1,0:T(8,128)S(1)}, f32[1,1024]{1,0:T(1,128)S(1)}) custom-call(s32[1,256]{1,0:T(1,128)S(1)} %get-tuple-element.46.refs_0_, bf16[256,512]{1,0:T(8,128)(2,1)S(1)} %get-tuple-element.48.refs_1_.refs_4_, ...), custom_call_target="tpu_custom_call" | custom-call | tf_op jit(solution)/shard_map/local/pallas_call | solution.py:270
  13.5 2.2 %collective-permute-done.3.refs_1_ = f32[264,128]{1,0:T(8,128)S(1)} collective-permute-done((f32[264,128]{1,0:T(8,128)S(1)}, f32[264,128]{1,0:T(8,128)S(1)}, u32[]{:S(2)}, u32[]{:S(2)}) %collective-permute-start.3) | collective-permute-done | bytes 135200 | tf_op jit(solution)/shard_map/ppermute | solution.py:291
  15.7 1.9 %collective-permute-start.4 = (f32[264,128]{1,0:T(8,128)S(1)}, f32[264,128]{1,0:T(8,128)S(1)}, u32[]{:S(2)}, u32[]{:S(2)}) collective-permute-start(f32[264,128]{1,0:T(8,128)S(1)} %merge.5), channel_id=1, source_target_pairs={{0,8},{4,12},{8,16},{12,20},{16,24},{20,28},{24,32},{28,36},{32,40... | collective-permute-start | bytes 405512 | tf_op jit(solution)/shard_map/ppermute | solution.py:291
  17.7 0.9 %collective-permute-done.1.refs_1_ = f32[264,128]{1,0:T(8,128)S(1)} collective-permute-done((f32[264,128]{1,0:T(8,128)S(1)}, f32[264,128]{1,0:T(8,128)S(1)}, u32[]{:S(2)}, u32[]{:S(2)}) %collective-permute-start.1) | collective-permute-done | bytes 135200 | tf_op jit(solution)/shard_map/ppermute | solution.py:291
  18.6 3.2 %collective-permute-start.2 = (f32[264,128]{1,0:T(8,128)S(1)}, f32[264,128]{1,0:T(8,128)S(1)}, u32[]{:S(2)}, u32[]{:S(2)}) collective-permute-start(f32[264,128]{1,0:T(8,128)S(1)} %merge.4), channel_id=1, source_target_pairs={{0,8},{4,12},{8,16},{12,20},{16,24},{20,28},{24,32},{28,36},{32,40... | collective-permute-start | bytes 405512 | tf_op jit(solution)/shard_map/ppermute | solution.py:291
  21.9 1.7 %collective-permute-done.4.refs_0_ = f32[264,128]{1,0:T(8,128)S(1)} collective-permute-done((f32[264,128]{1,0:T(8,128)S(1)}, f32[264,128]{1,0:T(8,128)S(1)}, u32[]{:S(2)}, u32[]{:S(2)}) %collective-permute-start.4) | collective-permute-done | bytes 135200 | tf_op jit(solution)/shard_map/ppermute | solution.py:291
  23.6 2.4 %collective-permute-start.6 = (f32[264,128]{1,0:T(8,128)S(1)}, f32[264,128]{1,0:T(8,128)S(1)}, u32[]{:S(2)}, u32[]{:S(2)}) collective-permute-start(f32[264,128]{1,0:T(8,128)S(1)} %get-tuple-element.64), channel_id=1, source_target_pairs={{0,4},{4,0},{8,12},{12,8},{16,20},{20,16},{24,28},{28,24},{32,36},... | collective-permute-start | bytes 405512 | tf_op jit(solution)/shard_map/ppermute | solution.py:287
  26.1 1.2 %collective-permute-done.2.refs_0_ = f32[264,128]{1,0:T(8,128)S(1)} collective-permute-done((f32[264,128]{1,0:T(8,128)S(1)}, f32[264,128]{1,0:T(8,128)S(1)}, u32[]{:S(2)}, u32[]{:S(2)}) %collective-permute-start.2) | collective-permute-done | bytes 135200 | tf_op jit(solution)/shard_map/ppermute | solution.py:291
  27.3 1.6 %collective-permute-start.5 = (f32[264,128]{1,0:T(8,128)S(1)}, f32[264,128]{1,0:T(8,128)S(1)}, u32[]{:S(2)}, u32[]{:S(2)}) collective-permute-start(f32[264,128]{1,0:T(8,128)S(1)} %get-tuple-element.63), channel_id=1, source_target_pairs={{0,4},{4,0},{8,12},{12,8},{16,20},{20,16},{24,28},{28,24},{32,36},... | collective-permute-start | bytes 405512 | tf_op jit(solution)/shard_map/ppermute | solution.py:287
  28.8 0.7 %attend.2 = (bf16[256,512]{1,0:T(8,128)(2,1)S(1)}, bf16[512,128]{1,0:T(8,128)(2,1)S(1)}, f32[8,256]{1,0:T(8,128)S(1)}) custom-call(s32[1,256]{1,0:T(1,128)S(1)} %get-tuple-element.46.refs_0_, bf16[256,1024]{1,0:T(8,128)(2,1)S(1)} %get-tuple-element.54.refs_1_, f32[256,1024]{1,0:T(8,128)S(1)} %get-tuple-element.58.refs_2_, ...), custom_call_target="tpu_custom_call" | custom-call | tf_op jit(solution)/shard_map/attend/pallas_call | solution.py:270
  29.5 0.0 collective-permute-done.6.refs_5_
  29.5 0.3 collective-permute-done.5.refs_4_
  29.8 0.7 %attend.3 = (bf16[256,512]{1,0:T(8,128)(2,1)S(1)}, bf16[512,128]{1,0:T(8,128)(2,1)S(1)}, f32[8,256]{1,0:T(8,128)S(1)}) custom-call(s32[1,256]{1,0:T(1,128)S(1)} %get-tuple-element.46.refs_0_, bf16[256,1024]{1,0:T(8,128)(2,1)S(1)} %get-tuple-element.54.refs_1_, f32[256,1024]{1,0:T(8,128)S(1)} %get-tuple-element.58.refs_2_, ...), custom_call_target="tpu_custom_call" | custom-call | tf_op jit(solution)/shard_map/attend/pallas_call | solution.py:270
  30.5 1.3 %collective-permute-start.7 = (f32[8,256]{1,0:T(8,128)S(1)}, f32[8,256]{1,0:T(8,128)S(1)}, u32[]{:S(2)}, u32[]{:S(2)}) collective-permute-start(f32[8,256]{1,0:T(8,128)S(1)} %get-tuple-element.66.refs_4_.refs_14_), channel_id=1, source_target_pairs={{0,1},{1,2},{2,3},{3,0},{4,5},{5,6},{6,7},{7,4},{8,9},{9,10},{10,1... | collective-permute-start | bytes 24584 | tf_op jit(solution)/shard_map/ppermute | solution.py:365
  31.8 2.6 %collective-permute-start.8 = (f32[8,256]{1,0:T(8,128)S(1)}, f32[8,256]{1,0:T(8,128)S(1)}, u32[]{:S(2)}, u32[]{:S(2)}) collective-permute-start(f32[8,256]{1,0:T(8,128)S(1)} %get-tuple-element.66.refs_4_.refs_14_), channel_id=1, source_target_pairs={{0,2},{1,3},{2,0},{3,1},{4,6},{5,7},{6,4},{7,5},{8,10},{9,11},{10,... | collective-permute-start | bytes 24584 | tf_op jit(solution)/shard_map/ppermute | solution.py:365
  34.5 1.1 %collective-permute-start.9 = (f32[8,256]{1,0:T(8,128)S(1)}, f32[8,256]{1,0:T(8,128)S(1)}, u32[]{:S(2)}, u32[]{:S(2)}) collective-permute-start(f32[8,256]{1,0:T(8,128)S(1)} %get-tuple-element.66.refs_4_.refs_14_), channel_id=1, source_target_pairs={{0,3},{1,0},{2,1},{3,2},{4,7},{5,4},{6,5},{7,6},{8,11},{9,8},{10,9... | collective-permute-start | bytes 24584 | tf_op jit(solution)/shard_map/ppermute | solution.py:365
  35.5 0.0 collective-permute-done.7.refs_5_.refs_15_
  35.5 0.3 collective-permute-done.8.refs_6_.refs_16_
  35.8 1.4 %collective-permute-done.9.refs_7_.refs_17_ = f32[8,256]{1,0:T(8,128)S(1)} collective-permute-done((f32[8,256]{1,0:T(8,128)S(1)}, f32[8,256]{1,0:T(8,128)S(1)}, u32[]{:S(2)}, u32[]{:S(2)}) %collective-permute-start.9) | collective-permute-done | bytes 8224 | tf_op jit(solution)/shard_map/ppermute | solution.py:365
  37.2 0.4 grad.2
  37.7 1.9 %collective-permute-start.10 = (f32[520,128]{1,0:T(8,128)S(1)}, f32[520,128]{1,0:T(8,128)S(1)}, u32[]{:S(2)}, u32[]{:S(2)}) collective-permute-start(f32[520,128]{1,0:T(8,128)S(1)} %get-tuple-element.68.refs_8_), channel_id=1, source_target_pairs={{0,4},{4,0},{8,12},{12,8},{16,20},{20,16},{24,28},{28,24},{32,36},... | collective-permute-start | bytes 798728 | tf_op jit(solution)/shard_map/ppermute | solution.py:287
  39.6 0.4 grad.3
  40.0 0.7 %collective-permute-done.10.refs_1_.refs_2_ = f32[520,128]{1,0:T(8,128)S(1)} collective-permute-done((f32[520,128]{1,0:T(8,128)S(1)}, f32[520,128]{1,0:T(8,128)S(1)}, u32[]{:S(2)}, u32[]{:S(2)}) %collective-permute-start.10) | collective-permute-done | bytes 266272 | tf_op jit(solution)/shard_map/ppermute | solution.py:287
  40.8 2.7 %collective-permute-start.14 = (f32[264,128]{1,0:T(8,128)S(1)}, f32[264,128]{1,0:T(8,128)S(1)}, u32[]{:S(2)}, u32[]{:S(2)}) collective-permute-start(f32[264,128]{1,0:T(8,128)S(1)} %get-tuple-element.74.refs_18_.refs_0_), channel_id=1, source_target_pairs={{8,0},{12,4},{16,8},{20,12},{24,16},{28,20},{32,24},{36,28},{40,32... | collective-permute-start | bytes 405512 | tf_op jit(solution)/shard_map/ppermute | solution.py:291
  43.5 1.9 %collective-permute-start.11 = (f32[264,128]{1,0:T(8,128)S(1)}, f32[264,128]{1,0:T(8,128)S(1)}, u32[]{:S(2)}, u32[]{:S(2)}) collective-permute-start(f32[264,128]{1,0:T(8,128)S(1)} %get-tuple-element.79.refs_0_), channel_id=1, source_target_pairs={{8,0},{12,4},{16,8},{20,12},{24,16},{28,20},{32,24},{36,28},{40,32... | collective-permute-start | bytes 405512 | tf_op jit(solution)/shard_map/ppermute | solution.py:291
  45.4 3.7 %back.1 = (bf16[256,1024]{1,0:T(8,128)(2,1)}, bf16[256,1024]{1,0:T(8,128)(2,1)}, f32[256,1024]{1,0:T(8,128)S(1)}, f32[256,1024]{1,0:T(8,128)S(1)}) custom-call(s32[1,256]{1,0:T(1,128)S(1)} %get-tuple-element.46.refs_0_, bf16[256,1024]{1,0:T(8,128)(2,1)S(1)} %get-tuple-element.54.refs_1_, bf16[8,256,256]{2,1,0:T(8,128)(2,1)S(1)} %get-tuple-element.55.refs_2_, ...), custom_call_target="tpu_custom_call" | custom-call | tf_op jit(solution)/shard_map/back/pallas_call | solution.py:270
  49.1 0.0 collective-permute-done.14.refs_1_
  49.2 3.1 %collective-permute-start.15 = (f32[264,128]{1,0:T(8,128)S(1)}, f32[264,128]{1,0:T(8,128)S(1)}, u32[]{:S(2)}, u32[]{:S(2)}) collective-permute-start(f32[264,128]{1,0:T(8,128)S(1)} %merge.7), channel_id=1, source_target_pairs={{8,0},{12,4},{16,8},{20,12},{24,16},{28,20},{32,24},{36,28},{40,32... | collective-permute-start | bytes 405512 | tf_op jit(solution)/shard_map/ppermute | solution.py:291
  52.3 0.0 collective-permute-done.11.refs_1_
  52.3 3.7 %collective-permute-start.12 = (f32[264,128]{1,0:T(8,128)S(1)}, f32[264,128]{1,0:T(8,128)S(1)}, u32[]{:S(2)}, u32[]{:S(2)}) collective-permute-start(f32[264,128]{1,0:T(8,128)S(1)} %merge.6), channel_id=1, source_target_pairs={{8,0},{12,4},{16,8},{20,12},{24,16},{28,20},{32,24},{36,28},{40,32... | collective-permute-start | bytes 405512 | tf_op jit(solution)/shard_map/ppermute | solution.py:291
  56.1 0.0 collective-permute-done.15.refs_0_
  56.1 1.6 %collective-permute-start.16 = (f32[264,128]{1,0:T(8,128)S(1)}, f32[264,128]{1,0:T(8,128)S(1)}, u32[]{:S(2)}, u32[]{:S(2)}) collective-permute-start(f32[264,128]{1,0:T(8,128)S(1)} %get-tuple-element.81), channel_id=1, source_target_pairs={{0,4},{4,0},{8,12},{12,8},{16,20},{20,16},{24,28},{28,24},{32,36},... | collective-permute-start | bytes 405512 | tf_op jit(solution)/shard_map/ppermute | solution.py:287
  57.7 0.5 collective-permute-done.12.refs_0_
  58.2 3.5 %collective-permute-start.13 = (f32[264,128]{1,0:T(8,128)S(1)}, f32[264,128]{1,0:T(8,128)S(1)}, u32[]{:S(2)}, u32[]{:S(2)}) collective-permute-start(f32[264,128]{1,0:T(8,128)S(1)} %get-tuple-element.80), channel_id=1, source_target_pairs={{0,4},{4,0},{8,12},{12,8},{16,20},{20,16},{24,28},{28,24},{32,36},... | collective-permute-start | bytes 405512 | tf_op jit(solution)/shard_map/ppermute | solution.py:287
  61.7 1.1 %last.2 = (bf16[256,1024]{1,0:T(8,128)(2,1)}, bf16[256,1024]{1,0:T(8,128)(2,1)}) custom-call(s32[1,256]{1,0:T(1,128)S(1)} %get-tuple-element.46.refs_0_, bf16[256,512]{1,0:T(8,128)(2,1)S(1)} %get-tuple-element.48.refs_1_.refs_4_, bf16[256,512]{1,0:T(8,128)(2,1)S(1)} %get-tuple-element.50.refs_3_.refs_6_.refs_2_, ...), custom_call_target="tpu_custom_call" | custom-call | tf_op jit(solution)/shard_map/last/pallas_call | solution.py:270
  62.8 0.0 collective-permute-done.16.refs_6_
  62.8 0.0 collective-permute-done.13.refs_5_
  62.8 1.1 %last.3 = (bf16[256,1024]{1,0:T(8,128)(2,1)}, bf16[256,1024]{1,0:T(8,128)(2,1)}) custom-call(s32[1,256]{1,0:T(1,128)S(1)} %get-tuple-element.46.refs_0_, bf16[256,512]{1,0:T(8,128)(2,1)S(1)} %get-tuple-element.49.refs_2_.refs_5_.refs_1_, ...), custom_call_target="tpu_custom_call", output_to_operand_aliasing={{0}: (7, {}), {1}: (8, {})} | custom-call | tf_op jit(solution)/shard_map/last/pallas_call | solution.py:270
  (9 shorter events, 0.2 us)
Async XLA Ops:
  2.0 2.1 %collective-permute-start = (f32[520,128]{1,0:T(8,128)S(1)}, f32[520,128]{1,0:T(8,128)S(1)}, u32[]{:S(2)}, u32[]{:S(2)}) collective-permute-start(f32[520,128]{1,0:T(8,128)S(1)} %get-tuple-element.47.refs_3_), channel_id=1, source_target_pairs={{0,4},{4,0},{8,12},{12,8},{16,20},{20,16},{24,28},{28,24},{32,36},... | collective-permute-start | bytes 798728 | tf_op jit(solution)/shard_map/ppermute | solution.py:287
  4.2 11.5 %collective-permute-start.3 = (f32[264,128]{1,0:T(8,128)S(1)}, f32[264,128]{1,0:T(8,128)S(1)}, u32[]{:S(2)}, u32[]{:S(2)}) collective-permute-start(f32[264,128]{1,0:T(8,128)S(1)} %get-tuple-element.53.refs_8_.refs_0_), channel_id=1, source_target_pairs={{0,8},{4,12},{8,16},{12,20},{16,24},{20,28},{24,32},{28,36},{32,40... | collective-permute-start | bytes 405512 | tf_op jit(solution)/shard_map/ppermute | solution.py:291
  7.7 10.9 %collective-permute-start.1 = (f32[264,128]{1,0:T(8,128)S(1)}, f32[264,128]{1,0:T(8,128)S(1)}, u32[]{:S(2)}, u32[]{:S(2)}) collective-permute-start(f32[264,128]{1,0:T(8,128)S(1)} %get-tuple-element.59.refs_0_), channel_id=1, source_target_pairs={{0,8},{4,12},{8,16},{12,20},{16,24},{20,28},{24,32},{28,36},{32,40... | collective-permute-start | bytes 405512 | tf_op jit(solution)/shard_map/ppermute | solution.py:291
  15.7 7.9 %collective-permute-start.4 = (f32[264,128]{1,0:T(8,128)S(1)}, f32[264,128]{1,0:T(8,128)S(1)}, u32[]{:S(2)}, u32[]{:S(2)}) collective-permute-start(f32[264,128]{1,0:T(8,128)S(1)} %merge.5), channel_id=1, source_target_pairs={{0,8},{4,12},{8,16},{12,20},{16,24},{20,28},{24,32},{28,36},{32,40... | collective-permute-start | bytes 405512 | tf_op jit(solution)/shard_map/ppermute | solution.py:291
  18.6 8.6 %collective-permute-start.2 = (f32[264,128]{1,0:T(8,128)S(1)}, f32[264,128]{1,0:T(8,128)S(1)}, u32[]{:S(2)}, u32[]{:S(2)}) collective-permute-start(f32[264,128]{1,0:T(8,128)S(1)} %merge.4), channel_id=1, source_target_pairs={{0,8},{4,12},{8,16},{12,20},{16,24},{20,28},{24,32},{28,36},{32,40... | collective-permute-start | bytes 405512 | tf_op jit(solution)/shard_map/ppermute | solution.py:291
  23.6 5.9 %collective-permute-start.6 = (f32[264,128]{1,0:T(8,128)S(1)}, f32[264,128]{1,0:T(8,128)S(1)}, u32[]{:S(2)}, u32[]{:S(2)}) collective-permute-start(f32[264,128]{1,0:T(8,128)S(1)} %get-tuple-element.64), channel_id=1, source_target_pairs={{0,4},{4,0},{8,12},{12,8},{16,20},{20,16},{24,28},{28,24},{32,36},... | collective-permute-start | bytes 405512 | tf_op jit(solution)/shard_map/ppermute | solution.py:287
  27.3 2.6 %collective-permute-start.5 = (f32[264,128]{1,0:T(8,128)S(1)}, f32[264,128]{1,0:T(8,128)S(1)}, u32[]{:S(2)}, u32[]{:S(2)}) collective-permute-start(f32[264,128]{1,0:T(8,128)S(1)} %get-tuple-element.63), channel_id=1, source_target_pairs={{0,4},{4,0},{8,12},{12,8},{16,20},{20,16},{24,28},{28,24},{32,36},... | collective-permute-start | bytes 405512 | tf_op jit(solution)/shard_map/ppermute | solution.py:287
  30.5 5.0 %collective-permute-start.7 = (f32[8,256]{1,0:T(8,128)S(1)}, f32[8,256]{1,0:T(8,128)S(1)}, u32[]{:S(2)}, u32[]{:S(2)}) collective-permute-start(f32[8,256]{1,0:T(8,128)S(1)} %get-tuple-element.66.refs_4_.refs_14_), channel_id=1, source_target_pairs={{0,1},{1,2},{2,3},{3,0},{4,5},{5,6},{6,7},{7,4},{8,9},{9,10},{10,1... | collective-permute-start | bytes 24584 | tf_op jit(solution)/shard_map/ppermute | solution.py:365
  31.8 4.0 %collective-permute-start.8 = (f32[8,256]{1,0:T(8,128)S(1)}, f32[8,256]{1,0:T(8,128)S(1)}, u32[]{:S(2)}, u32[]{:S(2)}) collective-permute-start(f32[8,256]{1,0:T(8,128)S(1)} %get-tuple-element.66.refs_4_.refs_14_), channel_id=1, source_target_pairs={{0,2},{1,3},{2,0},{3,1},{4,6},{5,7},{6,4},{7,5},{8,10},{9,11},{10,... | collective-permute-start | bytes 24584 | tf_op jit(solution)/shard_map/ppermute | solution.py:365
  34.5 2.8 %collective-permute-start.9 = (f32[8,256]{1,0:T(8,128)S(1)}, f32[8,256]{1,0:T(8,128)S(1)}, u32[]{:S(2)}, u32[]{:S(2)}) collective-permute-start(f32[8,256]{1,0:T(8,128)S(1)} %get-tuple-element.66.refs_4_.refs_14_), channel_id=1, source_target_pairs={{0,3},{1,0},{2,1},{3,2},{4,7},{5,4},{6,5},{7,6},{8,11},{9,8},{10,9... | collective-permute-start | bytes 24584 | tf_op jit(solution)/shard_map/ppermute | solution.py:365
  37.7 3.0 %collective-permute-start.10 = (f32[520,128]{1,0:T(8,128)S(1)}, f32[520,128]{1,0:T(8,128)S(1)}, u32[]{:S(2)}, u32[]{:S(2)}) collective-permute-start(f32[520,128]{1,0:T(8,128)S(1)} %get-tuple-element.68.refs_8_), channel_id=1, source_target_pairs={{0,4},{4,0},{8,12},{12,8},{16,20},{20,16},{24,28},{28,24},{32,36},... | collective-permute-start | bytes 798728 | tf_op jit(solution)/shard_map/ppermute | solution.py:287
  40.8 8.4 %collective-permute-start.14 = (f32[264,128]{1,0:T(8,128)S(1)}, f32[264,128]{1,0:T(8,128)S(1)}, u32[]{:S(2)}, u32[]{:S(2)}) collective-permute-start(f32[264,128]{1,0:T(8,128)S(1)} %get-tuple-element.74.refs_18_.refs_0_), channel_id=1, source_target_pairs={{8,0},{12,4},{16,8},{20,12},{24,16},{28,20},{32,24},{36,28},{40,32... | collective-permute-start | bytes 405512 | tf_op jit(solution)/shard_map/ppermute | solution.py:291
  43.5 8.8 %collective-permute-start.11 = (f32[264,128]{1,0:T(8,128)S(1)}, f32[264,128]{1,0:T(8,128)S(1)}, u32[]{:S(2)}, u32[]{:S(2)}) collective-permute-start(f32[264,128]{1,0:T(8,128)S(1)} %get-tuple-element.79.refs_0_), channel_id=1, source_target_pairs={{8,0},{12,4},{16,8},{20,12},{24,16},{28,20},{32,24},{36,28},{40,32... | collective-permute-start | bytes 405512 | tf_op jit(solution)/shard_map/ppermute | solution.py:291
  49.2 6.9 %collective-permute-start.15 = (f32[264,128]{1,0:T(8,128)S(1)}, f32[264,128]{1,0:T(8,128)S(1)}, u32[]{:S(2)}, u32[]{:S(2)}) collective-permute-start(f32[264,128]{1,0:T(8,128)S(1)} %merge.7), channel_id=1, source_target_pairs={{8,0},{12,4},{16,8},{20,12},{24,16},{28,20},{32,24},{36,28},{40,32... | collective-permute-start | bytes 405512 | tf_op jit(solution)/shard_map/ppermute | solution.py:291
  52.3 5.9 %collective-permute-start.12 = (f32[264,128]{1,0:T(8,128)S(1)}, f32[264,128]{1,0:T(8,128)S(1)}, u32[]{:S(2)}, u32[]{:S(2)}) collective-permute-start(f32[264,128]{1,0:T(8,128)S(1)} %merge.6), channel_id=1, source_target_pairs={{8,0},{12,4},{16,8},{20,12},{24,16},{28,20},{32,24},{36,28},{40,32... | collective-permute-start | bytes 405512 | tf_op jit(solution)/shard_map/ppermute | solution.py:291
  56.1 6.7 %collective-permute-start.16 = (f32[264,128]{1,0:T(8,128)S(1)}, f32[264,128]{1,0:T(8,128)S(1)}, u32[]{:S(2)}, u32[]{:S(2)}) collective-permute-start(f32[264,128]{1,0:T(8,128)S(1)} %get-tuple-element.81), channel_id=1, source_target_pairs={{0,4},{4,0},{8,12},{12,8},{16,20},{20,16},{24,28},{28,24},{32,36},... | collective-permute-start | bytes 405512 | tf_op jit(solution)/shard_map/ppermute | solution.py:287
  58.2 4.6 %collective-permute-start.13 = (f32[264,128]{1,0:T(8,128)S(1)}, f32[264,128]{1,0:T(8,128)S(1)}, u32[]{:S(2)}, u32[]{:S(2)}) collective-permute-start(f32[264,128]{1,0:T(8,128)S(1)} %get-tuple-element.80), channel_id=1, source_target_pairs={{0,4},{4,0},{8,12},{12,8},{16,20},{20,16},{24,28},{28,24},{32,36},... | collective-permute-start | bytes 405512 | tf_op jit(solution)/shard_map/ppermute | solution.py:287

commit v5 on v4

--- a/solution.py
+++ b/solution.py
@@ -64,23 +64,27 @@
     else:
         out, k, v, sems = rest[-4:]
     rows, width = k.shape
-    span = columns(half, width)
-    copies = [
-        pltpu.make_async_copy(k_hbm.at[:, span], k, sems.at[1]),
-        pltpu.make_async_copy(v_hbm.at[:, span], v, sems.at[2]),
-    ]
+    n = width // HD
+    at_core = core() if half == 0 else 1 - core()
+    copies = []
     if half:
-        copies.insert(0, pltpu.make_async_copy(row, row_out, sems.at[0]))
+        copies.append(pltpu.make_async_copy(row, row_out, sems.at[2 * n]))
         row = row_out
+    for h in range(n):
+        span = pl.ds(pl.multiple_of(at_core * width + h * HD, HD), HD)
+        for i, (hbm, held) in enumerate(((k_hbm, k), (v_hbm, v))):
+            copies.append(
+                pltpu.make_async_copy(hbm.at[:, span], held.at[:, head(h)], sems.at[2 * h + i])
+            )
     for copy in copies:
         copy.start()
     if half:
         copies.pop(0).wait()
     keep = in_doc(row, rows - 1).astype(BF16)
     out[width:, :] = jnp.broadcast_to(tag(row, rows - 1), (TAG, HD))
-    for copy in copies:
-        copy.wait()
-    for h in range(width // HD):
+    for h in range(n):
+        copies[2 * h].wait()
+        copies[2 * h + 1].wait()
         out[head(h), :] = dot(k[:, head(h)] * keep, v[:, head(h)], TN)
 
 
@@ -287,8 +291,7 @@
         return lax.ppermute(value, "ctx", [(i, i ^ 1) for i in range(blocks)])
 
     def hop(value):
-        pairs = [(i, i + step) for i in range(blocks) if 0 <= i + step < blocks]
-        return lax.ppermute(value, "ctx", pairs)
+        return lax.ppermute(value, "ctx", [(i, (i + step) % blocks) for i in range(blocks)])
 
     sent = other()
     came = swap(sent)
@@ -308,7 +311,7 @@
     return keep, back, work
 
 
-CHUNKS = 2
+CHUNKS = 1
 
 
 def local(queries, key_rows, value_rows, grad_out, doc_ids, out_gain):
@@ -327,7 +330,7 @@
         out, held["k", which], held["v", which], *row = call(
             state_kernel, [which], [state, half, half] + [((1, rows), jnp.int32)] * which,
             [[ids] if which else held["row"], [key_rows], [value_rows]],
-            after=after, scratch=[DMA((3,))],
+            after=after, scratch=[DMA((heads + 1,))],
         )
         if which:
             (held["row"],) = row

time: 64.3 us -> 66.3 us (1.031)
  the two profiles are of different devices: /device:TPU:7 before, /device:TPU:1 now
where the time goes in v5:
time: 66.3 us; the launch traced here: 66.1 us
  waiting for transfers between devices  34.2 us (52%)
  starting transfers between devices  16.8 us (25%)
  Pallas kernels  14.2 us (21%)
  between operations  0.91 us (1%)
    ppermute x4, waiting for transfers between devices, hop(): lax.ppermute(value, 'ctx', [(i, (i + step) % blocks) for i in range(block...  29.9 us
    pallas_call x16, Pallas kernels, call(): pl.pallas_call(lambda *refs: kernel(*fixed, *refs), out_shape=[jax.ShapeD...  14.2 us
    ppermute x4, starting transfers between devices, swap(): return lax.ppermute(value, 'ctx', [(i, i ^ 1) for i in range(blocks)])  8.85 us
    ppermute x4, starting transfers between devices, hop(): lax.ppermute(value, 'ctx', [(i, (i + step) % blocks) for i in range(block...  4.11 us
    ppermute x3, starting transfers between devices, local(): lax.ppermute(stats[0], 'head', [(i, (i + apart) % ranks) for i in range(r...  3.8 us
    ppermute x3, waiting for transfers between devices, local(): lax.ppermute(stats[0], 'head', [(i, (i + apart) % ranks) for i in range(r...  3.05 us
  transfers between devices with their start and end apart: 11, of which 8 were waited for; matrix products, arithmetic and copies ran while one was open for 0% of the time, Pallas kernels for 15%

profile of v5, /device:TPU:1, one launch (start us, length us, event | category | flops | bytes accessed | tf_op | source)
XLA Modules:
  0.0 66.1 jit_solution(1284973247517382535)
XLA Ops:
  0.6 1.8 %state.2 = (f32[520,128]{1,0:T(8,128)S(1)}, bf16[256,512]{1,0:T(8,128)(2,1)S(1)}, bf16[256,512]{1,0:T(8,128)(2,1)S(1)}, s32[1,256]{1,0:T(1,128)S(1)}) custom-call(s32[1,256]{1,0:T(1,128)} %bitcast.3, bf16[256,1024]{1,0:T(8,128)(2,1)} %refs_1_.3, bf16[256,1024]{1,0:T(8,128)(2,1)} %refs_2_.3), custom_call_target="tpu_custom_call" | custom-call | tf_op jit(solution)/shard_map/state/pallas_call | solution.py:274
  2.4 3.3 %collective-permute-start = (f32[520,128]{1,0:T(8,128)S(1)}, f32[520,128]{1,0:T(8,128)S(1)}, u32[]{:S(2)}, u32[]{:S(2)}) collective-permute-start(f32[520,128]{1,0:T(8,128)S(1)} %get-tuple-element.39.refs_3_), channel_id=1, source_target_pairs={{0,4},{4,0},{8,12},{12,8},{16,20},{20,16},{24,28},{28,24},{32,36},... | collective-permute-start | bytes 798728 | tf_op jit(solution)/shard_map/ppermute | solution.py:291
  5.7 1.8 %state.3 = (f32[520,128]{1,0:T(8,128)S(1)}, bf16[256,512]{1,0:T(8,128)(2,1)S(1)}, bf16[256,512]{1,0:T(8,128)(2,1)S(1)}) custom-call(s32[1,256]{1,0:T(1,128)S(1)} %get-tuple-element.38.refs_0_, bf16[256,1024]{1,0:T(8,128)(2,1)} %refs_1_.3, bf16[256,1024]{1,0:T(8,128)(2,1)} %refs_2_.3, f32[520,128]{1,0:T(8,128)S(1)} %get-tuple-element.39.refs_3_), custom_call_target="tpu_custom_call" | custom-call | tf_op jit(solution)/shard_map/state/pallas_call | solution.py:274
  7.5 0.0 collective-permute-done.refs_1_.refs_2_
  7.5 0.1 pair.2.refs_8_.refs_0_
  7.6 0.1 collective-permute-start.1
  7.7 2.2 %local.1 = (bf16[8,256,256]{2,1,0:T(8,128)(2,1)S(1)}, f32[256,1024]{1,0:T(8,128)S(1)}, bf16[256,1024]{1,0:T(8,128)(2,1)S(1)}, f32[256,1024]{1,0:T(8,128)S(1)}, f32[1,1024]{1,0:T(1,128)S(1)}) custom-call(s32[1,256]{1,0:T(1,128)S(1)} %get-tuple-element.38.refs_0_, bf16[256,512]{1,0:T(8,128)(2,1)S(1)} %get-tuple-element.40.refs_1_.refs_4_, ...), custom_call_target="tpu_custom_call" | custom-call | tf_op jit(solution)/shard_map/local/pallas_call | solution.py:274
  9.9 10.6 %collective-permute-done.1.refs_1_ = f32[520,128]{1,0:T(8,128)S(1)} collective-permute-done((f32[520,128]{1,0:T(8,128)S(1)}, f32[520,128]{1,0:T(8,128)S(1)}, u32[]{:S(2)}, u32[]{:S(2)}) %collective-permute-start.1) | collective-permute-done | bytes 266272 | tf_op jit(solution)/shard_map/ppermute | solution.py:294
  20.5 0.1 collective-permute-start.2
  20.6 10.7 %collective-permute-done.2.refs_0_ = f32[520,128]{1,0:T(8,128)S(1)} collective-permute-done((f32[520,128]{1,0:T(8,128)S(1)}, f32[520,128]{1,0:T(8,128)S(1)}, u32[]{:S(2)}, u32[]{:S(2)}) %collective-permute-start.2) | collective-permute-done | bytes 266272 | tf_op jit(solution)/shard_map/ppermute | solution.py:294
  31.3 1.5 %collective-permute-start.3 = (f32[520,128]{1,0:T(8,128)S(1)}, f32[520,128]{1,0:T(8,128)S(1)}, u32[]{:S(2)}, u32[]{:S(2)}) collective-permute-start(f32[520,128]{1,0:T(8,128)S(1)} %get-tuple-element.52), channel_id=1, source_target_pairs={{0,4},{4,0},{8,12},{12,8},{16,20},{20,16},{24,28},{28,24},{32,36},... | collective-permute-start | bytes 798728 | tf_op jit(solution)/shard_map/ppermute | solution.py:291
  32.9 0.7 %attend.2 = (bf16[256,512]{1,0:T(8,128)(2,1)S(1)}, bf16[512,128]{1,0:T(8,128)(2,1)S(1)}, f32[8,256]{1,0:T(8,128)S(1)}) custom-call(s32[1,256]{1,0:T(1,128)S(1)} %get-tuple-element.38.refs_0_, bf16[256,1024]{1,0:T(8,128)(2,1)S(1)} %get-tuple-element.45.refs_1_, f32[256,1024]{1,0:T(8,128)S(1)} %get-tuple-element.49.refs_2_, ...), custom_call_target="tpu_custom_call" | custom-call | tf_op jit(solution)/shard_map/attend/pallas_call | solution.py:274
  33.5 0.5 collective-permute-done.3.refs_4_
  34.0 0.7 %attend.3 = (bf16[256,512]{1,0:T(8,128)(2,1)S(1)}, bf16[512,128]{1,0:T(8,128)(2,1)S(1)}, f32[8,256]{1,0:T(8,128)S(1)}) custom-call(s32[1,256]{1,0:T(1,128)S(1)} %get-tuple-element.38.refs_0_, bf16[256,1024]{1,0:T(8,128)(2,1)S(1)} %get-tuple-element.45.refs_1_, f32[256,1024]{1,0:T(8,128)S(1)} %get-tuple-element.49.refs_2_, ...), custom_call_target="tpu_custom_call" | custom-call | tf_op jit(solution)/shard_map/attend/pallas_call | solution.py:274
  34.7 2.8 %collective-permute-start.6 = (f32[8,256]{1,0:T(8,128)S(1)}, f32[8,256]{1,0:T(8,128)S(1)}, u32[]{:S(2)}, u32[]{:S(2)}) collective-permute-start(f32[8,256]{1,0:T(8,128)S(1)} %get-tuple-element.54.refs_4_.refs_14_), channel_id=1, source_target_pairs={{0,3},{1,0},{2,1},{3,2},{4,7},{5,4},{6,5},{7,6},{8,11},{9,8},{10,9... | collective-permute-start | bytes 24584 | tf_op jit(solution)/shard_map/ppermute | solution.py:368
  37.5 0.3 collective-permute-start.5
  37.8 0.7 %collective-permute-start.4 = (f32[8,256]{1,0:T(8,128)S(1)}, f32[8,256]{1,0:T(8,128)S(1)}, u32[]{:S(2)}, u32[]{:S(2)}) collective-permute-start(f32[8,256]{1,0:T(8,128)S(1)} %get-tuple-element.54.refs_4_.refs_14_), channel_id=1, source_target_pairs={{0,1},{1,2},{2,3},{3,0},{4,5},{5,6},{6,7},{7,4},{8,9},{9,10},{10,1... | collective-permute-start | bytes 24584 | tf_op jit(solution)/shard_map/ppermute | solution.py:368
  38.5 0.0 collective-permute-done.6.refs_7_.refs_17_
  38.5 3.0 %collective-permute-done.5.refs_6_.refs_16_ = f32[8,256]{1,0:T(8,128)S(1)} collective-permute-done((f32[8,256]{1,0:T(8,128)S(1)}, f32[8,256]{1,0:T(8,128)S(1)}, u32[]{:S(2)}, u32[]{:S(2)}) %collective-permute-start.5) | collective-permute-done | bytes 8224 | tf_op jit(solution)/shard_map/ppermute | solution.py:368
  41.5 0.1 collective-permute-done.4.refs_5_.refs_15_
  41.6 0.4 grad.2
  42.0 2.1 %collective-permute-start.7 = (f32[520,128]{1,0:T(8,128)S(1)}, f32[520,128]{1,0:T(8,128)S(1)}, u32[]{:S(2)}, u32[]{:S(2)}) collective-permute-start(f32[520,128]{1,0:T(8,128)S(1)} %get-tuple-element.56.refs_8_), channel_id=1, source_target_pairs={{0,4},{4,0},{8,12},{12,8},{16,20},{20,16},{24,28},{28,24},{32,36},... | collective-permute-start | bytes 798728 | tf_op jit(solution)/shard_map/ppermute | solution.py:291
  44.2 0.4 grad.3
  44.6 0.7 %collective-permute-done.7.refs_1_.refs_2_ = f32[520,128]{1,0:T(8,128)S(1)} collective-permute-done((f32[520,128]{1,0:T(8,128)S(1)}, f32[520,128]{1,0:T(8,128)S(1)}, u32[]{:S(2)}, u32[]{:S(2)}) %collective-permute-start.7) | collective-permute-done | bytes 266272 | tf_op jit(solution)/shard_map/ppermute | solution.py:291
  45.4 0.3 collective-permute-start.8
  45.6 3.7 %back.1 = (bf16[256,1024]{1,0:T(8,128)(2,1)}, bf16[256,1024]{1,0:T(8,128)(2,1)}, f32[256,1024]{1,0:T(8,128)S(1)}, f32[256,1024]{1,0:T(8,128)S(1)}) custom-call(s32[1,256]{1,0:T(1,128)S(1)} %get-tuple-element.38.refs_0_, bf16[256,1024]{1,0:T(8,128)(2,1)S(1)} %get-tuple-element.45.refs_1_, bf16[8,256,256]{2,1,0:T(8,128)(2,1)S(1)} %get-tuple-element.46.refs_2_, ...), custom_call_target="tpu_custom_call" | custom-call | tf_op jit(solution)/shard_map/back/pallas_call | solution.py:274
  49.4 3.8 %collective-permute-done.8.refs_1_ = f32[520,128]{1,0:T(8,128)S(1)} collective-permute-done((f32[520,128]{1,0:T(8,128)S(1)}, f32[520,128]{1,0:T(8,128)S(1)}, u32[]{:S(2)}, u32[]{:S(2)}) %collective-permute-start.8) | collective-permute-done | bytes 266272 | tf_op jit(solution)/shard_map/ppermute | solution.py:294
  53.2 3.7 %collective-permute-start.9 = (f32[520,128]{1,0:T(8,128)S(1)}, f32[520,128]{1,0:T(8,128)S(1)}, u32[]{:S(2)}, u32[]{:S(2)}) collective-permute-start(f32[520,128]{1,0:T(8,128)S(1)} %merge.3), channel_id=1, source_target_pairs={{0,248},{4,252},{8,0},{12,4},{16,8},{20,12},{24,16},{28,20},{32,24... | collective-permute-start | bytes 798728 | tf_op jit(solution)/shard_map/ppermute | solution.py:294
  56.9 4.8 %collective-permute-done.9.refs_0_ = f32[520,128]{1,0:T(8,128)S(1)} collective-permute-done((f32[520,128]{1,0:T(8,128)S(1)}, f32[520,128]{1,0:T(8,128)S(1)}, u32[]{:S(2)}, u32[]{:S(2)}) %collective-permute-start.9) | collective-permute-done | bytes 266272 | tf_op jit(solution)/shard_map/ppermute | solution.py:294
  61.8 1.9 %collective-permute-start.10 = (f32[520,128]{1,0:T(8,128)S(1)}, f32[520,128]{1,0:T(8,128)S(1)}, u32[]{:S(2)}, u32[]{:S(2)}) collective-permute-start(f32[520,128]{1,0:T(8,128)S(1)} %get-tuple-element.66), channel_id=1, source_target_pairs={{0,4},{4,0},{8,12},{12,8},{16,20},{20,16},{24,28},{28,24},{32,36},... | collective-permute-start | bytes 798728 | tf_op jit(solution)/shard_map/ppermute | solution.py:291
  63.7 1.1 %last.2 = (bf16[256,1024]{1,0:T(8,128)(2,1)}, bf16[256,1024]{1,0:T(8,128)(2,1)}) custom-call(s32[1,256]{1,0:T(1,128)S(1)} %get-tuple-element.38.refs_0_, bf16[256,512]{1,0:T(8,128)(2,1)S(1)} %get-tuple-element.40.refs_1_.refs_4_, bf16[256,512]{1,0:T(8,128)(2,1)S(1)} %get-tuple-element.42.refs_3_.refs_6_.refs_2_, ...), custom_call_target="tpu_custom_call" | custom-call | tf_op jit(solution)/shard_map/last/pallas_call | solution.py:274
  64.8 0.0 collective-permute-done.10.refs_5_
  64.8 1.1 %last.3 = (bf16[256,1024]{1,0:T(8,128)(2,1)}, bf16[256,1024]{1,0:T(8,128)(2,1)}) custom-call(s32[1,256]{1,0:T(1,128)S(1)} %get-tuple-element.38.refs_0_, bf16[256,512]{1,0:T(8,128)(2,1)S(1)} %get-tuple-element.41.refs_2_.refs_5_.refs_1_, ...), custom_call_target="tpu_custom_call", output_to_operand_aliasing={{0}: (6, {}), {1}: (7, {})} | custom-call | tf_op jit(solution)/shard_map/last/pallas_call | solution.py:274
  (5 shorter events, 0.2 us)
Async XLA Ops:
  2.4 5.1 %collective-permute-start = (f32[520,128]{1,0:T(8,128)S(1)}, f32[520,128]{1,0:T(8,128)S(1)}, u32[]{:S(2)}, u32[]{:S(2)}) collective-permute-start(f32[520,128]{1,0:T(8,128)S(1)} %get-tuple-element.39.refs_3_), channel_id=1, source_target_pairs={{0,4},{4,0},{8,12},{12,8},{16,20},{20,16},{24,28},{28,24},{32,36},... | collective-permute-start | bytes 798728 | tf_op jit(solution)/shard_map/ppermute | solution.py:291
  7.6 12.9 %collective-permute-start.1 = (f32[520,128]{1,0:T(8,128)S(1)}, f32[520,128]{1,0:T(8,128)S(1)}, u32[]{:S(2)}, u32[]{:S(2)}) collective-permute-start(f32[520,128]{1,0:T(8,128)S(1)} %pair.2.refs_8_.refs_0_), channel_id=1, source_target_pairs={{0,8},{4,12},{8,16},{12,20},{16,24},{20,28},{24,32},{28,36},{32,40... | collective-permute-start | bytes 798728 | tf_op jit(solution)/shard_map/ppermute | solution.py:294
  20.5 10.8 %collective-permute-start.2 = (f32[520,128]{1,0:T(8,128)S(1)}, f32[520,128]{1,0:T(8,128)S(1)}, u32[]{:S(2)}, u32[]{:S(2)}) collective-permute-start(f32[520,128]{1,0:T(8,128)S(1)} %merge.2), channel_id=1, source_target_pairs={{0,8},{4,12},{8,16},{12,20},{16,24},{20,28},{24,32},{28,36},{32,40... | collective-permute-start | bytes 798728 | tf_op jit(solution)/shard_map/ppermute | solution.py:294
  31.3 2.7 %collective-permute-start.3 = (f32[520,128]{1,0:T(8,128)S(1)}, f32[520,128]{1,0:T(8,128)S(1)}, u32[]{:S(2)}, u32[]{:S(2)}) collective-permute-start(f32[520,128]{1,0:T(8,128)S(1)} %get-tuple-element.52), channel_id=1, source_target_pairs={{0,4},{4,0},{8,12},{12,8},{16,20},{20,16},{24,28},{28,24},{32,36},... | collective-permute-start | bytes 798728 | tf_op jit(solution)/shard_map/ppermute | solution.py:291
  34.7 3.8 %collective-permute-start.6 = (f32[8,256]{1,0:T(8,128)S(1)}, f32[8,256]{1,0:T(8,128)S(1)}, u32[]{:S(2)}, u32[]{:S(2)}) collective-permute-start(f32[8,256]{1,0:T(8,128)S(1)} %get-tuple-element.54.refs_4_.refs_14_), channel_id=1, source_target_pairs={{0,3},{1,0},{2,1},{3,2},{4,7},{5,4},{6,5},{7,6},{8,11},{9,8},{10,9... | collective-permute-start | bytes 24584 | tf_op jit(solution)/shard_map/ppermute | solution.py:368
  37.5 4.0 %collective-permute-start.5 = (f32[8,256]{1,0:T(8,128)S(1)}, f32[8,256]{1,0:T(8,128)S(1)}, u32[]{:S(2)}, u32[]{:S(2)}) collective-permute-start(f32[8,256]{1,0:T(8,128)S(1)} %get-tuple-element.54.refs_4_.refs_14_), channel_id=1, source_target_pairs={{0,2},{1,3},{2,0},{3,1},{4,6},{5,7},{6,4},{7,5},{8,10},{9,11},{10,... | collective-permute-start | bytes 24584 | tf_op jit(solution)/shard_map/ppermute | solution.py:368
  37.8 3.7 %collective-permute-start.4 = (f32[8,256]{1,0:T(8,128)S(1)}, f32[8,256]{1,0:T(8,128)S(1)}, u32[]{:S(2)}, u32[]{:S(2)}) collective-permute-start(f32[8,256]{1,0:T(8,128)S(1)} %get-tuple-element.54.refs_4_.refs_14_), channel_id=1, source_target_pairs={{0,1},{1,2},{2,3},{3,0},{4,5},{5,6},{6,7},{7,4},{8,9},{9,10},{10,1... | collective-permute-start | bytes 24584 | tf_op jit(solution)/shard_map/ppermute | solution.py:368
  42.0 3.3 %collective-permute-start.7 = (f32[520,128]{1,0:T(8,128)S(1)}, f32[520,128]{1,0:T(8,128)S(1)}, u32[]{:S(2)}, u32[]{:S(2)}) collective-permute-start(f32[520,128]{1,0:T(8,128)S(1)} %get-tuple-element.56.refs_8_), channel_id=1, source_target_pairs={{0,4},{4,0},{8,12},{12,8},{16,20},{20,16},{24,28},{28,24},{32,36},... | collective-permute-start | bytes 798728 | tf_op jit(solution)/shard_map/ppermute | solution.py:291
  45.4 7.8 %collective-permute-start.8 = (f32[520,128]{1,0:T(8,128)S(1)}, f32[520,128]{1,0:T(8,128)S(1)}, u32[]{:S(2)}, u32[]{:S(2)}) collective-permute-start(f32[520,128]{1,0:T(8,128)S(1)} %pair.3.refs_18_.refs_0_), channel_id=1, source_target_pairs={{0,248},{4,252},{8,0},{12,4},{16,8},{20,12},{24,16},{28,20},{32,24... | collective-permute-start | bytes 798728 | tf_op jit(solution)/shard_map/ppermute | solution.py:294
  53.2 8.5 %collective-permute-start.9 = (f32[520,128]{1,0:T(8,128)S(1)}, f32[520,128]{1,0:T(8,128)S(1)}, u32[]{:S(2)}, u32[]{:S(2)}) collective-permute-start(f32[520,128]{1,0:T(8,128)S(1)} %merge.3), channel_id=1, source_target_pairs={{0,248},{4,252},{8,0},{12,4},{16,8},{20,12},{24,16},{28,20},{32,24... | collective-permute-start | bytes 798728 | tf_op jit(solution)/shard_map/ppermute | solution.py:294
  61.8 3.1 %collective-permute-start.10 = (f32[520,128]{1,0:T(8,128)S(1)}, f32[520,128]{1,0:T(8,128)S(1)}, u32[]{:S(2)}, u32[]{:S(2)}) collective-permute-start(f32[520,128]{1,0:T(8,128)S(1)} %get-tuple-element.66), channel_id=1, source_target_pairs={{0,4},{4,0},{8,12},{12,8},{16,20},{20,16},{24,28},{28,24},{32,36},... | collective-permute-start | bytes 798728 | tf_op jit(solution)/shard_map/ppermute | solution.py:291

commit v6 on v4

--- a/solution.py
+++ b/solution.py
@@ -109,7 +109,8 @@
     add_into(rest[-1], near, far, 0, 0)
 
 
-def split_kernel(backward, part, entering, mine, came, keep, send):
+def split_kernel(backward, part, entering, mine, came, *rest):
+    keep, send = rest[-2:]
     size = entering.shape[0] - TAG
     upstream = core() == int(backward)
 
@@ -150,30 +151,28 @@
         weighted[:, head(h)] = gain[:, head(h)] * grad[:, head(h)].astype(F32)
 
 
-def pieces(refs):
-    for ref in refs:
-        size = ref.shape[0] - TAG
-        for h in range(size // HD):
-            yield ref[head(h), :], ref[size:size + 1, :]
-
-
-def attend_kernel(half, chunks, row, q, part, weighted, *rest):
-    came, rest = rest[:chunks], rest[chunks:]
-    attended, carried, stats = rest[-3:]
-    rows, width = attended.shape
+def attend_kernel(parts, chunks, row, q, part, weighted, *rest):
+    n = len(parts)
+    came, sofar = rest[:n], rest[n:n + 1]
+    outs, stats = rest[-2 * n - 1:-1], rest[-1]
+    rows, width = q.shape
     keep = in_doc(row, 0)
     first = tag(row, 0)
     square = jnp.zeros((rows, HD), F32)
     inner = jnp.zeros((rows, HD), F32)
-    for h, (state, its) in enumerate(pieces(came)):
-        at = head(half * (width // HD) + h)
-        state = jnp.where(its == first, state, 0.0).astype(BF16)
-        carried[head(h), :] = state
-        att = (part[:, at] + keep * dot(q[:, at], state, NN)).astype(BF16)
-        attended[:, head(h)] = att
-        att = att.astype(F32)
-        square = square + att * att
-        inner = inner + weighted[:, at] * att
+    for i, (half, chunk) in enumerate(parts):
+        states, attended, carried = came[i], outs[i], outs[n + i]
+        size = states.shape[0] - TAG
+        same = states[size:size + 1, :] == first
+        for h in range(size // HD):
+            at = head((half * chunks + chunk) * (size // HD) + h)
+            state = jnp.where(same, states[head(h), :], 0.0).astype(BF16)
+            carried[head(h), :] = state
+            att = (part[:, at] + keep * dot(q[:, at], state, NN)).astype(BF16)
+            attended[:, head(h)] = att
+            att = att.astype(F32)
+            square = square + att * att
+            inner = inner + weighted[:, at] * att
     ones = jnp.ones((TAG, HD), F32)
     upper = lax.broadcasted_iota(jnp.int32, (TAG, rows), 0) < TAG // 2
     exact = lax.Precision.HIGHEST
@@ -182,7 +181,7 @@
         for x in (square, inner)
     ]
     sums = jnp.where(upper, sums[0], sums[1])
-    stats[...] = sums + rest[0][...] if len(rest) > 3 else sums
+    stats[...] = sums + sofar[0][...] if len(rest) > 3 * n + 1 else sums
 
 
 def norm_scales(parts):
@@ -195,20 +194,23 @@
     return as_column(inv), as_column(back)
 
 
-def grad_kernel(half, ranks, row, q, weighted, attended, *rest):
+def grad_kernel(half, chunks, ranks, row, q, weighted, *rest):
     g_out, out = rest[-2:]
-    rows, width = attended.shape
+    rows, width = g_out.shape
+    each = width // HD // chunks
     keep = in_doc(row, 0).astype(BF16)
-    inv, back = norm_scales(rest[:ranks])
+    inv, back = norm_scales(rest[chunks:chunks + ranks])
     for h in range(width // HD):
         at = head(half * (width // HD) + h)
-        g = (inv * weighted[:, at] - attended[:, head(h)].astype(F32) * back).astype(BF16)
+        att = rest[h // each][:, head(h % each)].astype(F32)
+        g = (inv * weighted[:, at] - att * back).astype(BF16)
         g_out[:, head(h)] = g
         out[head(h), :] = dot(q[:, at] * keep, g, TN)
     out[width:, :] = jnp.broadcast_to(tag(row, 0), (TAG, HD))
 
 
-def back_kernel(ranks, row, q, scores, gain, k0, k1, v0, v1, g0, g1, a0, a1, c0, c1, *rest):
+def back_kernel(chunks, ranks, row, q, scores, gain, k0, k1, v0, v1, g0, g1, *rest):
+    attended, carried, rest = rest[:2 * chunks], rest[2 * chunks:4 * chunks], rest[4 * chunks:]
     normed_hbm, grad_q_hbm, part_k, part_v, normed, grad_q, sems = rest[-7:]
     rows, width = k0.shape
     inv, _ = norm_scales(rest[:ranks])
@@ -216,14 +218,17 @@
     seen = visible(row)
     n = width // HD
     copies = []
-    for half, (k, v, g, attended, carried) in enumerate(((k0, v0, g0, a0, c0), (k1, v1, g1, a1, c1))):
+    each = n // chunks
+    for half, (k, v, g) in enumerate(((k0, v0, g0), (k1, v1, g1))):
         for h in range(n):
             at = head(half * n + h)
             gh = g[:, head(h)]
-            normed[:, at] = (gain[:, at] * attended[:, head(h)].astype(F32) * inv).astype(BF16)
+            att = attended[half * chunks + h // each][:, head(h % each)].astype(F32)
+            state = carried[half * chunks + h // each][head(h % each), :]
+            normed[:, at] = (gain[:, at] * att * inv).astype(BF16)
             gs = dot(gh, v[:, head(h)], NT)
             gs = jnp.where(seen, gs, 0.0).astype(BF16)
-            whole = dot(gs, k[:, head(h)], NN) + keep * dot(gh, carried[head(h), :], NT)
+            whole = dot(gs, k[:, head(h)], NN) + keep * dot(gh, state, NT)
             grad_q[:, at] = whole.astype(BF16)
             part_k[:, at] = dot(gs, q[:, at], TN)
             part_v[:, at] = dot(scores[half * n + h], gh, TN)
@@ -239,25 +244,36 @@
         copy.wait()
 
 
-def last_kernel(half, chunks, row, k, v, part_k, part_v, *rest):
-    came = rest[:chunks]
+def last_kernel(parts, chunks, row, part_k, part_v, *rest):
+    n = len(parts)
     k_hbm, v_hbm, grad_k, grad_v, sems = rest[-5:]
-    rows, width = k.shape
+    rows, width = part_k.shape
     keep = in_doc(row, rows - 1)
     last = tag(row, rows - 1)
-    at_core = core() if half == 0 else 1 - core()
     copies = []
-    for h, (state, its) in enumerate(pieces(came)):
-        at = head(half * (width // HD) + h)
-        later = jnp.where(its == last, state, 0.0).astype(BF16)
-        grad_k[:, head(h)] = (part_k[:, at] + keep * dot(v[:, head(h)], later, NT)).astype(BF16)
-        grad_v[:, head(h)] = (part_v[:, at] + keep * dot(k[:, head(h)], later, NN)).astype(BF16)
-        span = pl.ds(pl.multiple_of(at_core * width + h * HD, HD), HD)
-        for i, (held, out) in enumerate(((grad_k, k_hbm), (grad_v, v_hbm))):
-            copies.append(
-                pltpu.make_async_copy(held.at[:, head(h)], out.at[:, span], sems.at[2 * h + i])
-            )
-            copies[-1].start()
+    for i, (half, chunk) in enumerate(parts):
+        states, k, v = rest[3 * i:3 * i + 3]
+        size = states.shape[0] - TAG
+        same = states[size:size + 1, :] == last
+        at_core = core() if half == 0 else 1 - core()
+        for h in range(size // HD):
+            own = head(chunk * (size // HD) + h)
+            at = head((half * chunks + chunk) * (size // HD) + h)
+            mine = len(copies) // 2
+            later = jnp.where(same, states[head(h), :], 0.0).astype(BF16)
+            new_k = part_k[:, at] + keep * dot(v[:, own], later, NT)
+            new_v = part_v[:, at] + keep * dot(k[:, own], later, NN)
+            grad_k[:, head(mine)] = new_k.astype(BF16)
+            grad_v[:, head(mine)] = new_v.astype(BF16)
+            start = at_core * (width // 2) + chunk * size + h * HD
+            span = pl.ds(pl.multiple_of(start, HD), HD)
+            for j, (held, out) in enumerate(((grad_k, k_hbm), (grad_v, v_hbm))):
+                copies.append(
+                    pltpu.make_async_copy(
+                        held.at[:, head(mine)], out.at[:, span], sems.at[2 * mine + j]
+                    )
+                )
+                copies[-1].start()
     for copy in copies:
         copy.wait()
 
@@ -279,7 +295,7 @@
     )(*args, *after)
 
 
-def carry(mine, other, chunks, backward, beside):
+def carry(mine, other, chunks, backward, beside, finish):
     blocks = lax.axis_size("ctx")
     step = -2 if backward else 2
 
@@ -287,8 +303,7 @@
         return lax.ppermute(value, "ctx", [(i, i ^ 1) for i in range(blocks)])
 
     def hop(value):
-        pairs = [(i, i + step) for i in range(blocks) if 0 <= i + step < blocks]
-        return lax.ppermute(value, "ctx", pairs)
+        return lax.ppermute(value, "ctx", [(i, (i + step) % blocks) for i in range(blocks)])
 
     sent = other()
     came = swap(sent)
@@ -300,12 +315,13 @@
     work, token = beside(both[-1])
     window = [call(merge_kernel, [], [chunk], [b, o], [token])[0] for b, o in zip(both, once)]
     entering = [hop(w) for w in window]
-    keep, back = [], []
+    ready = []
     for i, e in enumerate(entering):
         kept, send = call(split_kernel, [backward, i], [chunk] * 2, [e, mine, came])
-        keep.append(kept)
-        back.append(swap(send))
-    return keep, back, work
+        ready += [((0, i), kept), ((1, i), swap(send))]
+    finish(*map(list, zip(*ready[:-1])), work)
+    finish(*map(list, zip(*ready[-1:])), work)
+    return work
 
 
 CHUNKS = 2
@@ -350,16 +366,24 @@
         v.extend(held["v", i] for i in range(2))
         return out
 
-    own, other, work = carry(own_state, lambda: make_state(1), CHUNKS, False, local_work)
+    attended, carried, stats = {}, {}, []
+    piece = part_width // CHUNKS
+
+    def attend(parts, states, work):
+        _, part, q, weighted, _ = work
+        n = len(parts)
+        out = call(
+            attend_kernel, [parts, CHUNKS],
+            [((rows, piece), BF16)] * n + [((piece, HD), BF16)] * n + [sums],
+            [held["row"], q, part, weighted, *states, *stats[-1:]],
+        )
+        attended.update(zip(parts, out))
+        carried.update(zip(parts, out[n:]))
+        stats.append(out[-1])
+
+    work = carry(own_state, lambda: make_state(1), CHUNKS, False, local_work, attend)
     scores, part, q, weighted, gain = work
-    attended, carried, stats = [], [], []
-    for which, came in enumerate((own, other)):
-        out = call(
-            attend_kernel, [which, CHUNKS], [half, ((part_width, HD), BF16), sums],
-            [held["row"], q, part, weighted, *came, *stats[-1:]],
-        )
-        for kept, new in zip((attended, carried, stats), out):
-            kept.append(new)
+    order = [(which, i) for which in range(2) for i in range(CHUNKS)]
     stats = stats[-1:]
     stats += [
         lax.ppermute(stats[0], "head", [(i, (i + apart) % ranks) for i in range(ranks)])
@@ -368,34 +392,42 @@
 
     def make_grad(which, after=()):
         held["g", which], out = call(
-            grad_kernel, [which, ranks], [half, state],
-            [held["row"], q, weighted, attended[which], *stats], after=after,
+            grad_kernel, [which, CHUNKS, ranks], [half, state],
+            [held["row"], q, weighted, *(attended[which, i] for i in range(CHUNKS)), *stats],
+            after=after,
         )
         return out
 
     def back_work(token):
         out = call(
-            back_kernel, [ranks], [((rows, width), BF16, HBM)] * 2 + [wide, wide],
-            [held["row"], q, scores, gain, *k, *v, held["g", 0], held["g", 1], *attended, *carried, *stats],
+            back_kernel, [CHUNKS, ranks], [((rows, width), BF16, HBM)] * 2 + [wide, wide],
+            [held["row"], q, scores, gain, *k, *v, held["g", 0], held["g", 1],
+             *(attended[x] for x in order), *(carried[x] for x in order), *stats],
             after=[token],
             scratch=[VMEM((rows, width), BF16), VMEM((rows, width), BF16), DMA((4,))],
         )
         return out, out[2]
 
-    own, other, work = carry(
-        lambda sent: make_grad(0, [sent]), lambda: make_grad(1), CHUNKS, True, back_work
+    done = []
+
+    def last(parts, states, work):
+        args = [held["row"], work[2], work[3]]
+        for (which, _), state in zip(parts, states):
+            args += [state, k[which], v[which]]
+        n = len(args)
+        size = len(parts) * piece
+        out = call(
+            last_kernel, [parts, CHUNKS], [((rows, width), BF16, HBM)] * 2, args,
+            after=done[-1] if done else (),
+            scratch=[VMEM((rows, size), BF16), VMEM((rows, size), BF16), DMA((2 * size // HD,))],
+            aliases={n: 0, n + 1: 1} if done else {},
+        )
+        done.append(out)
+
+    work = carry(
+        lambda sent: make_grad(0, [sent]), lambda: make_grad(1), CHUNKS, True, back_work, last
     )
-    normed, grad_q, part_k, part_v = work
-    done = ()
-    for which, came in enumerate((own, other)):
-        n = 5 + CHUNKS
-        done = call(
-            last_kernel, [which, CHUNKS], [((rows, width), BF16, HBM)] * 2,
-            [held["row"], k[which], v[which], part_k, part_v, *came], after=done,
-            scratch=[VMEM(*half), VMEM(*half), DMA((heads,))],
-            aliases={n: 0, n + 1: 1} if done else {},
-        )
-    return normed, grad_q, *done
+    return work[0], work[1], *done[-1]
 
 
 def solution(mesh):

time: 64.3 us -> 59.4 us (0.924)
  the two profiles are of different devices: /device:TPU:7 before, /device:TPU:1 now
where the time goes in v6:
time: 59.4 us; the launch traced here: 59.3 us
  starting transfers between devices  26.3 us (44%)
  waiting for transfers between devices  18.7 us (31%)
  Pallas kernels  13.3 us (22%)
  between operations  0.97 us (2%)
    ppermute x8, waiting for transfers between devices, hop(): lax.ppermute(value, 'ctx', [(i, (i + step) % blocks) for i in range(block...  16.1 us
    pallas_call x20, Pallas kernels, call(): pl.pallas_call(lambda *refs: kernel(*fixed, *refs), out_shape=[jax.ShapeD...  13.3 us
    ppermute x6, starting transfers between devices, swap(): return lax.ppermute(value, 'ctx', [(i, i ^ 1) for i in range(blocks)])  12.6 us
    ppermute x8, starting transfers between devices, hop(): lax.ppermute(value, 'ctx', [(i, (i + step) % blocks) for i in range(block...  8.71 us
    ppermute x3, starting transfers between devices, local(): lax.ppermute(stats[0], 'head', [(i, (i + apart) % ranks) for i in range(r...  5.01 us
    ppermute x3, waiting for transfers between devices, local(): lax.ppermute(stats[0], 'head', [(i, (i + apart) % ranks) for i in range(r...  1.72 us
  transfers between devices with their start and end apart: 17, of which 10 were waited for; matrix products, arithmetic and copies ran while one was open for 0% of the time, Pallas kernels for 17%

profile of v6, /device:TPU:1, one launch (start us, length us, event | category | flops | bytes accessed | tf_op | source)
XLA Modules:
  0.0 59.3 jit_solution(3795527989286092195)
XLA Ops:
  0.6 1.3 %state.2 = (f32[520,128]{1,0:T(8,128)S(1)}, bf16[256,512]{1,0:T(8,128)(2,1)S(1)}, bf16[256,512]{1,0:T(8,128)(2,1)S(1)}, s32[1,256]{1,0:T(1,128)S(1)}) custom-call(s32[1,256]{1,0:T(1,128)} %bitcast.3, bf16[256,1024]{1,0:T(8,128)(2,1)} %refs_1_.3, bf16[256,1024]{1,0:T(8,128)(2,1)} %refs_2_.3), custom_call_target="tpu_custom_call" | custom-call | tf_op jit(solution)/shard_map/state/pallas_call | solution.py:286
  2.0 3.3 %collective-permute-start = (f32[520,128]{1,0:T(8,128)S(1)}, f32[520,128]{1,0:T(8,128)S(1)}, u32[]{:S(2)}, u32[]{:S(2)}) collective-permute-start(f32[520,128]{1,0:T(8,128)S(1)} %get-tuple-element.51.refs_3_), channel_id=1, source_target_pairs={{0,4},{4,0},{8,12},{12,8},{16,20},{20,16},{24,28},{28,24},{32,36},... | collective-permute-start | bytes 798728 | tf_op jit(solution)/shard_map/ppermute | solution.py:303
  5.3 1.3 %state.3 = (f32[520,128]{1,0:T(8,128)S(1)}, bf16[256,512]{1,0:T(8,128)(2,1)S(1)}, bf16[256,512]{1,0:T(8,128)(2,1)S(1)}) custom-call(s32[1,256]{1,0:T(1,128)S(1)} %get-tuple-element.50.refs_0_, bf16[256,1024]{1,0:T(8,128)(2,1)} %refs_1_.3, bf16[256,1024]{1,0:T(8,128)(2,1)} %refs_2_.3, f32[520,128]{1,0:T(8,128)S(1)} %get-tuple-element.51.refs_3_), custom_call_target="tpu_custom_call" | custom-call | tf_op jit(solution)/shard_map/state/pallas_call | solution.py:286
  6.6 0.0 collective-permute-done.refs_1_.refs_2_
  6.6 0.1 pair.2
  6.7 0.1 collective-permute-start.1
  6.8 1.6 %collective-permute-start.4 = (f32[264,128]{1,0:T(8,128)S(1)}, f32[264,128]{1,0:T(8,128)S(1)}, u32[]{:S(2)}, u32[]{:S(2)}) collective-permute-start(f32[264,128]{1,0:T(8,128)S(1)} %get-tuple-element.57.refs_8_.refs_0_), channel_id=1, source_target_pairs={{0,8},{4,12},{8,16},{12,20},{16,24},{20,28},{24,32},{28,36},{32,40... | collective-permute-start | bytes 405512 | tf_op jit(solution)/shard_map/ppermute | solution.py:306
  8.3 2.2 %local.1 = (bf16[8,256,256]{2,1,0:T(8,128)(2,1)S(1)}, f32[256,1024]{1,0:T(8,128)S(1)}, bf16[256,1024]{1,0:T(8,128)(2,1)S(1)}, f32[256,1024]{1,0:T(8,128)S(1)}, f32[1,1024]{1,0:T(1,128)S(1)}) custom-call(s32[1,256]{1,0:T(1,128)S(1)} %get-tuple-element.50.refs_0_, bf16[256,512]{1,0:T(8,128)(2,1)S(1)} %get-tuple-element.52.refs_1_.refs_4_.refs_10_, ...), custom_call_target="tpu_custom_call" | custom-call | tf_op jit(solution)/shard_map/local/pallas_call | solution.py:286
  10.5 6.1 %collective-permute-done.1.refs_1_ = f32[264,128]{1,0:T(8,128)S(1)} collective-permute-done((f32[264,128]{1,0:T(8,128)S(1)}, f32[264,128]{1,0:T(8,128)S(1)}, u32[]{:S(2)}, u32[]{:S(2)}) %collective-permute-start.1) | collective-permute-done | bytes 135200 | tf_op jit(solution)/shard_map/ppermute | solution.py:306
  16.6 0.1 collective-permute-start.2
  16.7 2.8 %collective-permute-done.4.refs_1_ = f32[264,128]{1,0:T(8,128)S(1)} collective-permute-done((f32[264,128]{1,0:T(8,128)S(1)}, f32[264,128]{1,0:T(8,128)S(1)}, u32[]{:S(2)}, u32[]{:S(2)}) %collective-permute-start.4) | collective-permute-done | bytes 135200 | tf_op jit(solution)/shard_map/ppermute | solution.py:306
  19.5 0.1 collective-permute-start.5
  19.6 4.3 %collective-permute-done.2.refs_0_ = f32[264,128]{1,0:T(8,128)S(1)} collective-permute-done((f32[264,128]{1,0:T(8,128)S(1)}, f32[264,128]{1,0:T(8,128)S(1)}, u32[]{:S(2)}, u32[]{:S(2)}) %collective-permute-start.2) | collective-permute-done | bytes 135200 | tf_op jit(solution)/shard_map/ppermute | solution.py:306
  23.9 2.5 %collective-permute-start.3 = (f32[264,128]{1,0:T(8,128)S(1)}, f32[264,128]{1,0:T(8,128)S(1)}, u32[]{:S(2)}, u32[]{:S(2)}) collective-permute-start(f32[264,128]{1,0:T(8,128)S(1)} %get-tuple-element.65), channel_id=1, source_target_pairs={{0,4},{4,0},{8,12},{12,8},{16,20},{20,16},{24,28},{28,24},{32,36},... | collective-permute-start | bytes 405512 | tf_op jit(solution)/shard_map/ppermute | solution.py:303
  26.4 1.2 %collective-permute-done.5.refs_0_ = f32[264,128]{1,0:T(8,128)S(1)} collective-permute-done((f32[264,128]{1,0:T(8,128)S(1)}, f32[264,128]{1,0:T(8,128)S(1)}, u32[]{:S(2)}, u32[]{:S(2)}) %collective-permute-start.5) | collective-permute-done | bytes 135200 | tf_op jit(solution)/shard_map/ppermute | solution.py:306
  27.6 1.6 %collective-permute-start.6 = (f32[264,128]{1,0:T(8,128)S(1)}, f32[264,128]{1,0:T(8,128)S(1)}, u32[]{:S(2)}, u32[]{:S(2)}) collective-permute-start(f32[264,128]{1,0:T(8,128)S(1)} %get-tuple-element.69), channel_id=1, source_target_pairs={{0,4},{4,0},{8,12},{12,8},{16,20},{20,16},{24,28},{28,24},{32,36},... | collective-permute-start | bytes 405512 | tf_op jit(solution)/shard_map/ppermute | solution.py:303
  29.2 0.0 collective-permute-done.3.refs_5_
  29.2 0.8 %attend.2 = (bf16[256,256]{1,0:T(8,128)(2,1)S(1)}, bf16[256,256]{1,0:T(8,128)(2,1)S(1)}, bf16[256,256]{1,0:T(8,128)(2,1)S(1)}, bf16[256,128]{1,0:T(8,128)(2,1)S(...) custom-call(s32[1,256]{1,0:T(1,128)S(1)} %get-tuple-element.50.refs_0_, ...), custom_call_target="tpu_custom_call" | custom-call | tf_op jit(solution)/shard_map/attend/pallas_call | solution.py:286
  29.9 0.2 collective-permute-done.6.refs_4_
  30.2 0.6 attend.3
  30.7 1.3 %collective-permute-start.7 = (f32[8,256]{1,0:T(8,128)S(1)}, f32[8,256]{1,0:T(8,128)S(1)}, u32[]{:S(2)}, u32[]{:S(2)}) collective-permute-start(f32[8,256]{1,0:T(8,128)S(1)} %get-tuple-element.71.refs_5_.refs_18_), channel_id=1, source_target_pairs={{0,1},{1,2},{2,3},{3,0},{4,5},{5,6},{6,7},{7,4},{8,9},{9,10},{10,1... | collective-permute-start | bytes 24584 | tf_op jit(solution)/shard_map/ppermute | solution.py:389
  32.1 2.6 %collective-permute-start.8 = (f32[8,256]{1,0:T(8,128)S(1)}, f32[8,256]{1,0:T(8,128)S(1)}, u32[]{:S(2)}, u32[]{:S(2)}) collective-permute-start(f32[8,256]{1,0:T(8,128)S(1)} %get-tuple-element.71.refs_5_.refs_18_), channel_id=1, source_target_pairs={{0,2},{1,3},{2,0},{3,1},{4,6},{5,7},{6,4},{7,5},{8,10},{9,11},{10,... | collective-permute-start | bytes 24584 | tf_op jit(solution)/shard_map/ppermute | solution.py:389
  34.7 1.1 %collective-permute-start.9 = (f32[8,256]{1,0:T(8,128)S(1)}, f32[8,256]{1,0:T(8,128)S(1)}, u32[]{:S(2)}, u32[]{:S(2)}) collective-permute-start(f32[8,256]{1,0:T(8,128)S(1)} %get-tuple-element.71.refs_5_.refs_18_), channel_id=1, source_target_pairs={{0,3},{1,0},{2,1},{3,2},{4,7},{5,4},{6,5},{7,6},{8,11},{9,8},{10,9... | collective-permute-start | bytes 24584 | tf_op jit(solution)/shard_map/ppermute | solution.py:389
  35.8 0.0 collective-permute-done.7.refs_6_.refs_19_
  35.8 0.3 collective-permute-done.8.refs_7_.refs_20_
  36.1 1.4 %collective-permute-done.9.refs_8_.refs_21_ = f32[8,256]{1,0:T(8,128)S(1)} collective-permute-done((f32[8,256]{1,0:T(8,128)S(1)}, f32[8,256]{1,0:T(8,128)S(1)}, u32[]{:S(2)}, u32[]{:S(2)}) %collective-permute-start.9) | collective-permute-done | bytes 8224 | tf_op jit(solution)/shard_map/ppermute | solution.py:389
  37.5 0.4 grad.2
  37.9 1.9 %collective-permute-start.10 = (f32[520,128]{1,0:T(8,128)S(1)}, f32[520,128]{1,0:T(8,128)S(1)}, u32[]{:S(2)}, u32[]{:S(2)}) collective-permute-start(f32[520,128]{1,0:T(8,128)S(1)} %get-tuple-element.74.refs_9_), channel_id=1, source_target_pairs={{0,4},{4,0},{8,12},{12,8},{16,20},{20,16},{24,28},{28,24},{32,36},... | collective-permute-start | bytes 798728 | tf_op jit(solution)/shard_map/ppermute | solution.py:303
  39.8 0.4 grad.3
  40.2 0.7 %collective-permute-done.10.refs_1_.refs_2_ = f32[520,128]{1,0:T(8,128)S(1)} collective-permute-done((f32[520,128]{1,0:T(8,128)S(1)}, f32[520,128]{1,0:T(8,128)S(1)}, u32[]{:S(2)}, u32[]{:S(2)}) %collective-permute-start.10) | collective-permute-done | bytes 266272 | tf_op jit(solution)/shard_map/ppermute | solution.py:303
  41.0 0.1 collective-permute-start.14
  41.1 0.3 collective-permute-start.11
  41.4 3.7 %back.1 = (bf16[256,1024]{1,0:T(8,128)(2,1)}, bf16[256,1024]{1,0:T(8,128)(2,1)}, f32[256,1024]{1,0:T(8,128)S(1)}, f32[256,1024]{1,0:T(8,128)S(1)}) custom-call(s32[1,256]{1,0:T(1,128)S(1)} %get-tuple-element.50.refs_0_, bf16[256,1024]{1,0:T(8,128)(2,1)S(1)} %get-tuple-element.58.refs_1_, bf16[8,256,256]{2,1,0:T(8,128)(2,1)S(1)} %get-tuple-element.59.refs_2_, ...), custom_call_target="tpu_custom_call" | custom-call | tf_op jit(solution)/shard_map/back/pallas_call | solution.py:286
  45.1 0.8 %collective-permute-done.14.refs_1_ = f32[264,128]{1,0:T(8,128)S(1)} collective-permute-done((f32[264,128]{1,0:T(8,128)S(1)}, f32[264,128]{1,0:T(8,128)S(1)}, u32[]{:S(2)}, u32[]{:S(2)}) %collective-permute-start.14) | collective-permute-done | bytes 135200 | tf_op jit(solution)/shard_map/ppermute | solution.py:306
  45.9 3.7 %collective-permute-start.15 = (f32[264,128]{1,0:T(8,128)S(1)}, f32[264,128]{1,0:T(8,128)S(1)}, u32[]{:S(2)}, u32[]{:S(2)}) collective-permute-start(f32[264,128]{1,0:T(8,128)S(1)} %merge.7), channel_id=1, source_target_pairs={{0,248},{4,252},{8,0},{12,4},{16,8},{20,12},{24,16},{28,20},{32,24... | collective-permute-start | bytes 405512 | tf_op jit(solution)/shard_map/ppermute | solution.py:306
  49.5 0.0 collective-permute-done.11.refs_1_
  49.6 2.9 %collective-permute-start.12 = (f32[264,128]{1,0:T(8,128)S(1)}, f32[264,128]{1,0:T(8,128)S(1)}, u32[]{:S(2)}, u32[]{:S(2)}) collective-permute-start(f32[264,128]{1,0:T(8,128)S(1)} %merge.6), channel_id=1, source_target_pairs={{0,248},{4,252},{8,0},{12,4},{16,8},{20,12},{24,16},{28,20},{32,24... | collective-permute-start | bytes 405512 | tf_op jit(solution)/shard_map/ppermute | solution.py:306
  52.4 0.0 collective-permute-done.15.refs_0_
  52.5 2.0 %collective-permute-start.16 = (f32[264,128]{1,0:T(8,128)S(1)}, f32[264,128]{1,0:T(8,128)S(1)}, u32[]{:S(2)}, u32[]{:S(2)}) collective-permute-start(f32[264,128]{1,0:T(8,128)S(1)} %get-tuple-element.90), channel_id=1, source_target_pairs={{0,4},{4,0},{8,12},{12,8},{16,20},{20,16},{24,28},{28,24},{32,36},... | collective-permute-start | bytes 405512 | tf_op jit(solution)/shard_map/ppermute | solution.py:303
  54.5 1.0 %collective-permute-done.12.refs_0_ = f32[264,128]{1,0:T(8,128)S(1)} collective-permute-done((f32[264,128]{1,0:T(8,128)S(1)}, f32[264,128]{1,0:T(8,128)S(1)}, u32[]{:S(2)}, u32[]{:S(2)}) %collective-permute-start.12) | collective-permute-done | bytes 135200 | tf_op jit(solution)/shard_map/ppermute | solution.py:306
  55.5 1.4 %collective-permute-start.13 = (f32[264,128]{1,0:T(8,128)S(1)}, f32[264,128]{1,0:T(8,128)S(1)}, u32[]{:S(2)}, u32[]{:S(2)}) collective-permute-start(f32[264,128]{1,0:T(8,128)S(1)} %get-tuple-element.87), channel_id=1, source_target_pairs={{0,4},{4,0},{8,12},{12,8},{16,20},{20,16},{24,28},{28,24},{32,36},... | collective-permute-start | bytes 405512 | tf_op jit(solution)/shard_map/ppermute | solution.py:303
  56.9 0.0 collective-permute-done.16.refs_6_
  56.9 1.2 %last.2 = (bf16[256,1024]{1,0:T(8,128)(2,1)}, bf16[256,1024]{1,0:T(8,128)(2,1)}) custom-call(s32[1,256]{1,0:T(1,128)S(1)} %get-tuple-element.50.refs_0_, f32[256,1024]{1,0:T(8,128)S(1)} %get-tuple-element.85.refs_2_.refs_1_, f32[256,1024]{1,0:T(8,128)S(1)} %get-tuple-element.86.refs_2_, f32[264,128]{1,0:T(8,128)S(1)} %get-tuple-element.89.refs_3_, ...), custom_call_target="tpu_custom_call" | custom-call | tf_op jit(solution)/shard_map/last/pallas_call | solution.py:286
  58.1 0.0 collective-permute-done.13.refs_3_
  58.1 1.0 %last.3 = (bf16[256,1024]{1,0:T(8,128)(2,1)}, bf16[256,1024]{1,0:T(8,128)(2,1)}) custom-call(s32[1,256]{1,0:T(1,128)S(1)} %get-tuple-element.50.refs_0_, f32[256,1024]{1,0:T(8,128)S(1)} %get-tuple-element.85.refs_2_.refs_1_, f32[256,1024]{1,0:T(8,128)S(1)} %get-tuple-element.86.refs_2_, ...), custom_call_target="tpu_custom_call", output_to_operand_aliasing={{0}: (6, {}), {1}: (7, {})} | custom-call | tf_op jit(solution)/shard_map/last/pallas_call | solution.py:286
  (9 shorter events, 0.2 us)
Async XLA Ops:
  2.0 4.6 %collective-permute-start = (f32[520,128]{1,0:T(8,128)S(1)}, f32[520,128]{1,0:T(8,128)S(1)}, u32[]{:S(2)}, u32[]{:S(2)}) collective-permute-start(f32[520,128]{1,0:T(8,128)S(1)} %get-tuple-element.51.refs_3_), channel_id=1, source_target_pairs={{0,4},{4,0},{8,12},{12,8},{16,20},{20,16},{24,28},{28,24},{32,36},... | collective-permute-start | bytes 798728 | tf_op jit(solution)/shard_map/ppermute | solution.py:303
  6.7 9.9 %collective-permute-start.1 = (f32[264,128]{1,0:T(8,128)S(1)}, f32[264,128]{1,0:T(8,128)S(1)}, u32[]{:S(2)}, u32[]{:S(2)}) collective-permute-start(f32[264,128]{1,0:T(8,128)S(1)} %get-tuple-element.63.refs_0_), channel_id=1, source_target_pairs={{0,8},{4,12},{8,16},{12,20},{16,24},{20,28},{24,32},{28,36},{32,40... | collective-permute-start | bytes 405512 | tf_op jit(solution)/shard_map/ppermute | solution.py:306
  6.8 12.7 %collective-permute-start.4 = (f32[264,128]{1,0:T(8,128)S(1)}, f32[264,128]{1,0:T(8,128)S(1)}, u32[]{:S(2)}, u32[]{:S(2)}) collective-permute-start(f32[264,128]{1,0:T(8,128)S(1)} %get-tuple-element.57.refs_8_.refs_0_), channel_id=1, source_target_pairs={{0,8},{4,12},{8,16},{12,20},{16,24},{20,28},{24,32},{28,36},{32,40... | collective-permute-start | bytes 405512 | tf_op jit(solution)/shard_map/ppermute | solution.py:306
  16.6 7.3 %collective-permute-start.2 = (f32[264,128]{1,0:T(8,128)S(1)}, f32[264,128]{1,0:T(8,128)S(1)}, u32[]{:S(2)}, u32[]{:S(2)}) collective-permute-start(f32[264,128]{1,0:T(8,128)S(1)} %merge.4), channel_id=1, source_target_pairs={{0,8},{4,12},{8,16},{12,20},{16,24},{20,28},{24,32},{28,36},{32,40... | collective-permute-start | bytes 405512 | tf_op jit(solution)/shard_map/ppermute | solution.py:306
  19.5 8.0 %collective-permute-start.5 = (f32[264,128]{1,0:T(8,128)S(1)}, f32[264,128]{1,0:T(8,128)S(1)}, u32[]{:S(2)}, u32[]{:S(2)}) collective-permute-start(f32[264,128]{1,0:T(8,128)S(1)} %merge.5), channel_id=1, source_target_pairs={{0,8},{4,12},{8,16},{12,20},{16,24},{20,28},{24,32},{28,36},{32,40... | collective-permute-start | bytes 405512 | tf_op jit(solution)/shard_map/ppermute | solution.py:306
  23.9 5.2 %collective-permute-start.3 = (f32[264,128]{1,0:T(8,128)S(1)}, f32[264,128]{1,0:T(8,128)S(1)}, u32[]{:S(2)}, u32[]{:S(2)}) collective-permute-start(f32[264,128]{1,0:T(8,128)S(1)} %get-tuple-element.65), channel_id=1, source_target_pairs={{0,4},{4,0},{8,12},{12,8},{16,20},{20,16},{24,28},{28,24},{32,36},... | collective-permute-start | bytes 405512 | tf_op jit(solution)/shard_map/ppermute | solution.py:303
  27.6 2.6 %collective-permute-start.6 = (f32[264,128]{1,0:T(8,128)S(1)}, f32[264,128]{1,0:T(8,128)S(1)}, u32[]{:S(2)}, u32[]{:S(2)}) collective-permute-start(f32[264,128]{1,0:T(8,128)S(1)} %get-tuple-element.69), channel_id=1, source_target_pairs={{0,4},{4,0},{8,12},{12,8},{16,20},{20,16},{24,28},{28,24},{32,36},... | collective-permute-start | bytes 405512 | tf_op jit(solution)/shard_map/ppermute | solution.py:303
  30.7 5.0 %collective-permute-start.7 = (f32[8,256]{1,0:T(8,128)S(1)}, f32[8,256]{1,0:T(8,128)S(1)}, u32[]{:S(2)}, u32[]{:S(2)}) collective-permute-start(f32[8,256]{1,0:T(8,128)S(1)} %get-tuple-element.71.refs_5_.refs_18_), channel_id=1, source_target_pairs={{0,1},{1,2},{2,3},{3,0},{4,5},{5,6},{6,7},{7,4},{8,9},{9,10},{10,1... | collective-permute-start | bytes 24584 | tf_op jit(solution)/shard_map/ppermute | solution.py:389
  32.1 4.0 %collective-permute-start.8 = (f32[8,256]{1,0:T(8,128)S(1)}, f32[8,256]{1,0:T(8,128)S(1)}, u32[]{:S(2)}, u32[]{:S(2)}) collective-permute-start(f32[8,256]{1,0:T(8,128)S(1)} %get-tuple-element.71.refs_5_.refs_18_), channel_id=1, source_target_pairs={{0,2},{1,3},{2,0},{3,1},{4,6},{5,7},{6,4},{7,5},{8,10},{9,11},{10,... | collective-permute-start | bytes 24584 | tf_op jit(solution)/shard_map/ppermute | solution.py:389
  34.7 2.8 %collective-permute-start.9 = (f32[8,256]{1,0:T(8,128)S(1)}, f32[8,256]{1,0:T(8,128)S(1)}, u32[]{:S(2)}, u32[]{:S(2)}) collective-permute-start(f32[8,256]{1,0:T(8,128)S(1)} %get-tuple-element.71.refs_5_.refs_18_), channel_id=1, source_target_pairs={{0,3},{1,0},{2,1},{3,2},{4,7},{5,4},{6,5},{7,6},{8,11},{9,8},{10,9... | collective-permute-start | bytes 24584 | tf_op jit(solution)/shard_map/ppermute | solution.py:389
  37.9 3.0 %collective-permute-start.10 = (f32[520,128]{1,0:T(8,128)S(1)}, f32[520,128]{1,0:T(8,128)S(1)}, u32[]{:S(2)}, u32[]{:S(2)}) collective-permute-start(f32[520,128]{1,0:T(8,128)S(1)} %get-tuple-element.74.refs_9_), channel_id=1, source_target_pairs={{0,4},{4,0},{8,12},{12,8},{16,20},{20,16},{24,28},{28,24},{32,36},... | collective-permute-start | bytes 798728 | tf_op jit(solution)/shard_map/ppermute | solution.py:303
  41.0 4.8 %collective-permute-start.14 = (f32[264,128]{1,0:T(8,128)S(1)}, f32[264,128]{1,0:T(8,128)S(1)}, u32[]{:S(2)}, u32[]{:S(2)}) collective-permute-start(f32[264,128]{1,0:T(8,128)S(1)} %get-tuple-element.88.refs_0_), channel_id=1, source_target_pairs={{0,248},{4,252},{8,0},{12,4},{16,8},{20,12},{24,16},{28,20},{32,24... | collective-permute-start | bytes 405512 | tf_op jit(solution)/shard_map/ppermute | solution.py:306
  41.1 8.5 %collective-permute-start.11 = (f32[264,128]{1,0:T(8,128)S(1)}, f32[264,128]{1,0:T(8,128)S(1)}, u32[]{:S(2)}, u32[]{:S(2)}) collective-permute-start(f32[264,128]{1,0:T(8,128)S(1)} %get-tuple-element.82.refs_22_.refs_0_), channel_id=1, source_target_pairs={{0,248},{4,252},{8,0},{12,4},{16,8},{20,12},{24,16},{28,20},{32,24... | collective-permute-start | bytes 405512 | tf_op jit(solution)/shard_map/ppermute | solution.py:306
  45.9 6.6 %collective-permute-start.15 = (f32[264,128]{1,0:T(8,128)S(1)}, f32[264,128]{1,0:T(8,128)S(1)}, u32[]{:S(2)}, u32[]{:S(2)}) collective-permute-start(f32[264,128]{1,0:T(8,128)S(1)} %merge.7), channel_id=1, source_target_pairs={{0,248},{4,252},{8,0},{12,4},{16,8},{20,12},{24,16},{28,20},{32,24... | collective-permute-start | bytes 405512 | tf_op jit(solution)/shard_map/ppermute | solution.py:306
  49.6 5.9 %collective-permute-start.12 = (f32[264,128]{1,0:T(8,128)S(1)}, f32[264,128]{1,0:T(8,128)S(1)}, u32[]{:S(2)}, u32[]{:S(2)}) collective-permute-start(f32[264,128]{1,0:T(8,128)S(1)} %merge.6), channel_id=1, source_target_pairs={{0,248},{4,252},{8,0},{12,4},{16,8},{20,12},{24,16},{28,20},{32,24... | collective-permute-start | bytes 405512 | tf_op jit(solution)/shard_map/ppermute | solution.py:306
  52.5 4.4 %collective-permute-start.16 = (f32[264,128]{1,0:T(8,128)S(1)}, f32[264,128]{1,0:T(8,128)S(1)}, u32[]{:S(2)}, u32[]{:S(2)}) collective-permute-start(f32[264,128]{1,0:T(8,128)S(1)} %get-tuple-element.90), channel_id=1, source_target_pairs={{0,4},{4,0},{8,12},{12,8},{16,20},{20,16},{24,28},{28,24},{32,36},... | collective-permute-start | bytes 405512 | tf_op jit(solution)/shard_map/ppermute | solution.py:303
  55.5 2.6 %collective-permute-start.13 = (f32[264,128]{1,0:T(8,128)S(1)}, f32[264,128]{1,0:T(8,128)S(1)}, u32[]{:S(2)}, u32[]{:S(2)}) collective-permute-start(f32[264,128]{1,0:T(8,128)S(1)} %get-tuple-element.87), channel_id=1, source_target_pairs={{0,4},{4,0},{8,12},{12,8},{16,20},{20,16},{24,28},{28,24},{32,36},... | collective-permute-start | bytes 405512 | tf_op jit(solution)/shard_map/ppermute | solution.py:303

commit v7 on v6

--- a/solution.py
+++ b/solution.py
@@ -324,7 +324,7 @@
     return work
 
 
-CHUNKS = 2
+CHUNKS = 4
 
 
 def local(queries, key_rows, value_rows, grad_out, doc_ids, out_gain):

time: 59.4 us -> 60 us (1.010)
  starting transfers between devices: 26.3 us -> 37 us
  waiting for transfers between devices: 18.7 us -> 8.49 us
    ppermute x8 -> x16, waiting for transfers between devices: 16.1 us -> 5.88 us  [hop(): lax.ppermute(value, 'ctx', [(i, (i + step) % blocks) for i in range(block...]
    ppermute x8 -> x16, starting transfers between devices: 8.71 us -> 14.8 us  [hop(): lax.ppermute(value, 'ctx', [(i, (i + step) % blocks) for i in range(block...]
    ppermute x6 -> x10, starting transfers between devices: 12.6 us -> 17 us  [swap(): return lax.ppermute(value, 'ctx', [(i, i ^ 1) for i in range(blocks)])]
    pallas_call x20 -> x28, Pallas kernels: 13.3 us -> 13.4 us  [call(): pl.pallas_call(lambda *refs: kernel(*fixed, *refs), out_shape=[jax.ShapeD...]
  transfers between devices with their start and end apart: 17 -> 29, of which waited for: 10 -> 9; matrix products, arithmetic and copies ran while one was open for 0% -> 0% of each run, Pallas kernels for 17% -> 17%
where the time goes in v7:
time: 60 us; the launch traced here: 59.8 us
  starting transfers between devices  37 us (62%)
  Pallas kernels  13.4 us (22%)
  waiting for transfers between devices  8.49 us (14%)
  between operations  1.01 us (2%)
    ppermute x10, starting transfers between devices, swap(): return lax.ppermute(value, 'ctx', [(i, i ^ 1) for i in range(blocks)])  17 us
    ppermute x16, starting transfers between devices, hop(): lax.ppermute(value, 'ctx', [(i, (i + step) % blocks) for i in range(block...  14.8 us
    pallas_call x28, Pallas kernels, call(): pl.pallas_call(lambda *refs: kernel(*fixed, *refs), out_shape=[jax.ShapeD...  13.4 us
    ppermute x16, waiting for transfers between devices, hop(): lax.ppermute(value, 'ctx', [(i, (i + step) % blocks) for i in range(block...  5.88 us
    ppermute x3, starting transfers between devices, local(): lax.ppermute(stats[0], 'head', [(i, (i + apart) % ranks) for i in range(r...  5.15 us
    ppermute x3, waiting for transfers between devices, local(): lax.ppermute(stats[0], 'head', [(i, (i + apart) % ranks) for i in range(r...  1.7 us
  transfers between devices with their start and end apart: 29, of which 9 were waited for; matrix products, arithmetic and copies ran while one was open for 0% of the time, Pallas kernels for 17%

profile of v7, /device:TPU:1, one launch (start us, length us, event | category | flops | bytes accessed | tf_op | source)
XLA Modules:
  0.0 59.8 jit_solution(11274477353500344101)
XLA Ops:
  0.6 1.3 %state.2 = (f32[520,128]{1,0:T(8,128)S(1)}, bf16[256,512]{1,0:T(8,128)(2,1)S(1)}, bf16[256,512]{1,0:T(8,128)(2,1)S(1)}, s32[1,256]{1,0:T(1,128)S(1)}) custom-call(s32[1,256]{1,0:T(1,128)} %bitcast.3, bf16[256,1024]{1,0:T(8,128)(2,1)} %refs_1_.3, bf16[256,1024]{1,0:T(8,128)(2,1)} %refs_2_.3), custom_call_target="tpu_custom_call" | custom-call | tf_op jit(solution)/shard_map/state/pallas_call | solution.py:286
  2.0 3.3 %collective-permute-start = (f32[520,128]{1,0:T(8,128)S(1)}, f32[520,128]{1,0:T(8,128)S(1)}, u32[]{:S(2)}, u32[]{:S(2)}) collective-permute-start(f32[520,128]{1,0:T(8,128)S(1)} %get-tuple-element.71.refs_3_), channel_id=1, source_target_pairs={{0,4},{4,0},{8,12},{12,8},{16,20},{20,16},{24,28},{28,24},{32,36},... | collective-permute-start | bytes 798728 | tf_op jit(solution)/shard_map/ppermute | solution.py:303
  5.3 1.3 %state.3 = (f32[520,128]{1,0:T(8,128)S(1)}, bf16[256,512]{1,0:T(8,128)(2,1)S(1)}, bf16[256,512]{1,0:T(8,128)(2,1)S(1)}) custom-call(s32[1,256]{1,0:T(1,128)S(1)} %get-tuple-element.70.refs_0_, bf16[256,1024]{1,0:T(8,128)(2,1)} %refs_1_.3, bf16[256,1024]{1,0:T(8,128)(2,1)} %refs_2_.3, f32[520,128]{1,0:T(8,128)S(1)} %get-tuple-element.71.refs_3_), custom_call_target="tpu_custom_call" | custom-call | tf_op jit(solution)/shard_map/state/pallas_call | solution.py:286
  6.6 0.0 collective-permute-done.refs_1_.refs_2_
  6.6 0.1 pair.2
  6.7 0.1 collective-permute-start.7
  6.8 1.6 %collective-permute-start.4 = (f32[136,128]{1,0:T(8,128)S(1)}, f32[136,128]{1,0:T(8,128)S(1)}, u32[]{:S(2)}, u32[]{:S(2)}) collective-permute-start(f32[136,128]{1,0:T(8,128)S(1)} %get-tuple-element.86.refs_0_), channel_id=1, source_target_pairs={{0,8},{4,12},{8,16},{12,20},{16,24},{20,28},{24,32},{28,36},{32,40... | collective-permute-start | bytes 208904 | tf_op jit(solution)/shard_map/ppermute | solution.py:306
  8.3 1.6 %collective-permute-start.1 = (f32[136,128]{1,0:T(8,128)S(1)}, f32[136,128]{1,0:T(8,128)S(1)}, u32[]{:S(2)}, u32[]{:S(2)}) collective-permute-start(f32[136,128]{1,0:T(8,128)S(1)} %get-tuple-element.83.refs_0_), channel_id=1, source_target_pairs={{0,8},{4,12},{8,16},{12,20},{16,24},{20,28},{24,32},{28,36},{32,40... | collective-permute-start | bytes 208904 | tf_op jit(solution)/shard_map/ppermute | solution.py:306
  10.0 2.9 %collective-permute-start.10 = (f32[136,128]{1,0:T(8,128)S(1)}, f32[136,128]{1,0:T(8,128)S(1)}, u32[]{:S(2)}, u32[]{:S(2)}) collective-permute-start(f32[136,128]{1,0:T(8,128)S(1)} %get-tuple-element.77.refs_8_.refs_0_), channel_id=1, source_target_pairs={{0,8},{4,12},{8,16},{12,20},{16,24},{20,28},{24,32},{28,36},{32,40... | collective-permute-start | bytes 208904 | tf_op jit(solution)/shard_map/ppermute | solution.py:306
  12.8 2.2 %local.1 = (bf16[8,256,256]{2,1,0:T(8,128)(2,1)S(1)}, f32[256,1024]{1,0:T(8,128)S(1)}, bf16[256,1024]{1,0:T(8,128)(2,1)S(1)}, f32[256,1024]{1,0:T(8,128)S(1)}, f32[1,1024]{1,0:T(1,128)S(1)}) custom-call(s32[1,256]{1,0:T(1,128)S(1)} %get-tuple-element.70.refs_0_, bf16[256,512]{1,0:T(8,128)(2,1)S(1)} %get-tuple-element.72.refs_1_.refs_4_.refs_10_.refs_16_.refs_22_, ...), custom_call_target="tpu_custom_call" | custom-call | tf_op jit(solution)/shard_map/local/pallas_call | solution.py:286
  15.0 0.2 collective-permute-done.7.refs_1_
  15.3 0.6 %collective-permute-start.8 = (f32[136,128]{1,0:T(8,128)S(1)}, f32[136,128]{1,0:T(8,128)S(1)}, u32[]{:S(2)}, u32[]{:S(2)}) collective-permute-start(f32[136,128]{1,0:T(8,128)S(1)} %merge.10), channel_id=1, source_target_pairs={{0,8},{4,12},{8,16},{12,20},{16,24},{20,28},{24,32},{28,36},{32,40... | collective-permute-start | bytes 208904 | tf_op jit(solution)/shard_map/ppermute | solution.py:306
  15.9 0.9 %collective-permute-done.4.refs_1_ = f32[136,128]{1,0:T(8,128)S(1)} collective-permute-done((f32[136,128]{1,0:T(8,128)S(1)}, f32[136,128]{1,0:T(8,128)S(1)}, u32[]{:S(2)}, u32[]{:S(2)}) %collective-permute-start.4) | collective-permute-done | bytes 69664 | tf_op jit(solution)/shard_map/ppermute | solution.py:306
  16.7 0.1 collective-permute-start.5
  16.8 1.4 %collective-permute-done.1.refs_1_ = f32[136,128]{1,0:T(8,128)S(1)} collective-permute-done((f32[136,128]{1,0:T(8,128)S(1)}, f32[136,128]{1,0:T(8,128)S(1)}, u32[]{:S(2)}, u32[]{:S(2)}) %collective-permute-start.1) | collective-permute-done | bytes 69664 | tf_op jit(solution)/shard_map/ppermute | solution.py:306
  18.2 0.1 collective-permute-start.2
  18.3 1.4 %collective-permute-done.10.refs_1_ = f32[136,128]{1,0:T(8,128)S(1)} collective-permute-done((f32[136,128]{1,0:T(8,128)S(1)}, f32[136,128]{1,0:T(8,128)S(1)}, u32[]{:S(2)}, u32[]{:S(2)}) %collective-permute-start.10) | collective-permute-done | bytes 69664 | tf_op jit(solution)/shard_map/ppermute | solution.py:306
  19.7 0.1 collective-permute-start.11
  19.8 2.0 %collective-permute-done.8.refs_0_ = f32[136,128]{1,0:T(8,128)S(1)} collective-permute-done((f32[136,128]{1,0:T(8,128)S(1)}, f32[136,128]{1,0:T(8,128)S(1)}, u32[]{:S(2)}, u32[]{:S(2)}) %collective-permute-start.8) | collective-permute-done | bytes 69664 | tf_op jit(solution)/shard_map/ppermute | solution.py:306
  21.8 3.0 %collective-permute-start.9 = (f32[136,128]{1,0:T(8,128)S(1)}, f32[136,128]{1,0:T(8,128)S(1)}, u32[]{:S(2)}, u32[]{:S(2)}) collective-permute-start(f32[136,128]{1,0:T(8,128)S(1)} %get-tuple-element.91), channel_id=1, source_target_pairs={{0,4},{4,0},{8,12},{12,8},{16,20},{20,16},{24,28},{28,24},{32,36},... | collective-permute-start | bytes 208904 | tf_op jit(solution)/shard_map/ppermute | solution.py:303
  24.9 0.0 collective-permute-done.5.refs_0_
  24.9 1.5 %collective-permute-start.6 = (f32[136,128]{1,0:T(8,128)S(1)}, f32[136,128]{1,0:T(8,128)S(1)}, u32[]{:S(2)}, u32[]{:S(2)}) collective-permute-start(f32[136,128]{1,0:T(8,128)S(1)} %get-tuple-element.88), channel_id=1, source_target_pairs={{0,4},{4,0},{8,12},{12,8},{16,20},{20,16},{24,28},{28,24},{32,36},... | collective-permute-start | bytes 208904 | tf_op jit(solution)/shard_map/ppermute | solution.py:303
  26.3 0.0 collective-permute-done.2.refs_0_
  26.4 1.5 %collective-permute-start.3 = (f32[136,128]{1,0:T(8,128)S(1)}, f32[136,128]{1,0:T(8,128)S(1)}, u32[]{:S(2)}, u32[]{:S(2)}) collective-permute-start(f32[136,128]{1,0:T(8,128)S(1)} %get-tuple-element.85), channel_id=1, source_target_pairs={{0,4},{4,0},{8,12},{12,8},{16,20},{20,16},{24,28},{28,24},{32,36},... | collective-permute-start | bytes 208904 | tf_op jit(solution)/shard_map/ppermute | solution.py:303
  27.8 0.0 collective-permute-done.11.refs_0_
  27.9 0.7 %collective-permute-start.12 = (f32[136,128]{1,0:T(8,128)S(1)}, f32[136,128]{1,0:T(8,128)S(1)}, u32[]{:S(2)}, u32[]{:S(2)}) collective-permute-start(f32[136,128]{1,0:T(8,128)S(1)} %get-tuple-element.97), channel_id=1, source_target_pairs={{0,4},{4,0},{8,12},{12,8},{16,20},{20,16},{24,28},{28,24},{32,36},... | collective-permute-start | bytes 208904 | tf_op jit(solution)/shard_map/ppermute | solution.py:303
  28.6 0.0 collective-permute-done.9.refs_9_
  28.6 0.0 collective-permute-done.6.refs_7_
  28.6 0.2 collective-permute-done.3.refs_5_
  28.7 0.8 %attend.2 = (bf16[256,128]{1,0:T(8,128)(2,1)S(1)}, bf16[256,128]{1,0:T(8,128)(2,1)S(1)}, bf16[256,128]{1,0:T(8,128)(2,1)S(1)}, bf16[256,128]{1,0:T(8,128)(2,1)S(...) custom-call(s32[1,256]{1,0:T(1,128)S(1)} %get-tuple-element.70.refs_, ...), custom_call_target="tpu_custom_call" | custom-call | tf_op jit(solution)/shard_map/attend/pallas_call | solution.py:286
  29.5 0.0 collective-permute-done.12.refs_4_
  29.5 0.6 attend.3
  30.1 1.5 %collective-permute-start.13 = (f32[8,256]{1,0:T(8,128)S(1)}, f32[8,256]{1,0:T(8,128)S(1)}, u32[]{:S(2)}, u32[]{:S(2)}) collective-permute-start(f32[8,256]{1,0:T(8,128)S(1)} %get-tuple-element.99.refs_7_.refs_26_), channel_id=1, source_target_pairs={{0,1},{1,2},{2,3},{3,0},{4,5},{5,6},{6,7},{7,4},{8,9},{9,10},{10,1... | collective-permute-start | bytes 24584 | tf_op jit(solution)/shard_map/ppermute | solution.py:389
  31.6 2.6 %collective-permute-start.14 = (f32[8,256]{1,0:T(8,128)S(1)}, f32[8,256]{1,0:T(8,128)S(1)}, u32[]{:S(2)}, u32[]{:S(2)}) collective-permute-start(f32[8,256]{1,0:T(8,128)S(1)} %get-tuple-element.99.refs_7_.refs_26_), channel_id=1, source_target_pairs={{0,2},{1,3},{2,0},{3,1},{4,6},{5,7},{6,4},{7,5},{8,10},{9,11},{10,... | collective-permute-start | bytes 24584 | tf_op jit(solution)/shard_map/ppermute | solution.py:389
  34.2 1.1 %collective-permute-start.15 = (f32[8,256]{1,0:T(8,128)S(1)}, f32[8,256]{1,0:T(8,128)S(1)}, u32[]{:S(2)}, u32[]{:S(2)}) collective-permute-start(f32[8,256]{1,0:T(8,128)S(1)} %get-tuple-element.99.refs_7_.refs_26_), channel_id=1, source_target_pairs={{0,3},{1,0},{2,1},{3,2},{4,7},{5,4},{6,5},{7,6},{8,11},{9,8},{10,9... | collective-permute-start | bytes 24584 | tf_op jit(solution)/shard_map/ppermute | solution.py:389
  35.3 0.3 collective-permute-done.14.refs_9_.refs_28_
  35.6 1.4 %collective-permute-done.15.refs_10_.refs_29_ = f32[8,256]{1,0:T(8,128)S(1)} collective-permute-done((f32[8,256]{1,0:T(8,128)S(1)}, f32[8,256]{1,0:T(8,128)S(1)}, u32[]{:S(2)}, u32[]{:S(2)}) %collective-permute-start.15) | collective-permute-done | bytes 8224 | tf_op jit(solution)/shard_map/ppermute | solution.py:389
  37.0 0.4 grad.2
  37.4 1.9 %collective-permute-start.16 = (f32[520,128]{1,0:T(8,128)S(1)}, f32[520,128]{1,0:T(8,128)S(1)}, u32[]{:S(2)}, u32[]{:S(2)}) collective-permute-start(f32[520,128]{1,0:T(8,128)S(1)} %get-tuple-element.104.refs_11_), channel_id=1, source_target_pairs={{0,4},{4,0},{8,12},{12,8},{16,20},{20,16},{24,28},{28,24},{32,36},... | collective-permute-start | bytes 798728 | tf_op jit(solution)/shard_map/ppermute | solution.py:303
  39.3 0.4 grad.3
  39.7 0.7 %collective-permute-done.16.refs_1_.refs_2_ = f32[520,128]{1,0:T(8,128)S(1)} collective-permute-done((f32[520,128]{1,0:T(8,128)S(1)}, f32[520,128]{1,0:T(8,128)S(1)}, u32[]{:S(2)}, u32[]{:S(2)}) %collective-permute-start.16) | collective-permute-done | bytes 266272 | tf_op jit(solution)/shard_map/ppermute | solution.py:303
  40.5 0.4 collective-permute-start.26
  40.9 0.4 collective-permute-start.23
  41.2 0.3 collective-permute-start.20
  41.6 2.0 %collective-permute-start.17 = (f32[136,128]{1,0:T(8,128)S(1)}, f32[136,128]{1,0:T(8,128)S(1)}, u32[]{:S(2)}, u32[]{:S(2)}) collective-permute-start(f32[136,128]{1,0:T(8,128)S(1)} %get-tuple-element.116.refs_30_.refs_0_), channel_id=1, source_target_pairs={{0,248},{4,252},{8,0},{12,4},{16,8},{20,12},{24,16},{28,20},{32,24... | collective-permute-start | bytes 208904 | tf_op jit(solution)/shard_map/ppermute | solution.py:306
  43.6 3.7 %back.1 = (bf16[256,1024]{1,0:T(8,128)(2,1)}, bf16[256,1024]{1,0:T(8,128)(2,1)}, f32[256,1024]{1,0:T(8,128)S(1)}, f32[256,1024]{1,0:T(8,128)S(1)}) custom-call(s32[1,256]{1,0:T(1,128)S(1)} %get-tuple-element.70.refs_0_, bf16[256,1024]{1,0:T(8,128)(2,1)S(1)} %get-tuple-element.78.refs_1_, bf16[8,256,256]{2,1,0:T(8,128)(2,1)S(1)} %get-tuple-element.79.refs_2_, ...), custom_call_target="tpu_custom_call" | custom-call | tf_op jit(solution)/shard_map/back/pallas_call | solution.py:286
  47.3 0.4 collective-permute-start.27
  47.7 0.0 collective-permute-done.23.refs_1_
  47.7 1.4 %collective-permute-start.24 = (f32[136,128]{1,0:T(8,128)S(1)}, f32[136,128]{1,0:T(8,128)S(1)}, u32[]{:S(2)}, u32[]{:S(2)}) collective-permute-start(f32[136,128]{1,0:T(8,128)S(1)} %merge.14), channel_id=1, source_target_pairs={{0,248},{4,252},{8,0},{12,4},{16,8},{20,12},{24,16},{28,20},{32,24... | collective-permute-start | bytes 208904 | tf_op jit(solution)/shard_map/ppermute | solution.py:306
  49.2 1.5 %collective-permute-start.21 = (f32[136,128]{1,0:T(8,128)S(1)}, f32[136,128]{1,0:T(8,128)S(1)}, u32[]{:S(2)}, u32[]{:S(2)}) collective-permute-start(f32[136,128]{1,0:T(8,128)S(1)} %merge.13), channel_id=1, source_target_pairs={{0,248},{4,252},{8,0},{12,4},{16,8},{20,12},{24,16},{28,20},{32,24... | collective-permute-start | bytes 208904 | tf_op jit(solution)/shard_map/ppermute | solution.py:306
  50.6 0.0 collective-permute-done.17.refs_1_
  50.6 1.5 %collective-permute-start.18 = (f32[136,128]{1,0:T(8,128)S(1)}, f32[136,128]{1,0:T(8,128)S(1)}, u32[]{:S(2)}, u32[]{:S(2)}) collective-permute-start(f32[136,128]{1,0:T(8,128)S(1)} %merge.12), channel_id=1, source_target_pairs={{0,248},{4,252},{8,0},{12,4},{16,8},{20,12},{24,16},{28,20},{32,24... | collective-permute-start | bytes 208904 | tf_op jit(solution)/shard_map/ppermute | solution.py:306
  52.1 0.0 collective-permute-done.27.refs_0_
  52.1 2.5 %collective-permute-start.28 = (f32[136,128]{1,0:T(8,128)S(1)}, f32[136,128]{1,0:T(8,128)S(1)}, u32[]{:S(2)}, u32[]{:S(2)}) collective-permute-start(f32[136,128]{1,0:T(8,128)S(1)} %get-tuple-element.130), channel_id=1, source_target_pairs={{0,4},{4,0},{8,12},{12,8},{16,20},{20,16},{24,28},{28,24},{32,36},... | collective-permute-start | bytes 208904 | tf_op jit(solution)/shard_map/ppermute | solution.py:303
  54.7 0.7 %collective-permute-start.25 = (f32[136,128]{1,0:T(8,128)S(1)}, f32[136,128]{1,0:T(8,128)S(1)}, u32[]{:S(2)}, u32[]{:S(2)}) collective-permute-start(f32[136,128]{1,0:T(8,128)S(1)} %get-tuple-element.127), channel_id=1, source_target_pairs={{0,4},{4,0},{8,12},{12,8},{16,20},{20,16},{24,28},{28,24},{32,36},... | collective-permute-start | bytes 208904 | tf_op jit(solution)/shard_map/ppermute | solution.py:303
  55.5 0.7 %collective-permute-start.22 = (f32[136,128]{1,0:T(8,128)S(1)}, f32[136,128]{1,0:T(8,128)S(1)}, u32[]{:S(2)}, u32[]{:S(2)}) collective-permute-start(f32[136,128]{1,0:T(8,128)S(1)} %get-tuple-element.124), channel_id=1, source_target_pairs={{0,4},{4,0},{8,12},{12,8},{16,20},{20,16},{24,28},{28,24},{32,36},... | collective-permute-start | bytes 208904 | tf_op jit(solution)/shard_map/ppermute | solution.py:303
  56.2 0.0 collective-permute-done.18.refs_0_
  56.2 1.2 %collective-permute-start.19 = (f32[136,128]{1,0:T(8,128)S(1)}, f32[136,128]{1,0:T(8,128)S(1)}, u32[]{:S(2)}, u32[]{:S(2)}) collective-permute-start(f32[136,128]{1,0:T(8,128)S(1)} %get-tuple-element.121), channel_id=1, source_target_pairs={{0,4},{4,0},{8,12},{12,8},{16,20},{20,16},{24,28},{28,24},{32,36},... | collective-permute-start | bytes 208904 | tf_op jit(solution)/shard_map/ppermute | solution.py:303
  57.4 0.0 collective-permute-done.28.refs_18_
  57.4 0.0 collective-permute-done.25.refs_12_
  57.4 0.0 collective-permute-done.22.refs_6_
  57.4 1.3 %last.2 = (bf16[256,1024]{1,0:T(8,128)(2,1)}, bf16[256,1024]{1,0:T(8,128)(2,1)}) custom-call(s32[1,256]{1,0:T(1,128)S(1)} %get-tuple-element.70.refs_0_, f32[256,1024]{1,0:T(8,128)S(1)} %get-tuple-element.119.refs_2_.refs_1_, f32[256,1024]{1,0:T(8,128)S(1)} %get-tuple-element.120.refs_2_, f32[136,128]{1,0:T(8,128)S(1)} %get-tuple-element.123.refs_3_, ...), custom_call_target="tpu_custom_call" | custom-call | tf_op jit(solution)/shard_map/last/pallas_call | solution.py:286
  58.7 0.0 collective-permute-done.19.refs_3_
  58.7 0.9 %last.3 = (bf16[256,1024]{1,0:T(8,128)(2,1)}, bf16[256,1024]{1,0:T(8,128)(2,1)}) custom-call(s32[1,256]{1,0:T(1,128)S(1)} %get-tuple-element.70.refs_0_, f32[256,1024]{1,0:T(8,128)S(1)} %get-tuple-element.119.refs_2_.refs_1_, f32[256,1024]{1,0:T(8,128)S(1)} %get-tuple-element.120.refs_2_, ...), custom_call_target="tpu_custom_call", output_to_operand_aliasing={{0}: (6, {}), {1}: (7, {})} | custom-call | tf_op jit(solution)/shard_map/last/pallas_call | solution.py:286
  (22 shorter events, 0.3 us)
Async XLA Ops:
  2.0 4.6 %collective-permute-start = (f32[520,128]{1,0:T(8,128)S(1)}, f32[520,128]{1,0:T(8,128)S(1)}, u32[]{:S(2)}, u32[]{:S(2)}) collective-permute-start(f32[520,128]{1,0:T(8,128)S(1)} %get-tuple-element.71.refs_3_), channel_id=1, source_target_pairs={{0,4},{4,0},{8,12},{12,8},{16,20},{20,16},{24,28},{28,24},{32,36},... | collective-permute-start | bytes 798728 | tf_op jit(solution)/shard_map/ppermute | solution.py:303
  6.7 8.5 %collective-permute-start.7 = (f32[136,128]{1,0:T(8,128)S(1)}, f32[136,128]{1,0:T(8,128)S(1)}, u32[]{:S(2)}, u32[]{:S(2)}) collective-permute-start(f32[136,128]{1,0:T(8,128)S(1)} %get-tuple-element.89.refs_0_), channel_id=1, source_target_pairs={{0,8},{4,12},{8,16},{12,20},{16,24},{20,28},{24,32},{28,36},{32,40... | collective-permute-start | bytes 208904 | tf_op jit(solution)/shard_map/ppermute | solution.py:306
  6.8 9.9 %collective-permute-start.4 = (f32[136,128]{1,0:T(8,128)S(1)}, f32[136,128]{1,0:T(8,128)S(1)}, u32[]{:S(2)}, u32[]{:S(2)}) collective-permute-start(f32[136,128]{1,0:T(8,128)S(1)} %get-tuple-element.86.refs_0_), channel_id=1, source_target_pairs={{0,8},{4,12},{8,16},{12,20},{16,24},{20,28},{24,32},{28,36},{32,40... | collective-permute-start | bytes 208904 | tf_op jit(solution)/shard_map/ppermute | solution.py:306
  8.3 9.9 %collective-permute-start.1 = (f32[136,128]{1,0:T(8,128)S(1)}, f32[136,128]{1,0:T(8,128)S(1)}, u32[]{:S(2)}, u32[]{:S(2)}) collective-permute-start(f32[136,128]{1,0:T(8,128)S(1)} %get-tuple-element.83.refs_0_), channel_id=1, source_target_pairs={{0,8},{4,12},{8,16},{12,20},{16,24},{20,28},{24,32},{28,36},{32,40... | collective-permute-start | bytes 208904 | tf_op jit(solution)/shard_map/ppermute | solution.py:306
  10.0 9.7 %collective-permute-start.10 = (f32[136,128]{1,0:T(8,128)S(1)}, f32[136,128]{1,0:T(8,128)S(1)}, u32[]{:S(2)}, u32[]{:S(2)}) collective-permute-start(f32[136,128]{1,0:T(8,128)S(1)} %get-tuple-element.77.refs_8_.refs_0_), channel_id=1, source_target_pairs={{0,8},{4,12},{8,16},{12,20},{16,24},{20,28},{24,32},{28,36},{32,40... | collective-permute-start | bytes 208904 | tf_op jit(solution)/shard_map/ppermute | solution.py:306
  15.3 6.6 %collective-permute-start.8 = (f32[136,128]{1,0:T(8,128)S(1)}, f32[136,128]{1,0:T(8,128)S(1)}, u32[]{:S(2)}, u32[]{:S(2)}) collective-permute-start(f32[136,128]{1,0:T(8,128)S(1)} %merge.10), channel_id=1, source_target_pairs={{0,8},{4,12},{8,16},{12,20},{16,24},{20,28},{24,32},{28,36},{32,40... | collective-permute-start | bytes 208904 | tf_op jit(solution)/shard_map/ppermute | solution.py:306
  16.7 8.1 %collective-permute-start.5 = (f32[136,128]{1,0:T(8,128)S(1)}, f32[136,128]{1,0:T(8,128)S(1)}, u32[]{:S(2)}, u32[]{:S(2)}) collective-permute-start(f32[136,128]{1,0:T(8,128)S(1)} %merge.9), channel_id=1, source_target_pairs={{0,8},{4,12},{8,16},{12,20},{16,24},{20,28},{24,32},{28,36},{32,40... | collective-permute-start | bytes 208904 | tf_op jit(solution)/shard_map/ppermute | solution.py:306
  18.2 8.1 %collective-permute-start.2 = (f32[136,128]{1,0:T(8,128)S(1)}, f32[136,128]{1,0:T(8,128)S(1)}, u32[]{:S(2)}, u32[]{:S(2)}) collective-permute-start(f32[136,128]{1,0:T(8,128)S(1)} %merge.8), channel_id=1, source_target_pairs={{0,8},{4,12},{8,16},{12,20},{16,24},{20,28},{24,32},{28,36},{32,40... | collective-permute-start | bytes 208904 | tf_op jit(solution)/shard_map/ppermute | solution.py:306
  19.7 8.1 %collective-permute-start.11 = (f32[136,128]{1,0:T(8,128)S(1)}, f32[136,128]{1,0:T(8,128)S(1)}, u32[]{:S(2)}, u32[]{:S(2)}) collective-permute-start(f32[136,128]{1,0:T(8,128)S(1)} %merge.11), channel_id=1, source_target_pairs={{0,8},{4,12},{8,16},{12,20},{16,24},{20,28},{24,32},{28,36},{32,40... | collective-permute-start | bytes 208904 | tf_op jit(solution)/shard_map/ppermute | solution.py:306
  21.8 6.8 %collective-permute-start.9 = (f32[136,128]{1,0:T(8,128)S(1)}, f32[136,128]{1,0:T(8,128)S(1)}, u32[]{:S(2)}, u32[]{:S(2)}) collective-permute-start(f32[136,128]{1,0:T(8,128)S(1)} %get-tuple-element.91), channel_id=1, source_target_pairs={{0,4},{4,0},{8,12},{12,8},{16,20},{20,16},{24,28},{28,24},{32,36},... | collective-permute-start | bytes 208904 | tf_op jit(solution)/shard_map/ppermute | solution.py:303
  24.9 3.7 %collective-permute-start.6 = (f32[136,128]{1,0:T(8,128)S(1)}, f32[136,128]{1,0:T(8,128)S(1)}, u32[]{:S(2)}, u32[]{:S(2)}) collective-permute-start(f32[136,128]{1,0:T(8,128)S(1)} %get-tuple-element.88), channel_id=1, source_target_pairs={{0,4},{4,0},{8,12},{12,8},{16,20},{20,16},{24,28},{28,24},{32,36},... | collective-permute-start | bytes 208904 | tf_op jit(solution)/shard_map/ppermute | solution.py:303
  26.4 2.4 %collective-permute-start.3 = (f32[136,128]{1,0:T(8,128)S(1)}, f32[136,128]{1,0:T(8,128)S(1)}, u32[]{:S(2)}, u32[]{:S(2)}) collective-permute-start(f32[136,128]{1,0:T(8,128)S(1)} %get-tuple-element.85), channel_id=1, source_target_pairs={{0,4},{4,0},{8,12},{12,8},{16,20},{20,16},{24,28},{28,24},{32,36},... | collective-permute-start | bytes 208904 | tf_op jit(solution)/shard_map/ppermute | solution.py:303
  27.9 1.7 %collective-permute-start.12 = (f32[136,128]{1,0:T(8,128)S(1)}, f32[136,128]{1,0:T(8,128)S(1)}, u32[]{:S(2)}, u32[]{:S(2)}) collective-permute-start(f32[136,128]{1,0:T(8,128)S(1)} %get-tuple-element.97), channel_id=1, source_target_pairs={{0,4},{4,0},{8,12},{12,8},{16,20},{20,16},{24,28},{28,24},{32,36},... | collective-permute-start | bytes 208904 | tf_op jit(solution)/shard_map/ppermute | solution.py:303
  30.1 5.2 %collective-permute-start.13 = (f32[8,256]{1,0:T(8,128)S(1)}, f32[8,256]{1,0:T(8,128)S(1)}, u32[]{:S(2)}, u32[]{:S(2)}) collective-permute-start(f32[8,256]{1,0:T(8,128)S(1)} %get-tuple-element.99.refs_7_.refs_26_), channel_id=1, source_target_pairs={{0,1},{1,2},{2,3},{3,0},{4,5},{5,6},{6,7},{7,4},{8,9},{9,10},{10,1... | collective-permute-start | bytes 24584 | tf_op jit(solution)/shard_map/ppermute | solution.py:389
  31.6 4.0 %collective-permute-start.14 = (f32[8,256]{1,0:T(8,128)S(1)}, f32[8,256]{1,0:T(8,128)S(1)}, u32[]{:S(2)}, u32[]{:S(2)}) collective-permute-start(f32[8,256]{1,0:T(8,128)S(1)} %get-tuple-element.99.refs_7_.refs_26_), channel_id=1, source_target_pairs={{0,2},{1,3},{2,0},{3,1},{4,6},{5,7},{6,4},{7,5},{8,10},{9,11},{10,... | collective-permute-start | bytes 24584 | tf_op jit(solution)/shard_map/ppermute | solution.py:389
  34.2 2.8 %collective-permute-start.15 = (f32[8,256]{1,0:T(8,128)S(1)}, f32[8,256]{1,0:T(8,128)S(1)}, u32[]{:S(2)}, u32[]{:S(2)}) collective-permute-start(f32[8,256]{1,0:T(8,128)S(1)} %get-tuple-element.99.refs_7_.refs_26_), channel_id=1, source_target_pairs={{0,3},{1,0},{2,1},{3,2},{4,7},{5,4},{6,5},{7,6},{8,11},{9,8},{10,9... | collective-permute-start | bytes 24584 | tf_op jit(solution)/shard_map/ppermute | solution.py:389
  37.4 3.1 %collective-permute-start.16 = (f32[520,128]{1,0:T(8,128)S(1)}, f32[520,128]{1,0:T(8,128)S(1)}, u32[]{:S(2)}, u32[]{:S(2)}) collective-permute-start(f32[520,128]{1,0:T(8,128)S(1)} %get-tuple-element.104.refs_11_), channel_id=1, source_target_pairs={{0,4},{4,0},{8,12},{12,8},{16,20},{20,16},{24,28},{28,24},{32,36},... | collective-permute-start | bytes 798728 | tf_op jit(solution)/shard_map/ppermute | solution.py:303
  40.5 6.8 %collective-permute-start.26 = (f32[136,128]{1,0:T(8,128)S(1)}, f32[136,128]{1,0:T(8,128)S(1)}, u32[]{:S(2)}, u32[]{:S(2)}) collective-permute-start(f32[136,128]{1,0:T(8,128)S(1)} %get-tuple-element.128.refs_0_), channel_id=1, source_target_pairs={{0,248},{4,252},{8,0},{12,4},{16,8},{20,12},{24,16},{28,20},{32,24... | collective-permute-start | bytes 208904 | tf_op jit(solution)/shard_map/ppermute | solution.py:306
  40.9 6.9 %collective-permute-start.23 = (f32[136,128]{1,0:T(8,128)S(1)}, f32[136,128]{1,0:T(8,128)S(1)}, u32[]{:S(2)}, u32[]{:S(2)}) collective-permute-start(f32[136,128]{1,0:T(8,128)S(1)} %get-tuple-element.125.refs_0_), channel_id=1, source_target_pairs={{0,248},{4,252},{8,0},{12,4},{16,8},{20,12},{24,16},{28,20},{32,24... | collective-permute-start | bytes 208904 | tf_op jit(solution)/shard_map/ppermute | solution.py:306
  41.2 7.9 %collective-permute-start.20 = (f32[136,128]{1,0:T(8,128)S(1)}, f32[136,128]{1,0:T(8,128)S(1)}, u32[]{:S(2)}, u32[]{:S(2)}) collective-permute-start(f32[136,128]{1,0:T(8,128)S(1)} %get-tuple-element.122.refs_0_), channel_id=1, source_target_pairs={{0,248},{4,252},{8,0},{12,4},{16,8},{20,12},{24,16},{28,20},{32,24... | collective-permute-start | bytes 208904 | tf_op jit(solution)/shard_map/ppermute | solution.py:306
  41.6 9.1 %collective-permute-start.17 = (f32[136,128]{1,0:T(8,128)S(1)}, f32[136,128]{1,0:T(8,128)S(1)}, u32[]{:S(2)}, u32[]{:S(2)}) collective-permute-start(f32[136,128]{1,0:T(8,128)S(1)} %get-tuple-element.116.refs_30_.refs_0_), channel_id=1, source_target_pairs={{0,248},{4,252},{8,0},{12,4},{16,8},{20,12},{24,16},{28,20},{32,24... | collective-permute-start | bytes 208904 | tf_op jit(solution)/shard_map/ppermute | solution.py:306
  47.3 4.8 %collective-permute-start.27 = (f32[136,128]{1,0:T(8,128)S(1)}, f32[136,128]{1,0:T(8,128)S(1)}, u32[]{:S(2)}, u32[]{:S(2)}) collective-permute-start(f32[136,128]{1,0:T(8,128)S(1)} %merge.15), channel_id=1, source_target_pairs={{0,248},{4,252},{8,0},{12,4},{16,8},{20,12},{24,16},{28,20},{32,24... | collective-permute-start | bytes 208904 | tf_op jit(solution)/shard_map/ppermute | solution.py:306
  47.7 7.0 %collective-permute-start.24 = (f32[136,128]{1,0:T(8,128)S(1)}, f32[136,128]{1,0:T(8,128)S(1)}, u32[]{:S(2)}, u32[]{:S(2)}) collective-permute-start(f32[136,128]{1,0:T(8,128)S(1)} %merge.14), channel_id=1, source_target_pairs={{0,248},{4,252},{8,0},{12,4},{16,8},{20,12},{24,16},{28,20},{32,24... | collective-permute-start | bytes 208904 | tf_op jit(solution)/shard_map/ppermute | solution.py:306
  49.2 6.3 %collective-permute-start.21 = (f32[136,128]{1,0:T(8,128)S(1)}, f32[136,128]{1,0:T(8,128)S(1)}, u32[]{:S(2)}, u32[]{:S(2)}) collective-permute-start(f32[136,128]{1,0:T(8,128)S(1)} %merge.13), channel_id=1, source_target_pairs={{0,248},{4,252},{8,0},{12,4},{16,8},{20,12},{24,16},{28,20},{32,24... | collective-permute-start | bytes 208904 | tf_op jit(solution)/shard_map/ppermute | solution.py:306
  50.6 5.5 %collective-permute-start.18 = (f32[136,128]{1,0:T(8,128)S(1)}, f32[136,128]{1,0:T(8,128)S(1)}, u32[]{:S(2)}, u32[]{:S(2)}) collective-permute-start(f32[136,128]{1,0:T(8,128)S(1)} %merge.12), channel_id=1, source_target_pairs={{0,248},{4,252},{8,0},{12,4},{16,8},{20,12},{24,16},{28,20},{32,24... | collective-permute-start | bytes 208904 | tf_op jit(solution)/shard_map/ppermute | solution.py:306
  52.1 5.3 %collective-permute-start.28 = (f32[136,128]{1,0:T(8,128)S(1)}, f32[136,128]{1,0:T(8,128)S(1)}, u32[]{:S(2)}, u32[]{:S(2)}) collective-permute-start(f32[136,128]{1,0:T(8,128)S(1)} %get-tuple-element.130), channel_id=1, source_target_pairs={{0,4},{4,0},{8,12},{12,8},{16,20},{20,16},{24,28},{28,24},{32,36},... | collective-permute-start | bytes 208904 | tf_op jit(solution)/shard_map/ppermute | solution.py:303
  54.7 2.7 %collective-permute-start.25 = (f32[136,128]{1,0:T(8,128)S(1)}, f32[136,128]{1,0:T(8,128)S(1)}, u32[]{:S(2)}, u32[]{:S(2)}) collective-permute-start(f32[136,128]{1,0:T(8,128)S(1)} %get-tuple-element.127), channel_id=1, source_target_pairs={{0,4},{4,0},{8,12},{12,8},{16,20},{20,16},{24,28},{28,24},{32,36},... | collective-permute-start | bytes 208904 | tf_op jit(solution)/shard_map/ppermute | solution.py:303
  55.5 2.0 %collective-permute-start.22 = (f32[136,128]{1,0:T(8,128)S(1)}, f32[136,128]{1,0:T(8,128)S(1)}, u32[]{:S(2)}, u32[]{:S(2)}) collective-permute-start(f32[136,128]{1,0:T(8,128)S(1)} %get-tuple-element.124), channel_id=1, source_target_pairs={{0,4},{4,0},{8,12},{12,8},{16,20},{20,16},{24,28},{28,24},{32,36},... | collective-permute-start | bytes 208904 | tf_op jit(solution)/shard_map/ppermute | solution.py:303
  56.2 2.5 %collective-permute-start.19 = (f32[136,128]{1,0:T(8,128)S(1)}, f32[136,128]{1,0:T(8,128)S(1)}, u32[]{:S(2)}, u32[]{:S(2)}) collective-permute-start(f32[136,128]{1,0:T(8,128)S(1)} %get-tuple-element.121), channel_id=1, source_target_pairs={{0,4},{4,0},{8,12},{12,8},{16,20},{20,16},{24,28},{28,24},{32,36},... | collective-permute-start | bytes 208904 | tf_op jit(solution)/shard_map/ppermute | solution.py:303

commit v8 on v6

--- a/solution.py
+++ b/solution.py
@@ -332,6 +332,7 @@
     heads = width // HD
     part_width = width // 2
     ranks = lax.axis_size("head")
+    blocks = lax.axis_size("ctx")
     ids = doc_ids.reshape(1, rows)
     gain = out_gain.reshape(1, width)
     wide, half, sums = ((rows, width), F32), ((rows, part_width), BF16), ((TAG, rows), F32)
@@ -385,9 +386,15 @@
     scores, part, q, weighted, gain = work
     order = [(which, i) for which in range(2) for i in range(CHUNKS)]
     stats = stats[-1:]
+
+    def around(apart):
+        return [
+            (c * ranks + i, c * ranks + (i + (apart if c % 2 else -apart)) % ranks)
+            for c in range(blocks) for i in range(ranks)
+        ]
+
     stats += [
-        lax.ppermute(stats[0], "head", [(i, (i + apart) % ranks) for i in range(ranks)])
-        for apart in range(1, ranks)
+        lax.ppermute(stats[0], ("ctx", "head"), around(apart)) for apart in range(1, ranks)
     ]
 
     def make_grad(which, after=()):

time: 59.4 us -> 59.8 us (level)
  starting transfers between devices: 26.3 us -> 27 us
    ppermute x6, starting transfers between devices: 12.6 us -> 13.3 us  [swap(): return lax.ppermute(value, 'ctx', [(i, i ^ 1) for i in range(blocks)])]
where the time goes in v8:
time: 59.8 us; the launch traced here: 59.7 us
  starting transfers between devices  27 us (45%)
  waiting for transfers between devices  18.4 us (31%)
  Pallas kernels  13.3 us (22%)
  between operations  0.97 us (2%)
    ppermute x8, waiting for transfers between devices, hop(): lax.ppermute(value, 'ctx', [(i, (i + step) % blocks) for i in range(block...  16 us
    pallas_call x20, Pallas kernels, call(): pl.pallas_call(lambda *refs: kernel(*fixed, *refs), out_shape=[jax.ShapeD...  13.3 us
    ppermute x6, starting transfers between devices, swap(): return lax.ppermute(value, 'ctx', [(i, i ^ 1) for i in range(blocks)])  13.3 us
    ppermute x8, starting transfers between devices, hop(): lax.ppermute(value, 'ctx', [(i, (i + step) % blocks) for i in range(block...  8.71 us
    ppermute x3, starting transfers between devices, local(): lax.ppermute(stats[0], ('ctx', 'head'), around(apart))  5.01 us
    ppermute x3, waiting for transfers between devices, local(): lax.ppermute(stats[0], ('ctx', 'head'), around(apart))  1.43 us
  transfers between devices with their start and end apart: 17, of which 10 were waited for; matrix products, arithmetic and copies ran while one was open for 0% of the time, Pallas kernels for 17%

profile of v8, /device:TPU:1, one launch (start us, length us, event | category | flops | bytes accessed | tf_op | source)
XLA Modules:
  0.0 59.7 jit_solution(7618254530781307118)
XLA Ops:
  0.6 1.3 %state.2 = (f32[520,128]{1,0:T(8,128)S(1)}, bf16[256,512]{1,0:T(8,128)(2,1)S(1)}, bf16[256,512]{1,0:T(8,128)(2,1)S(1)}, s32[1,256]{1,0:T(1,128)S(1)}) custom-call(s32[1,256]{1,0:T(1,128)} %bitcast.3, bf16[256,1024]{1,0:T(8,128)(2,1)} %refs_1_.3, bf16[256,1024]{1,0:T(8,128)(2,1)} %refs_2_.3), custom_call_target="tpu_custom_call" | custom-call | tf_op jit(solution)/shard_map/state/pallas_call | solution.py:286
  2.0 3.3 %collective-permute-start = (f32[520,128]{1,0:T(8,128)S(1)}, f32[520,128]{1,0:T(8,128)S(1)}, u32[]{:S(2)}, u32[]{:S(2)}) collective-permute-start(f32[520,128]{1,0:T(8,128)S(1)} %get-tuple-element.51.refs_3_), channel_id=1, source_target_pairs={{0,4},{4,0},{8,12},{12,8},{16,20},{20,16},{24,28},{28,24},{32,36},... | collective-permute-start | bytes 798728 | tf_op jit(solution)/shard_map/ppermute | solution.py:303
  5.3 1.3 %state.3 = (f32[520,128]{1,0:T(8,128)S(1)}, bf16[256,512]{1,0:T(8,128)(2,1)S(1)}, bf16[256,512]{1,0:T(8,128)(2,1)S(1)}) custom-call(s32[1,256]{1,0:T(1,128)S(1)} %get-tuple-element.50.refs_0_, bf16[256,1024]{1,0:T(8,128)(2,1)} %refs_1_.3, bf16[256,1024]{1,0:T(8,128)(2,1)} %refs_2_.3, f32[520,128]{1,0:T(8,128)S(1)} %get-tuple-element.51.refs_3_), custom_call_target="tpu_custom_call" | custom-call | tf_op jit(solution)/shard_map/state/pallas_call | solution.py:286
  6.6 0.0 collective-permute-done.refs_1_.refs_2_
  6.6 0.1 pair.2
  6.7 0.1 collective-permute-start.1
  6.8 1.6 %collective-permute-start.4 = (f32[264,128]{1,0:T(8,128)S(1)}, f32[264,128]{1,0:T(8,128)S(1)}, u32[]{:S(2)}, u32[]{:S(2)}) collective-permute-start(f32[264,128]{1,0:T(8,128)S(1)} %get-tuple-element.57.refs_8_.refs_0_), channel_id=1, source_target_pairs={{0,8},{4,12},{8,16},{12,20},{16,24},{20,28},{24,32},{28,36},{32,40... | collective-permute-start | bytes 405512 | tf_op jit(solution)/shard_map/ppermute | solution.py:306
  8.3 2.2 %local.1 = (bf16[8,256,256]{2,1,0:T(8,128)(2,1)S(1)}, f32[256,1024]{1,0:T(8,128)S(1)}, bf16[256,1024]{1,0:T(8,128)(2,1)S(1)}, f32[256,1024]{1,0:T(8,128)S(1)}, f32[1,1024]{1,0:T(1,128)S(1)}) custom-call(s32[1,256]{1,0:T(1,128)S(1)} %get-tuple-element.50.refs_0_, bf16[256,512]{1,0:T(8,128)(2,1)S(1)} %get-tuple-element.52.refs_1_.refs_4_.refs_10_, ...), custom_call_target="tpu_custom_call" | custom-call | tf_op jit(solution)/shard_map/local/pallas_call | solution.py:286
  10.5 6.1 %collective-permute-done.1.refs_1_ = f32[264,128]{1,0:T(8,128)S(1)} collective-permute-done((f32[264,128]{1,0:T(8,128)S(1)}, f32[264,128]{1,0:T(8,128)S(1)}, u32[]{:S(2)}, u32[]{:S(2)}) %collective-permute-start.1) | collective-permute-done | bytes 135200 | tf_op jit(solution)/shard_map/ppermute | solution.py:306
  16.6 0.1 collective-permute-start.2
  16.7 2.8 %collective-permute-done.4.refs_1_ = f32[264,128]{1,0:T(8,128)S(1)} collective-permute-done((f32[264,128]{1,0:T(8,128)S(1)}, f32[264,128]{1,0:T(8,128)S(1)}, u32[]{:S(2)}, u32[]{:S(2)}) %collective-permute-start.4) | collective-permute-done | bytes 135200 | tf_op jit(solution)/shard_map/ppermute | solution.py:306
  19.5 0.1 collective-permute-start.5
  19.6 4.3 %collective-permute-done.2.refs_0_ = f32[264,128]{1,0:T(8,128)S(1)} collective-permute-done((f32[264,128]{1,0:T(8,128)S(1)}, f32[264,128]{1,0:T(8,128)S(1)}, u32[]{:S(2)}, u32[]{:S(2)}) %collective-permute-start.2) | collective-permute-done | bytes 135200 | tf_op jit(solution)/shard_map/ppermute | solution.py:306
  23.9 2.5 %collective-permute-start.3 = (f32[264,128]{1,0:T(8,128)S(1)}, f32[264,128]{1,0:T(8,128)S(1)}, u32[]{:S(2)}, u32[]{:S(2)}) collective-permute-start(f32[264,128]{1,0:T(8,128)S(1)} %get-tuple-element.65), channel_id=1, source_target_pairs={{0,4},{4,0},{8,12},{12,8},{16,20},{20,16},{24,28},{28,24},{32,36},... | collective-permute-start | bytes 405512 | tf_op jit(solution)/shard_map/ppermute | solution.py:303
  26.4 1.2 %collective-permute-done.5.refs_0_ = f32[264,128]{1,0:T(8,128)S(1)} collective-permute-done((f32[264,128]{1,0:T(8,128)S(1)}, f32[264,128]{1,0:T(8,128)S(1)}, u32[]{:S(2)}, u32[]{:S(2)}) %collective-permute-start.5) | collective-permute-done | bytes 135200 | tf_op jit(solution)/shard_map/ppermute | solution.py:306
  27.6 1.6 %collective-permute-start.6 = (f32[264,128]{1,0:T(8,128)S(1)}, f32[264,128]{1,0:T(8,128)S(1)}, u32[]{:S(2)}, u32[]{:S(2)}) collective-permute-start(f32[264,128]{1,0:T(8,128)S(1)} %get-tuple-element.69), channel_id=1, source_target_pairs={{0,4},{4,0},{8,12},{12,8},{16,20},{20,16},{24,28},{28,24},{32,36},... | collective-permute-start | bytes 405512 | tf_op jit(solution)/shard_map/ppermute | solution.py:303
  29.2 0.0 collective-permute-done.3.refs_5_
  29.2 0.8 %attend.2 = (bf16[256,256]{1,0:T(8,128)(2,1)S(1)}, bf16[256,256]{1,0:T(8,128)(2,1)S(1)}, bf16[256,256]{1,0:T(8,128)(2,1)S(1)}, bf16[256,128]{1,0:T(8,128)(2,1)S(...) custom-call(s32[1,256]{1,0:T(1,128)S(1)} %get-tuple-element.50.refs_0_, ...), custom_call_target="tpu_custom_call" | custom-call | tf_op jit(solution)/shard_map/attend/pallas_call | solution.py:286
  29.9 0.2 collective-permute-done.6.refs_4_
  30.2 0.6 attend.3
  30.7 1.3 %collective-permute-start.7 = (f32[8,256]{1,0:T(8,128)S(1)}, f32[8,256]{1,0:T(8,128)S(1)}, u32[]{:S(2)}, u32[]{:S(2)}) collective-permute-start(f32[8,256]{1,0:T(8,128)S(1)} %get-tuple-element.71.refs_5_.refs_18_), channel_id=1, source_target_pairs={{0,3},{1,0},{2,1},{3,2},{4,5},{5,6},{6,7},{7,4},{8,11},{9,8},{10,9... | collective-permute-start | bytes 24584 | tf_op jit(solution)/shard_map/ppermute | solution.py:397
  32.1 2.6 %collective-permute-start.8 = (f32[8,256]{1,0:T(8,128)S(1)}, f32[8,256]{1,0:T(8,128)S(1)}, u32[]{:S(2)}, u32[]{:S(2)}) collective-permute-start(f32[8,256]{1,0:T(8,128)S(1)} %get-tuple-element.71.refs_5_.refs_18_), channel_id=1, source_target_pairs={{0,2},{1,3},{2,0},{3,1},{4,6},{5,7},{6,4},{7,5},{8,10},{9,11},{10,... | collective-permute-start | bytes 24584 | tf_op jit(solution)/shard_map/ppermute | solution.py:397
  34.7 1.1 %collective-permute-start.9 = (f32[8,256]{1,0:T(8,128)S(1)}, f32[8,256]{1,0:T(8,128)S(1)}, u32[]{:S(2)}, u32[]{:S(2)}) collective-permute-start(f32[8,256]{1,0:T(8,128)S(1)} %get-tuple-element.71.refs_5_.refs_18_), channel_id=1, source_target_pairs={{0,1},{1,2},{2,3},{3,0},{4,7},{5,4},{6,5},{7,6},{8,9},{9,10},{10,1... | collective-permute-start | bytes 24584 | tf_op jit(solution)/shard_map/ppermute | solution.py:397
  35.8 0.0 collective-permute-done.7.refs_6_.refs_19_
  35.8 0.3 collective-permute-done.8.refs_7_.refs_20_
  36.1 1.1 %collective-permute-done.9.refs_8_.refs_21_ = f32[8,256]{1,0:T(8,128)S(1)} collective-permute-done((f32[8,256]{1,0:T(8,128)S(1)}, f32[8,256]{1,0:T(8,128)S(1)}, u32[]{:S(2)}, u32[]{:S(2)}) %collective-permute-start.9) | collective-permute-done | bytes 8224 | tf_op jit(solution)/shard_map/ppermute | solution.py:397
  37.2 0.4 grad.2
  37.6 2.5 %collective-permute-start.10 = (f32[520,128]{1,0:T(8,128)S(1)}, f32[520,128]{1,0:T(8,128)S(1)}, u32[]{:S(2)}, u32[]{:S(2)}) collective-permute-start(f32[520,128]{1,0:T(8,128)S(1)} %get-tuple-element.74.refs_9_), channel_id=1, source_target_pairs={{0,4},{4,0},{8,12},{12,8},{16,20},{20,16},{24,28},{28,24},{32,36},... | collective-permute-start | bytes 798728 | tf_op jit(solution)/shard_map/ppermute | solution.py:303
  40.2 0.4 grad.3
  40.6 0.7 %collective-permute-done.10.refs_1_.refs_2_ = f32[520,128]{1,0:T(8,128)S(1)} collective-permute-done((f32[520,128]{1,0:T(8,128)S(1)}, f32[520,128]{1,0:T(8,128)S(1)}, u32[]{:S(2)}, u32[]{:S(2)}) %collective-permute-start.10) | collective-permute-done | bytes 266272 | tf_op jit(solution)/shard_map/ppermute | solution.py:303
  41.4 0.1 collective-permute-start.14
  41.5 0.3 collective-permute-start.11
  41.7 3.7 %back.1 = (bf16[256,1024]{1,0:T(8,128)(2,1)}, bf16[256,1024]{1,0:T(8,128)(2,1)}, f32[256,1024]{1,0:T(8,128)S(1)}, f32[256,1024]{1,0:T(8,128)S(1)}) custom-call(s32[1,256]{1,0:T(1,128)S(1)} %get-tuple-element.50.refs_0_, bf16[256,1024]{1,0:T(8,128)(2,1)S(1)} %get-tuple-element.58.refs_1_, bf16[8,256,256]{2,1,0:T(8,128)(2,1)S(1)} %get-tuple-element.59.refs_2_, ...), custom_call_target="tpu_custom_call" | custom-call | tf_op jit(solution)/shard_map/back/pallas_call | solution.py:286
  45.5 0.7 %collective-permute-done.14.refs_1_ = f32[264,128]{1,0:T(8,128)S(1)} collective-permute-done((f32[264,128]{1,0:T(8,128)S(1)}, f32[264,128]{1,0:T(8,128)S(1)}, u32[]{:S(2)}, u32[]{:S(2)}) %collective-permute-start.14) | collective-permute-done | bytes 135200 | tf_op jit(solution)/shard_map/ppermute | solution.py:306
  46.2 3.7 %collective-permute-start.15 = (f32[264,128]{1,0:T(8,128)S(1)}, f32[264,128]{1,0:T(8,128)S(1)}, u32[]{:S(2)}, u32[]{:S(2)}) collective-permute-start(f32[264,128]{1,0:T(8,128)S(1)} %merge.7), channel_id=1, source_target_pairs={{0,248},{4,252},{8,0},{12,4},{16,8},{20,12},{24,16},{28,20},{32,24... | collective-permute-start | bytes 405512 | tf_op jit(solution)/shard_map/ppermute | solution.py:306
  49.9 0.0 collective-permute-done.11.refs_1_
  50.0 2.9 %collective-permute-start.12 = (f32[264,128]{1,0:T(8,128)S(1)}, f32[264,128]{1,0:T(8,128)S(1)}, u32[]{:S(2)}, u32[]{:S(2)}) collective-permute-start(f32[264,128]{1,0:T(8,128)S(1)} %merge.6), channel_id=1, source_target_pairs={{0,248},{4,252},{8,0},{12,4},{16,8},{20,12},{24,16},{28,20},{32,24... | collective-permute-start | bytes 405512 | tf_op jit(solution)/shard_map/ppermute | solution.py:306
  52.8 0.0 collective-permute-done.15.refs_0_
  52.9 2.0 %collective-permute-start.16 = (f32[264,128]{1,0:T(8,128)S(1)}, f32[264,128]{1,0:T(8,128)S(1)}, u32[]{:S(2)}, u32[]{:S(2)}) collective-permute-start(f32[264,128]{1,0:T(8,128)S(1)} %get-tuple-element.90), channel_id=1, source_target_pairs={{0,4},{4,0},{8,12},{12,8},{16,20},{20,16},{24,28},{28,24},{32,36},... | collective-permute-start | bytes 405512 | tf_op jit(solution)/shard_map/ppermute | solution.py:303
  54.9 1.0 %collective-permute-done.12.refs_0_ = f32[264,128]{1,0:T(8,128)S(1)} collective-permute-done((f32[264,128]{1,0:T(8,128)S(1)}, f32[264,128]{1,0:T(8,128)S(1)}, u32[]{:S(2)}, u32[]{:S(2)}) %collective-permute-start.12) | collective-permute-done | bytes 135200 | tf_op jit(solution)/shard_map/ppermute | solution.py:306
  55.9 1.4 %collective-permute-start.13 = (f32[264,128]{1,0:T(8,128)S(1)}, f32[264,128]{1,0:T(8,128)S(1)}, u32[]{:S(2)}, u32[]{:S(2)}) collective-permute-start(f32[264,128]{1,0:T(8,128)S(1)} %get-tuple-element.87), channel_id=1, source_target_pairs={{0,4},{4,0},{8,12},{12,8},{16,20},{20,16},{24,28},{28,24},{32,36},... | collective-permute-start | bytes 405512 | tf_op jit(solution)/shard_map/ppermute | solution.py:303
  57.3 0.0 collective-permute-done.16.refs_6_
  57.3 1.2 %last.2 = (bf16[256,1024]{1,0:T(8,128)(2,1)}, bf16[256,1024]{1,0:T(8,128)(2,1)}) custom-call(s32[1,256]{1,0:T(1,128)S(1)} %get-tuple-element.50.refs_0_, f32[256,1024]{1,0:T(8,128)S(1)} %get-tuple-element.85.refs_2_.refs_1_, f32[256,1024]{1,0:T(8,128)S(1)} %get-tuple-element.86.refs_2_, f32[264,128]{1,0:T(8,128)S(1)} %get-tuple-element.89.refs_3_, ...), custom_call_target="tpu_custom_call" | custom-call | tf_op jit(solution)/shard_map/last/pallas_call | solution.py:286
  58.5 0.0 collective-permute-done.13.refs_3_
  58.5 1.0 %last.3 = (bf16[256,1024]{1,0:T(8,128)(2,1)}, bf16[256,1024]{1,0:T(8,128)(2,1)}) custom-call(s32[1,256]{1,0:T(1,128)S(1)} %get-tuple-element.50.refs_0_, f32[256,1024]{1,0:T(8,128)S(1)} %get-tuple-element.85.refs_2_.refs_1_, f32[256,1024]{1,0:T(8,128)S(1)} %get-tuple-element.86.refs_2_, ...), custom_call_target="tpu_custom_call", output_to_operand_aliasing={{0}: (6, {}), {1}: (7, {})} | custom-call | tf_op jit(solution)/shard_map/last/pallas_call | solution.py:286
  (9 shorter events, 0.2 us)
Async XLA Ops:
  2.0 4.6 %collective-permute-start = (f32[520,128]{1,0:T(8,128)S(1)}, f32[520,128]{1,0:T(8,128)S(1)}, u32[]{:S(2)}, u32[]{:S(2)}) collective-permute-start(f32[520,128]{1,0:T(8,128)S(1)} %get-tuple-element.51.refs_3_), channel_id=1, source_target_pairs={{0,4},{4,0},{8,12},{12,8},{16,20},{20,16},{24,28},{28,24},{32,36},... | collective-permute-start | bytes 798728 | tf_op jit(solution)/shard_map/ppermute | solution.py:303
  6.7 9.9 %collective-permute-start.1 = (f32[264,128]{1,0:T(8,128)S(1)}, f32[264,128]{1,0:T(8,128)S(1)}, u32[]{:S(2)}, u32[]{:S(2)}) collective-permute-start(f32[264,128]{1,0:T(8,128)S(1)} %get-tuple-element.63.refs_0_), channel_id=1, source_target_pairs={{0,8},{4,12},{8,16},{12,20},{16,24},{20,28},{24,32},{28,36},{32,40... | collective-permute-start | bytes 405512 | tf_op jit(solution)/shard_map/ppermute | solution.py:306
  6.8 12.7 %collective-permute-start.4 = (f32[264,128]{1,0:T(8,128)S(1)}, f32[264,128]{1,0:T(8,128)S(1)}, u32[]{:S(2)}, u32[]{:S(2)}) collective-permute-start(f32[264,128]{1,0:T(8,128)S(1)} %get-tuple-element.57.refs_8_.refs_0_), channel_id=1, source_target_pairs={{0,8},{4,12},{8,16},{12,20},{16,24},{20,28},{24,32},{28,36},{32,40... | collective-permute-start | bytes 405512 | tf_op jit(solution)/shard_map/ppermute | solution.py:306
  16.6 7.3 %collective-permute-start.2 = (f32[264,128]{1,0:T(8,128)S(1)}, f32[264,128]{1,0:T(8,128)S(1)}, u32[]{:S(2)}, u32[]{:S(2)}) collective-permute-start(f32[264,128]{1,0:T(8,128)S(1)} %merge.4), channel_id=1, source_target_pairs={{0,8},{4,12},{8,16},{12,20},{16,24},{20,28},{24,32},{28,36},{32,40... | collective-permute-start | bytes 405512 | tf_op jit(solution)/shard_map/ppermute | solution.py:306
  19.5 8.0 %collective-permute-start.5 = (f32[264,128]{1,0:T(8,128)S(1)}, f32[264,128]{1,0:T(8,128)S(1)}, u32[]{:S(2)}, u32[]{:S(2)}) collective-permute-start(f32[264,128]{1,0:T(8,128)S(1)} %merge.5), channel_id=1, source_target_pairs={{0,8},{4,12},{8,16},{12,20},{16,24},{20,28},{24,32},{28,36},{32,40... | collective-permute-start | bytes 405512 | tf_op jit(solution)/shard_map/ppermute | solution.py:306
  23.9 5.2 %collective-permute-start.3 = (f32[264,128]{1,0:T(8,128)S(1)}, f32[264,128]{1,0:T(8,128)S(1)}, u32[]{:S(2)}, u32[]{:S(2)}) collective-permute-start(f32[264,128]{1,0:T(8,128)S(1)} %get-tuple-element.65), channel_id=1, source_target_pairs={{0,4},{4,0},{8,12},{12,8},{16,20},{20,16},{24,28},{28,24},{32,36},... | collective-permute-start | bytes 405512 | tf_op jit(solution)/shard_map/ppermute | solution.py:303
  27.6 2.6 %collective-permute-start.6 = (f32[264,128]{1,0:T(8,128)S(1)}, f32[264,128]{1,0:T(8,128)S(1)}, u32[]{:S(2)}, u32[]{:S(2)}) collective-permute-start(f32[264,128]{1,0:T(8,128)S(1)} %get-tuple-element.69), channel_id=1, source_target_pairs={{0,4},{4,0},{8,12},{12,8},{16,20},{20,16},{24,28},{28,24},{32,36},... | collective-permute-start | bytes 405512 | tf_op jit(solution)/shard_map/ppermute | solution.py:303
  30.7 5.0 %collective-permute-start.7 = (f32[8,256]{1,0:T(8,128)S(1)}, f32[8,256]{1,0:T(8,128)S(1)}, u32[]{:S(2)}, u32[]{:S(2)}) collective-permute-start(f32[8,256]{1,0:T(8,128)S(1)} %get-tuple-element.71.refs_5_.refs_18_), channel_id=1, source_target_pairs={{0,3},{1,0},{2,1},{3,2},{4,5},{5,6},{6,7},{7,4},{8,11},{9,8},{10,9... | collective-permute-start | bytes 24584 | tf_op jit(solution)/shard_map/ppermute | solution.py:397
  32.1 4.0 %collective-permute-start.8 = (f32[8,256]{1,0:T(8,128)S(1)}, f32[8,256]{1,0:T(8,128)S(1)}, u32[]{:S(2)}, u32[]{:S(2)}) collective-permute-start(f32[8,256]{1,0:T(8,128)S(1)} %get-tuple-element.71.refs_5_.refs_18_), channel_id=1, source_target_pairs={{0,2},{1,3},{2,0},{3,1},{4,6},{5,7},{6,4},{7,5},{8,10},{9,11},{10,... | collective-permute-start | bytes 24584 | tf_op jit(solution)/shard_map/ppermute | solution.py:397
  34.7 2.5 %collective-permute-start.9 = (f32[8,256]{1,0:T(8,128)S(1)}, f32[8,256]{1,0:T(8,128)S(1)}, u32[]{:S(2)}, u32[]{:S(2)}) collective-permute-start(f32[8,256]{1,0:T(8,128)S(1)} %get-tuple-element.71.refs_5_.refs_18_), channel_id=1, source_target_pairs={{0,1},{1,2},{2,3},{3,0},{4,7},{5,4},{6,5},{7,6},{8,9},{9,10},{10,1... | collective-permute-start | bytes 24584 | tf_op jit(solution)/shard_map/ppermute | solution.py:397
  37.6 3.7 %collective-permute-start.10 = (f32[520,128]{1,0:T(8,128)S(1)}, f32[520,128]{1,0:T(8,128)S(1)}, u32[]{:S(2)}, u32[]{:S(2)}) collective-permute-start(f32[520,128]{1,0:T(8,128)S(1)} %get-tuple-element.74.refs_9_), channel_id=1, source_target_pairs={{0,4},{4,0},{8,12},{12,8},{16,20},{20,16},{24,28},{28,24},{32,36},... | collective-permute-start | bytes 798728 | tf_op jit(solution)/shard_map/ppermute | solution.py:303
  41.4 4.8 %collective-permute-start.14 = (f32[264,128]{1,0:T(8,128)S(1)}, f32[264,128]{1,0:T(8,128)S(1)}, u32[]{:S(2)}, u32[]{:S(2)}) collective-permute-start(f32[264,128]{1,0:T(8,128)S(1)} %get-tuple-element.88.refs_0_), channel_id=1, source_target_pairs={{0,248},{4,252},{8,0},{12,4},{16,8},{20,12},{24,16},{28,20},{32,24... | collective-permute-start | bytes 405512 | tf_op jit(solution)/shard_map/ppermute | solution.py:306
  41.5 8.5 %collective-permute-start.11 = (f32[264,128]{1,0:T(8,128)S(1)}, f32[264,128]{1,0:T(8,128)S(1)}, u32[]{:S(2)}, u32[]{:S(2)}) collective-permute-start(f32[264,128]{1,0:T(8,128)S(1)} %get-tuple-element.82.refs_22_.refs_0_), channel_id=1, source_target_pairs={{0,248},{4,252},{8,0},{12,4},{16,8},{20,12},{24,16},{28,20},{32,24... | collective-permute-start | bytes 405512 | tf_op jit(solution)/shard_map/ppermute | solution.py:306
  46.2 6.6 %collective-permute-start.15 = (f32[264,128]{1,0:T(8,128)S(1)}, f32[264,128]{1,0:T(8,128)S(1)}, u32[]{:S(2)}, u32[]{:S(2)}) collective-permute-start(f32[264,128]{1,0:T(8,128)S(1)} %merge.7), channel_id=1, source_target_pairs={{0,248},{4,252},{8,0},{12,4},{16,8},{20,12},{24,16},{28,20},{32,24... | collective-permute-start | bytes 405512 | tf_op jit(solution)/shard_map/ppermute | solution.py:306
  50.0 5.9 %collective-permute-start.12 = (f32[264,128]{1,0:T(8,128)S(1)}, f32[264,128]{1,0:T(8,128)S(1)}, u32[]{:S(2)}, u32[]{:S(2)}) collective-permute-start(f32[264,128]{1,0:T(8,128)S(1)} %merge.6), channel_id=1, source_target_pairs={{0,248},{4,252},{8,0},{12,4},{16,8},{20,12},{24,16},{28,20},{32,24... | collective-permute-start | bytes 405512 | tf_op jit(solution)/shard_map/ppermute | solution.py:306
  52.9 4.4 %collective-permute-start.16 = (f32[264,128]{1,0:T(8,128)S(1)}, f32[264,128]{1,0:T(8,128)S(1)}, u32[]{:S(2)}, u32[]{:S(2)}) collective-permute-start(f32[264,128]{1,0:T(8,128)S(1)} %get-tuple-element.90), channel_id=1, source_target_pairs={{0,4},{4,0},{8,12},{12,8},{16,20},{20,16},{24,28},{28,24},{32,36},... | collective-permute-start | bytes 405512 | tf_op jit(solution)/shard_map/ppermute | solution.py:303
  55.9 2.6 %collective-permute-start.13 = (f32[264,128]{1,0:T(8,128)S(1)}, f32[264,128]{1,0:T(8,128)S(1)}, u32[]{:S(2)}, u32[]{:S(2)}) collective-permute-start(f32[264,128]{1,0:T(8,128)S(1)} %get-tuple-element.87), channel_id=1, source_target_pairs={{0,4},{4,0},{8,12},{12,8},{16,20},{20,16},{24,28},{28,24},{32,36},... | collective-permute-start | bytes 405512 | tf_op jit(solution)/shard_map/ppermute | solution.py:303

commit v9 on v6

--- a/solution.py
+++ b/solution.py
@@ -386,7 +386,7 @@
     order = [(which, i) for which in range(2) for i in range(CHUNKS)]
     stats = stats[-1:]
     stats += [
-        lax.ppermute(stats[0], "head", [(i, (i + apart) % ranks) for i in range(ranks)])
+        lax.ppermute(stats[0], "head", [(i, i ^ apart) for i in range(ranks)])
         for apart in range(1, ranks)
     ]
 

time: 59.4 us -> 60.7 us (1.022)
  waiting for transfers between devices: 18.7 us -> 20.7 us
  starting transfers between devices: 26.3 us -> 25.5 us
    ppermute x3, waiting for transfers between devices: 1.72 us -> 3.71 us  [local(): lax.ppermute(stats[0], 'head', [(i, i ^ apart) for i in range(ranks)])]
    ppermute x3, starting transfers between devices: 5.01 us -> 3.95 us  [local(): lax.ppermute(stats[0], 'head', [(i, i ^ apart) for i in range(ranks)])]
  transfers between devices with their start and end apart: 17 -> 17, of which waited for: 10 -> 10; matrix products, arithmetic and copies ran while one was open for 0% -> 0% of each run, Pallas kernels for 17% -> 16%
where the time goes in v9:
time: 60.7 us; the launch traced here: 60.5 us
  starting transfers between devices  25.5 us (42%)
  waiting for transfers between devices  20.7 us (34%)
  Pallas kernels  13.3 us (22%)
  between operations  0.97 us (2%)
    ppermute x8, waiting for transfers between devices, hop(): lax.ppermute(value, 'ctx', [(i, (i + step) % blocks) for i in range(block...  16.1 us
    pallas_call x20, Pallas kernels, call(): pl.pallas_call(lambda *refs: kernel(*fixed, *refs), out_shape=[jax.ShapeD...  13.3 us
    ppermute x6, starting transfers between devices, swap(): return lax.ppermute(value, 'ctx', [(i, i ^ 1) for i in range(blocks)])  12.9 us
    ppermute x8, starting transfers between devices, hop(): lax.ppermute(value, 'ctx', [(i, (i + step) % blocks) for i in range(block...  8.71 us
    ppermute x3, starting transfers between devices, local(): lax.ppermute(stats[0], 'head', [(i, i ^ apart) for i in range(ranks)])  3.95 us
    ppermute x3, waiting for transfers between devices, local(): lax.ppermute(stats[0], 'head', [(i, i ^ apart) for i in range(ranks)])  3.71 us
  transfers between devices with their start and end apart: 17, of which 10 were waited for; matrix products, arithmetic and copies ran while one was open for 0% of the time, Pallas kernels for 16%

profile of v9, /device:TPU:1, one launch (start us, length us, event | category | flops | bytes accessed | tf_op | source)
XLA Modules:
  0.0 60.5 jit_solution(15138540918099660569)
XLA Ops:
  0.6 1.3 %state.2 = (f32[520,128]{1,0:T(8,128)S(1)}, bf16[256,512]{1,0:T(8,128)(2,1)S(1)}, bf16[256,512]{1,0:T(8,128)(2,1)S(1)}, s32[1,256]{1,0:T(1,128)S(1)}) custom-call(s32[1,256]{1,0:T(1,128)} %bitcast.3, bf16[256,1024]{1,0:T(8,128)(2,1)} %refs_1_.3, bf16[256,1024]{1,0:T(8,128)(2,1)} %refs_2_.3), custom_call_target="tpu_custom_call" | custom-call | tf_op jit(solution)/shard_map/state/pallas_call | solution.py:286
  2.0 3.3 %collective-permute-start = (f32[520,128]{1,0:T(8,128)S(1)}, f32[520,128]{1,0:T(8,128)S(1)}, u32[]{:S(2)}, u32[]{:S(2)}) collective-permute-start(f32[520,128]{1,0:T(8,128)S(1)} %get-tuple-element.51.refs_3_), channel_id=1, source_target_pairs={{0,4},{4,0},{8,12},{12,8},{16,20},{20,16},{24,28},{28,24},{32,36},... | collective-permute-start | bytes 798728 | tf_op jit(solution)/shard_map/ppermute | solution.py:303
  5.3 1.3 %state.3 = (f32[520,128]{1,0:T(8,128)S(1)}, bf16[256,512]{1,0:T(8,128)(2,1)S(1)}, bf16[256,512]{1,0:T(8,128)(2,1)S(1)}) custom-call(s32[1,256]{1,0:T(1,128)S(1)} %get-tuple-element.50.refs_0_, bf16[256,1024]{1,0:T(8,128)(2,1)} %refs_1_.3, bf16[256,1024]{1,0:T(8,128)(2,1)} %refs_2_.3, f32[520,128]{1,0:T(8,128)S(1)} %get-tuple-element.51.refs_3_), custom_call_target="tpu_custom_call" | custom-call | tf_op jit(solution)/shard_map/state/pallas_call | solution.py:286
  6.6 0.0 collective-permute-done.refs_1_.refs_2_
  6.6 0.1 pair.2
  6.7 0.1 collective-permute-start.1
  6.8 1.6 %collective-permute-start.4 = (f32[264,128]{1,0:T(8,128)S(1)}, f32[264,128]{1,0:T(8,128)S(1)}, u32[]{:S(2)}, u32[]{:S(2)}) collective-permute-start(f32[264,128]{1,0:T(8,128)S(1)} %get-tuple-element.57.refs_8_.refs_0_), channel_id=1, source_target_pairs={{0,8},{4,12},{8,16},{12,20},{16,24},{20,28},{24,32},{28,36},{32,40... | collective-permute-start | bytes 405512 | tf_op jit(solution)/shard_map/ppermute | solution.py:306
  8.3 2.2 %local.1 = (bf16[8,256,256]{2,1,0:T(8,128)(2,1)S(1)}, f32[256,1024]{1,0:T(8,128)S(1)}, bf16[256,1024]{1,0:T(8,128)(2,1)S(1)}, f32[256,1024]{1,0:T(8,128)S(1)}, f32[1,1024]{1,0:T(1,128)S(1)}) custom-call(s32[1,256]{1,0:T(1,128)S(1)} %get-tuple-element.50.refs_0_, bf16[256,512]{1,0:T(8,128)(2,1)S(1)} %get-tuple-element.52.refs_1_.refs_4_.refs_10_, ...), custom_call_target="tpu_custom_call" | custom-call | tf_op jit(solution)/shard_map/local/pallas_call | solution.py:286
  10.5 6.1 %collective-permute-done.1.refs_1_ = f32[264,128]{1,0:T(8,128)S(1)} collective-permute-done((f32[264,128]{1,0:T(8,128)S(1)}, f32[264,128]{1,0:T(8,128)S(1)}, u32[]{:S(2)}, u32[]{:S(2)}) %collective-permute-start.1) | collective-permute-done | bytes 135200 | tf_op jit(solution)/shard_map/ppermute | solution.py:306
  16.6 0.1 collective-permute-start.2
  16.7 2.8 %collective-permute-done.4.refs_1_ = f32[264,128]{1,0:T(8,128)S(1)} collective-permute-done((f32[264,128]{1,0:T(8,128)S(1)}, f32[264,128]{1,0:T(8,128)S(1)}, u32[]{:S(2)}, u32[]{:S(2)}) %collective-permute-start.4) | collective-permute-done | bytes 135200 | tf_op jit(solution)/shard_map/ppermute | solution.py:306
  19.5 0.1 collective-permute-start.5
  19.6 4.3 %collective-permute-done.2.refs_0_ = f32[264,128]{1,0:T(8,128)S(1)} collective-permute-done((f32[264,128]{1,0:T(8,128)S(1)}, f32[264,128]{1,0:T(8,128)S(1)}, u32[]{:S(2)}, u32[]{:S(2)}) %collective-permute-start.2) | collective-permute-done | bytes 135200 | tf_op jit(solution)/shard_map/ppermute | solution.py:306
  23.9 2.5 %collective-permute-start.3 = (f32[264,128]{1,0:T(8,128)S(1)}, f32[264,128]{1,0:T(8,128)S(1)}, u32[]{:S(2)}, u32[]{:S(2)}) collective-permute-start(f32[264,128]{1,0:T(8,128)S(1)} %get-tuple-element.65), channel_id=1, source_target_pairs={{0,4},{4,0},{8,12},{12,8},{16,20},{20,16},{24,28},{28,24},{32,36},... | collective-permute-start | bytes 405512 | tf_op jit(solution)/shard_map/ppermute | solution.py:303
  26.4 1.2 %collective-permute-done.5.refs_0_ = f32[264,128]{1,0:T(8,128)S(1)} collective-permute-done((f32[264,128]{1,0:T(8,128)S(1)}, f32[264,128]{1,0:T(8,128)S(1)}, u32[]{:S(2)}, u32[]{:S(2)}) %collective-permute-start.5) | collective-permute-done | bytes 135200 | tf_op jit(solution)/shard_map/ppermute | solution.py:306
  27.6 1.6 %collective-permute-start.6 = (f32[264,128]{1,0:T(8,128)S(1)}, f32[264,128]{1,0:T(8,128)S(1)}, u32[]{:S(2)}, u32[]{:S(2)}) collective-permute-start(f32[264,128]{1,0:T(8,128)S(1)} %get-tuple-element.69), channel_id=1, source_target_pairs={{0,4},{4,0},{8,12},{12,8},{16,20},{20,16},{24,28},{28,24},{32,36},... | collective-permute-start | bytes 405512 | tf_op jit(solution)/shard_map/ppermute | solution.py:303
  29.2 0.0 collective-permute-done.3.refs_5_
  29.2 0.8 %attend.2 = (bf16[256,256]{1,0:T(8,128)(2,1)S(1)}, bf16[256,256]{1,0:T(8,128)(2,1)S(1)}, bf16[256,256]{1,0:T(8,128)(2,1)S(1)}, bf16[256,128]{1,0:T(8,128)(2,1)S(...) custom-call(s32[1,256]{1,0:T(1,128)S(1)} %get-tuple-element.50.refs_0_, ...), custom_call_target="tpu_custom_call" | custom-call | tf_op jit(solution)/shard_map/attend/pallas_call | solution.py:286
  29.9 0.2 collective-permute-done.6.refs_4_
  30.2 0.6 attend.3
  30.7 1.3 %collective-permute-start.7 = (f32[8,256]{1,0:T(8,128)S(1)}, f32[8,256]{1,0:T(8,128)S(1)}, u32[]{:S(2)}, u32[]{:S(2)}) collective-permute-start(f32[8,256]{1,0:T(8,128)S(1)} %get-tuple-element.71.refs_5_.refs_18_), channel_id=1, source_target_pairs={{0,1},{1,0},{2,3},{3,2},{4,5},{5,4},{6,7},{7,6},{8,9},{9,8},{10,11... | collective-permute-start | bytes 24584 | tf_op jit(solution)/shard_map/ppermute | solution.py:389
  32.1 2.6 %collective-permute-start.8 = (f32[8,256]{1,0:T(8,128)S(1)}, f32[8,256]{1,0:T(8,128)S(1)}, u32[]{:S(2)}, u32[]{:S(2)}) collective-permute-start(f32[8,256]{1,0:T(8,128)S(1)} %get-tuple-element.71.refs_5_.refs_18_), channel_id=1, source_target_pairs={{0,2},{1,3},{2,0},{3,1},{4,6},{5,7},{6,4},{7,5},{8,10},{9,11},{10,... | collective-permute-start | bytes 24584 | tf_op jit(solution)/shard_map/ppermute | solution.py:389
  34.7 0.0 collective-permute-start.9
  34.7 0.0 collective-permute-done.7.refs_6_.refs_19_
  34.7 1.4 %collective-permute-done.8.refs_7_.refs_20_ = f32[8,256]{1,0:T(8,128)S(1)} collective-permute-done((f32[8,256]{1,0:T(8,128)S(1)}, f32[8,256]{1,0:T(8,128)S(1)}, u32[]{:S(2)}, u32[]{:S(2)}) %collective-permute-start.8) | collective-permute-done | bytes 8224 | tf_op jit(solution)/shard_map/ppermute | solution.py:389
  36.1 2.3 %collective-permute-done.9.refs_8_.refs_21_ = f32[8,256]{1,0:T(8,128)S(1)} collective-permute-done((f32[8,256]{1,0:T(8,128)S(1)}, f32[8,256]{1,0:T(8,128)S(1)}, u32[]{:S(2)}, u32[]{:S(2)}) %collective-permute-start.9) | collective-permute-done | bytes 8224 | tf_op jit(solution)/shard_map/ppermute | solution.py:389
  38.4 0.4 grad.2
  38.8 2.2 %collective-permute-start.10 = (f32[520,128]{1,0:T(8,128)S(1)}, f32[520,128]{1,0:T(8,128)S(1)}, u32[]{:S(2)}, u32[]{:S(2)}) collective-permute-start(f32[520,128]{1,0:T(8,128)S(1)} %get-tuple-element.74.refs_9_), channel_id=1, source_target_pairs={{0,4},{4,0},{8,12},{12,8},{16,20},{20,16},{24,28},{28,24},{32,36},... | collective-permute-start | bytes 798728 | tf_op jit(solution)/shard_map/ppermute | solution.py:303
  41.0 0.4 grad.3
  41.4 0.7 %collective-permute-done.10.refs_1_.refs_2_ = f32[520,128]{1,0:T(8,128)S(1)} collective-permute-done((f32[520,128]{1,0:T(8,128)S(1)}, f32[520,128]{1,0:T(8,128)S(1)}, u32[]{:S(2)}, u32[]{:S(2)}) %collective-permute-start.10) | collective-permute-done | bytes 266272 | tf_op jit(solution)/shard_map/ppermute | solution.py:303
  42.2 0.1 collective-permute-start.14
  42.3 0.3 collective-permute-start.11
  42.6 3.7 %back.1 = (bf16[256,1024]{1,0:T(8,128)(2,1)}, bf16[256,1024]{1,0:T(8,128)(2,1)}, f32[256,1024]{1,0:T(8,128)S(1)}, f32[256,1024]{1,0:T(8,128)S(1)}) custom-call(s32[1,256]{1,0:T(1,128)S(1)} %get-tuple-element.50.refs_0_, bf16[256,1024]{1,0:T(8,128)(2,1)S(1)} %get-tuple-element.58.refs_1_, bf16[8,256,256]{2,1,0:T(8,128)(2,1)S(1)} %get-tuple-element.59.refs_2_, ...), custom_call_target="tpu_custom_call" | custom-call | tf_op jit(solution)/shard_map/back/pallas_call | solution.py:286
  46.3 0.8 %collective-permute-done.14.refs_1_ = f32[264,128]{1,0:T(8,128)S(1)} collective-permute-done((f32[264,128]{1,0:T(8,128)S(1)}, f32[264,128]{1,0:T(8,128)S(1)}, u32[]{:S(2)}, u32[]{:S(2)}) %collective-permute-start.14) | collective-permute-done | bytes 135200 | tf_op jit(solution)/shard_map/ppermute | solution.py:306
  47.1 3.7 %collective-permute-start.15 = (f32[264,128]{1,0:T(8,128)S(1)}, f32[264,128]{1,0:T(8,128)S(1)}, u32[]{:S(2)}, u32[]{:S(2)}) collective-permute-start(f32[264,128]{1,0:T(8,128)S(1)} %merge.7), channel_id=1, source_target_pairs={{0,248},{4,252},{8,0},{12,4},{16,8},{20,12},{24,16},{28,20},{32,24... | collective-permute-start | bytes 405512 | tf_op jit(solution)/shard_map/ppermute | solution.py:306
  50.8 0.0 collective-permute-done.11.refs_1_
  50.8 2.9 %collective-permute-start.12 = (f32[264,128]{1,0:T(8,128)S(1)}, f32[264,128]{1,0:T(8,128)S(1)}, u32[]{:S(2)}, u32[]{:S(2)}) collective-permute-start(f32[264,128]{1,0:T(8,128)S(1)} %merge.6), channel_id=1, source_target_pairs={{0,248},{4,252},{8,0},{12,4},{16,8},{20,12},{24,16},{28,20},{32,24... | collective-permute-start | bytes 405512 | tf_op jit(solution)/shard_map/ppermute | solution.py:306
  53.7 0.0 collective-permute-done.15.refs_0_
  53.7 2.0 %collective-permute-start.16 = (f32[264,128]{1,0:T(8,128)S(1)}, f32[264,128]{1,0:T(8,128)S(1)}, u32[]{:S(2)}, u32[]{:S(2)}) collective-permute-start(f32[264,128]{1,0:T(8,128)S(1)} %get-tuple-element.90), channel_id=1, source_target_pairs={{0,4},{4,0},{8,12},{12,8},{16,20},{20,16},{24,28},{28,24},{32,36},... | collective-permute-start | bytes 405512 | tf_op jit(solution)/shard_map/ppermute | solution.py:303
  55.7 1.0 %collective-permute-done.12.refs_0_ = f32[264,128]{1,0:T(8,128)S(1)} collective-permute-done((f32[264,128]{1,0:T(8,128)S(1)}, f32[264,128]{1,0:T(8,128)S(1)}, u32[]{:S(2)}, u32[]{:S(2)}) %collective-permute-start.12) | collective-permute-done | bytes 135200 | tf_op jit(solution)/shard_map/ppermute | solution.py:306
  56.7 1.4 %collective-permute-start.13 = (f32[264,128]{1,0:T(8,128)S(1)}, f32[264,128]{1,0:T(8,128)S(1)}, u32[]{:S(2)}, u32[]{:S(2)}) collective-permute-start(f32[264,128]{1,0:T(8,128)S(1)} %get-tuple-element.87), channel_id=1, source_target_pairs={{0,4},{4,0},{8,12},{12,8},{16,20},{20,16},{24,28},{28,24},{32,36},... | collective-permute-start | bytes 405512 | tf_op jit(solution)/shard_map/ppermute | solution.py:303
  58.1 0.0 collective-permute-done.16.refs_6_
  58.1 1.2 %last.2 = (bf16[256,1024]{1,0:T(8,128)(2,1)}, bf16[256,1024]{1,0:T(8,128)(2,1)}) custom-call(s32[1,256]{1,0:T(1,128)S(1)} %get-tuple-element.50.refs_0_, f32[256,1024]{1,0:T(8,128)S(1)} %get-tuple-element.85.refs_2_.refs_1_, f32[256,1024]{1,0:T(8,128)S(1)} %get-tuple-element.86.refs_2_, f32[264,128]{1,0:T(8,128)S(1)} %get-tuple-element.89.refs_3_, ...), custom_call_target="tpu_custom_call" | custom-call | tf_op jit(solution)/shard_map/last/pallas_call | solution.py:286
  59.3 0.0 collective-permute-done.13.refs_3_
  59.4 1.0 %last.3 = (bf16[256,1024]{1,0:T(8,128)(2,1)}, bf16[256,1024]{1,0:T(8,128)(2,1)}) custom-call(s32[1,256]{1,0:T(1,128)S(1)} %get-tuple-element.50.refs_0_, f32[256,1024]{1,0:T(8,128)S(1)} %get-tuple-element.85.refs_2_.refs_1_, f32[256,1024]{1,0:T(8,128)S(1)} %get-tuple-element.86.refs_2_, ...), custom_call_target="tpu_custom_call", output_to_operand_aliasing={{0}: (6, {}), {1}: (7, {})} | custom-call | tf_op jit(solution)/shard_map/last/pallas_call | solution.py:286
  (9 shorter events, 0.2 us)
Async XLA Ops:
  2.0 4.6 %collective-permute-start = (f32[520,128]{1,0:T(8,128)S(1)}, f32[520,128]{1,0:T(8,128)S(1)}, u32[]{:S(2)}, u32[]{:S(2)}) collective-permute-start(f32[520,128]{1,0:T(8,128)S(1)} %get-tuple-element.51.refs_3_), channel_id=1, source_target_pairs={{0,4},{4,0},{8,12},{12,8},{16,20},{20,16},{24,28},{28,24},{32,36},... | collective-permute-start | bytes 798728 | tf_op jit(solution)/shard_map/ppermute | solution.py:303
  6.7 9.9 %collective-permute-start.1 = (f32[264,128]{1,0:T(8,128)S(1)}, f32[264,128]{1,0:T(8,128)S(1)}, u32[]{:S(2)}, u32[]{:S(2)}) collective-permute-start(f32[264,128]{1,0:T(8,128)S(1)} %get-tuple-element.63.refs_0_), channel_id=1, source_target_pairs={{0,8},{4,12},{8,16},{12,20},{16,24},{20,28},{24,32},{28,36},{32,40... | collective-permute-start | bytes 405512 | tf_op jit(solution)/shard_map/ppermute | solution.py:306
  6.8 12.7 %collective-permute-start.4 = (f32[264,128]{1,0:T(8,128)S(1)}, f32[264,128]{1,0:T(8,128)S(1)}, u32[]{:S(2)}, u32[]{:S(2)}) collective-permute-start(f32[264,128]{1,0:T(8,128)S(1)} %get-tuple-element.57.refs_8_.refs_0_), channel_id=1, source_target_pairs={{0,8},{4,12},{8,16},{12,20},{16,24},{20,28},{24,32},{28,36},{32,40... | collective-permute-start | bytes 405512 | tf_op jit(solution)/shard_map/ppermute | solution.py:306
  16.6 7.3 %collective-permute-start.2 = (f32[264,128]{1,0:T(8,128)S(1)}, f32[264,128]{1,0:T(8,128)S(1)}, u32[]{:S(2)}, u32[]{:S(2)}) collective-permute-start(f32[264,128]{1,0:T(8,128)S(1)} %merge.4), channel_id=1, source_target_pairs={{0,8},{4,12},{8,16},{12,20},{16,24},{20,28},{24,32},{28,36},{32,40... | collective-permute-start | bytes 405512 | tf_op jit(solution)/shard_map/ppermute | solution.py:306
  19.5 8.0 %collective-permute-start.5 = (f32[264,128]{1,0:T(8,128)S(1)}, f32[264,128]{1,0:T(8,128)S(1)}, u32[]{:S(2)}, u32[]{:S(2)}) collective-permute-start(f32[264,128]{1,0:T(8,128)S(1)} %merge.5), channel_id=1, source_target_pairs={{0,8},{4,12},{8,16},{12,20},{16,24},{20,28},{24,32},{28,36},{32,40... | collective-permute-start | bytes 405512 | tf_op jit(solution)/shard_map/ppermute | solution.py:306
  23.9 5.2 %collective-permute-start.3 = (f32[264,128]{1,0:T(8,128)S(1)}, f32[264,128]{1,0:T(8,128)S(1)}, u32[]{:S(2)}, u32[]{:S(2)}) collective-permute-start(f32[264,128]{1,0:T(8,128)S(1)} %get-tuple-element.65), channel_id=1, source_target_pairs={{0,4},{4,0},{8,12},{12,8},{16,20},{20,16},{24,28},{28,24},{32,36},... | collective-permute-start | bytes 405512 | tf_op jit(solution)/shard_map/ppermute | solution.py:303
  27.6 2.6 %collective-permute-start.6 = (f32[264,128]{1,0:T(8,128)S(1)}, f32[264,128]{1,0:T(8,128)S(1)}, u32[]{:S(2)}, u32[]{:S(2)}) collective-permute-start(f32[264,128]{1,0:T(8,128)S(1)} %get-tuple-element.69), channel_id=1, source_target_pairs={{0,4},{4,0},{8,12},{12,8},{16,20},{20,16},{24,28},{28,24},{32,36},... | collective-permute-start | bytes 405512 | tf_op jit(solution)/shard_map/ppermute | solution.py:303
  30.7 4.0 %collective-permute-start.7 = (f32[8,256]{1,0:T(8,128)S(1)}, f32[8,256]{1,0:T(8,128)S(1)}, u32[]{:S(2)}, u32[]{:S(2)}) collective-permute-start(f32[8,256]{1,0:T(8,128)S(1)} %get-tuple-element.71.refs_5_.refs_18_), channel_id=1, source_target_pairs={{0,1},{1,0},{2,3},{3,2},{4,5},{5,4},{6,7},{7,6},{8,9},{9,8},{10,11... | collective-permute-start | bytes 24584 | tf_op jit(solution)/shard_map/ppermute | solution.py:389
  32.1 4.0 %collective-permute-start.8 = (f32[8,256]{1,0:T(8,128)S(1)}, f32[8,256]{1,0:T(8,128)S(1)}, u32[]{:S(2)}, u32[]{:S(2)}) collective-permute-start(f32[8,256]{1,0:T(8,128)S(1)} %get-tuple-element.71.refs_5_.refs_18_), channel_id=1, source_target_pairs={{0,2},{1,3},{2,0},{3,1},{4,6},{5,7},{6,4},{7,5},{8,10},{9,11},{10,... | collective-permute-start | bytes 24584 | tf_op jit(solution)/shard_map/ppermute | solution.py:389
  34.7 3.7 %collective-permute-start.9 = (f32[8,256]{1,0:T(8,128)S(1)}, f32[8,256]{1,0:T(8,128)S(1)}, u32[]{:S(2)}, u32[]{:S(2)}) collective-permute-start(f32[8,256]{1,0:T(8,128)S(1)} %get-tuple-element.71.refs_5_.refs_18_), channel_id=1, source_target_pairs={{0,3},{1,2},{2,1},{3,0},{4,7},{5,6},{6,5},{7,4},{8,11},{9,10},{10,... | collective-permute-start | bytes 24584 | tf_op jit(solution)/shard_map/ppermute | solution.py:389
  38.8 3.3 %collective-permute-start.10 = (f32[520,128]{1,0:T(8,128)S(1)}, f32[520,128]{1,0:T(8,128)S(1)}, u32[]{:S(2)}, u32[]{:S(2)}) collective-permute-start(f32[520,128]{1,0:T(8,128)S(1)} %get-tuple-element.74.refs_9_), channel_id=1, source_target_pairs={{0,4},{4,0},{8,12},{12,8},{16,20},{20,16},{24,28},{28,24},{32,36},... | collective-permute-start | bytes 798728 | tf_op jit(solution)/shard_map/ppermute | solution.py:303
  42.2 4.8 %collective-permute-start.14 = (f32[264,128]{1,0:T(8,128)S(1)}, f32[264,128]{1,0:T(8,128)S(1)}, u32[]{:S(2)}, u32[]{:S(2)}) collective-permute-start(f32[264,128]{1,0:T(8,128)S(1)} %get-tuple-element.88.refs_0_), channel_id=1, source_target_pairs={{0,248},{4,252},{8,0},{12,4},{16,8},{20,12},{24,16},{28,20},{32,24... | collective-permute-start | bytes 405512 | tf_op jit(solution)/shard_map/ppermute | solution.py:306
  42.3 8.5 %collective-permute-start.11 = (f32[264,128]{1,0:T(8,128)S(1)}, f32[264,128]{1,0:T(8,128)S(1)}, u32[]{:S(2)}, u32[]{:S(2)}) collective-permute-start(f32[264,128]{1,0:T(8,128)S(1)} %get-tuple-element.82.refs_22_.refs_0_), channel_id=1, source_target_pairs={{0,248},{4,252},{8,0},{12,4},{16,8},{20,12},{24,16},{28,20},{32,24... | collective-permute-start | bytes 405512 | tf_op jit(solution)/shard_map/ppermute | solution.py:306
  47.1 6.6 %collective-permute-start.15 = (f32[264,128]{1,0:T(8,128)S(1)}, f32[264,128]{1,0:T(8,128)S(1)}, u32[]{:S(2)}, u32[]{:S(2)}) collective-permute-start(f32[264,128]{1,0:T(8,128)S(1)} %merge.7), channel_id=1, source_target_pairs={{0,248},{4,252},{8,0},{12,4},{16,8},{20,12},{24,16},{28,20},{32,24... | collective-permute-start | bytes 405512 | tf_op jit(solution)/shard_map/ppermute | solution.py:306
  50.8 5.9 %collective-permute-start.12 = (f32[264,128]{1,0:T(8,128)S(1)}, f32[264,128]{1,0:T(8,128)S(1)}, u32[]{:S(2)}, u32[]{:S(2)}) collective-permute-start(f32[264,128]{1,0:T(8,128)S(1)} %merge.6), channel_id=1, source_target_pairs={{0,248},{4,252},{8,0},{12,4},{16,8},{20,12},{24,16},{28,20},{32,24... | collective-permute-start | bytes 405512 | tf_op jit(solution)/shard_map/ppermute | solution.py:306
  53.7 4.4 %collective-permute-start.16 = (f32[264,128]{1,0:T(8,128)S(1)}, f32[264,128]{1,0:T(8,128)S(1)}, u32[]{:S(2)}, u32[]{:S(2)}) collective-permute-start(f32[264,128]{1,0:T(8,128)S(1)} %get-tuple-element.90), channel_id=1, source_target_pairs={{0,4},{4,0},{8,12},{12,8},{16,20},{20,16},{24,28},{28,24},{32,36},... | collective-permute-start | bytes 405512 | tf_op jit(solution)/shard_map/ppermute | solution.py:303
  56.7 2.6 %collective-permute-start.13 = (f32[264,128]{1,0:T(8,128)S(1)}, f32[264,128]{1,0:T(8,128)S(1)}, u32[]{:S(2)}, u32[]{:S(2)}) collective-permute-start(f32[264,128]{1,0:T(8,128)S(1)} %get-tuple-element.87), channel_id=1, source_target_pairs={{0,4},{4,0},{8,12},{12,8},{16,20},{20,16},{24,28},{28,24},{32,36},... | collective-permute-start | bytes 405512 | tf_op jit(solution)/shard_map/ppermute | solution.py:303

commit v10 on v6

--- a/solution.py
+++ b/solution.py
@@ -195,7 +195,7 @@
 
 
 def grad_kernel(half, chunks, ranks, row, q, weighted, *rest):
-    g_out, out = rest[-2:]
+    *_, g_out, out = rest if half else rest[:-1]
     rows, width = g_out.shape
     each = width // HD // chunks
     keep = in_doc(row, 0).astype(BF16)
@@ -207,39 +207,48 @@
         g_out[:, head(h)] = g
         out[head(h), :] = dot(q[:, at] * keep, g, TN)
     out[width:, :] = jnp.broadcast_to(tag(row, 0), (TAG, HD))
-
-
-def back_kernel(chunks, ranks, row, q, scores, gain, k0, k1, v0, v1, g0, g1, *rest):
-    attended, carried, rest = rest[:2 * chunks], rest[2 * chunks:4 * chunks], rest[4 * chunks:]
-    normed_hbm, grad_q_hbm, part_k, part_v, normed, grad_q, sems = rest[-7:]
+    if not half:
+        normed = rest[-1]
+        pieces = (*rest[:chunks], *rest[chunks + ranks:2 * chunks + ranks])
+        gain = rest[2 * chunks + ranks]
+        for h in range(2 * width // HD):
+            att = pieces[h // each][:, head(h % each)].astype(F32)
+            normed[:, head(h)] = (gain[:, head(h)] * att * inv).astype(BF16)
+
+
+def back_kernel(chunks, row, q, scores, normed, k0, k1, v0, v1, g0, g1, *rest):
+    carried = rest[:2 * chunks]
+    normed_hbm, grad_q_hbm, part_k, part_v, grad_q, sems = rest[-6:]
     rows, width = k0.shape
-    inv, _ = norm_scales(rest[:ranks])
     keep = in_doc(row, 0)
     seen = visible(row)
     n = width // HD
     copies = []
+
+    def send(half, i, held, out):
+        span = slice(half * width, (half + 1) * width)
+        copies.append(
+            pltpu.make_async_copy(
+                held.at[:, span], out.at[:, columns(half, width)], sems.at[2 * half + i]
+            )
+        )
+        copies[-1].start()
+
+    send(0, 0, normed, normed_hbm)
+    send(1, 0, normed, normed_hbm)
     each = n // chunks
     for half, (k, v, g) in enumerate(((k0, v0, g0), (k1, v1, g1))):
         for h in range(n):
             at = head(half * n + h)
             gh = g[:, head(h)]
-            att = attended[half * chunks + h // each][:, head(h % each)].astype(F32)
             state = carried[half * chunks + h // each][head(h % each), :]
-            normed[:, at] = (gain[:, at] * att * inv).astype(BF16)
             gs = dot(gh, v[:, head(h)], NT)
             gs = jnp.where(seen, gs, 0.0).astype(BF16)
             whole = dot(gs, k[:, head(h)], NN) + keep * dot(gh, state, NT)
             grad_q[:, at] = whole.astype(BF16)
             part_k[:, at] = dot(gs, q[:, at], TN)
             part_v[:, at] = dot(scores[half * n + h], gh, TN)
-        span = slice(half * width, (half + 1) * width)
-        for i, (held, out) in enumerate(((normed, normed_hbm), (grad_q, grad_q_hbm))):
-            copies.append(
-                pltpu.make_async_copy(
-                    held.at[:, span], out.at[:, columns(half, width)], sems.at[2 * half + i]
-                )
-            )
-            copies[-1].start()
+        send(half, 1, grad_q, grad_q_hbm)
     for copy in copies:
         copy.wait()
 
@@ -391,20 +400,24 @@
     ]
 
     def make_grad(which, after=()):
-        held["g", which], out = call(
-            grad_kernel, [which, CHUNKS, ranks], [half, state],
-            [held["row"], q, weighted, *(attended[which, i] for i in range(CHUNKS)), *stats],
-            after=after,
-        )
+        pieces = [[attended[w, i] for i in range(CHUNKS)] for w in range(2)]
+        extra = [] if which else [*pieces[1], gain]
+        held["g", which], out, *normed = call(
+            grad_kernel, [which, CHUNKS, ranks],
+            [half, state] + [((rows, width), BF16)] * (1 - which),
+            [held["row"], q, weighted, *pieces[which], *stats, *extra], after=after,
+        )
+        if not which:
+            (held["normed"],) = normed
         return out
 
     def back_work(token):
         out = call(
-            back_kernel, [CHUNKS, ranks], [((rows, width), BF16, HBM)] * 2 + [wide, wide],
-            [held["row"], q, scores, gain, *k, *v, held["g", 0], held["g", 1],
-             *(attended[x] for x in order), *(carried[x] for x in order), *stats],
+            back_kernel, [CHUNKS], [((rows, width), BF16, HBM)] * 2 + [wide, wide],
+            [held["row"], q, scores, held["normed"], *k, *v, held["g", 0], held["g", 1],
+             *(carried[x] for x in order)],
             after=[token],
-            scratch=[VMEM((rows, width), BF16), VMEM((rows, width), BF16), DMA((4,))],
+            scratch=[VMEM((rows, width), BF16), DMA((4,))],
         )
         return out, out[2]
 

time: 59.4 us -> 59.4 us (level)
  transfers between devices with their start and end apart: 17 -> 17, of which waited for: 10 -> 10; matrix products, arithmetic and copies ran while one was open for 0% -> 0% of each run, Pallas kernels for 17% -> 16%
where the time goes in v10:
time: 59.4 us; the launch traced here: 59.3 us
  starting transfers between devices  26.3 us (44%)
  waiting for transfers between devices  19 us (32%)
  Pallas kernels  13 us (22%)
  between operations  0.95 us (2%)
    ppermute x8, waiting for transfers between devices, hop(): lax.ppermute(value, 'ctx', [(i, (i + step) % blocks) for i in range(block...  16.5 us
    pallas_call x20, Pallas kernels, call(): pl.pallas_call(lambda *refs: kernel(*fixed, *refs), out_shape=[jax.ShapeD...  13 us
    ppermute x6, starting transfers between devices, swap(): return lax.ppermute(value, 'ctx', [(i, i ^ 1) for i in range(blocks)])  12.6 us
    ppermute x8, starting transfers between devices, hop(): lax.ppermute(value, 'ctx', [(i, (i + step) % blocks) for i in range(block...  8.7 us
    ppermute x3, starting transfers between devices, local(): lax.ppermute(stats[0], 'head', [(i, (i + apart) % ranks) for i in range(r...  5.01 us
    ppermute x3, waiting for transfers between devices, local(): lax.ppermute(stats[0], 'head', [(i, (i + apart) % ranks) for i in range(r...  1.72 us
  transfers between devices with their start and end apart: 17, of which 10 were waited for; matrix products, arithmetic and copies ran while one was open for 0% of the time, Pallas kernels for 16%

profile of v10, /device:TPU:1, one launch (start us, length us, event | category | flops | bytes accessed | tf_op | source)
XLA Modules:
  0.0 59.3 jit_solution(11563201822778109577)
XLA Ops:
  0.6 1.3 %state.2 = (f32[520,128]{1,0:T(8,128)S(1)}, bf16[256,512]{1,0:T(8,128)(2,1)S(1)}, bf16[256,512]{1,0:T(8,128)(2,1)S(1)}, s32[1,256]{1,0:T(1,128)S(1)}) custom-call(s32[1,256]{1,0:T(1,128)} %bitcast.3, bf16[256,1024]{1,0:T(8,128)(2,1)} %refs_1_.3, bf16[256,1024]{1,0:T(8,128)(2,1)} %refs_2_.3), custom_call_target="tpu_custom_call" | custom-call | tf_op jit(solution)/shard_map/state/pallas_call | solution.py:295
  2.0 3.3 %collective-permute-start = (f32[520,128]{1,0:T(8,128)S(1)}, f32[520,128]{1,0:T(8,128)S(1)}, u32[]{:S(2)}, u32[]{:S(2)}) collective-permute-start(f32[520,128]{1,0:T(8,128)S(1)} %get-tuple-element.52.refs_3_), channel_id=1, source_target_pairs={{0,4},{4,0},{8,12},{12,8},{16,20},{20,16},{24,28},{28,24},{32,36},... | collective-permute-start | bytes 798728 | tf_op jit(solution)/shard_map/ppermute | solution.py:312
  5.3 1.3 %state.3 = (f32[520,128]{1,0:T(8,128)S(1)}, bf16[256,512]{1,0:T(8,128)(2,1)S(1)}, bf16[256,512]{1,0:T(8,128)(2,1)S(1)}) custom-call(s32[1,256]{1,0:T(1,128)S(1)} %get-tuple-element.51.refs_0_, bf16[256,1024]{1,0:T(8,128)(2,1)} %refs_1_.3, bf16[256,1024]{1,0:T(8,128)(2,1)} %refs_2_.3, f32[520,128]{1,0:T(8,128)S(1)} %get-tuple-element.52.refs_3_), custom_call_target="tpu_custom_call" | custom-call | tf_op jit(solution)/shard_map/state/pallas_call | solution.py:295
  6.6 0.0 collective-permute-done.refs_1_.refs_2_
  6.6 0.1 pair.2
  6.7 0.1 collective-permute-start.1
  6.8 1.6 %collective-permute-start.4 = (f32[264,128]{1,0:T(8,128)S(1)}, f32[264,128]{1,0:T(8,128)S(1)}, u32[]{:S(2)}, u32[]{:S(2)}) collective-permute-start(f32[264,128]{1,0:T(8,128)S(1)} %get-tuple-element.58.refs_8_.refs_0_), channel_id=1, source_target_pairs={{0,8},{4,12},{8,16},{12,20},{16,24},{20,28},{24,32},{28,36},{32,40... | collective-permute-start | bytes 405512 | tf_op jit(solution)/shard_map/ppermute | solution.py:315
  8.3 2.2 %local.1 = (bf16[8,256,256]{2,1,0:T(8,128)(2,1)S(1)}, f32[256,1024]{1,0:T(8,128)S(1)}, bf16[256,1024]{1,0:T(8,128)(2,1)S(1)}, f32[256,1024]{1,0:T(8,128)S(1)}, f32[1,1024]{1,0:T(1,128)S(1)}) custom-call(s32[1,256]{1,0:T(1,128)S(1)} %get-tuple-element.51.refs_0_, bf16[256,512]{1,0:T(8,128)(2,1)S(1)} %get-tuple-element.53.refs_1_.refs_4_.refs_10_, ...), custom_call_target="tpu_custom_call" | custom-call | tf_op jit(solution)/shard_map/local/pallas_call | solution.py:295
  10.5 6.1 %collective-permute-done.1.refs_1_ = f32[264,128]{1,0:T(8,128)S(1)} collective-permute-done((f32[264,128]{1,0:T(8,128)S(1)}, f32[264,128]{1,0:T(8,128)S(1)}, u32[]{:S(2)}, u32[]{:S(2)}) %collective-permute-start.1) | collective-permute-done | bytes 135200 | tf_op jit(solution)/shard_map/ppermute | solution.py:315
  16.7 0.1 collective-permute-start.2
  16.7 2.8 %collective-permute-done.4.refs_1_ = f32[264,128]{1,0:T(8,128)S(1)} collective-permute-done((f32[264,128]{1,0:T(8,128)S(1)}, f32[264,128]{1,0:T(8,128)S(1)}, u32[]{:S(2)}, u32[]{:S(2)}) %collective-permute-start.4) | collective-permute-done | bytes 135200 | tf_op jit(solution)/shard_map/ppermute | solution.py:315
  19.6 0.1 collective-permute-start.5
  19.6 4.3 %collective-permute-done.2.refs_0_ = f32[264,128]{1,0:T(8,128)S(1)} collective-permute-done((f32[264,128]{1,0:T(8,128)S(1)}, f32[264,128]{1,0:T(8,128)S(1)}, u32[]{:S(2)}, u32[]{:S(2)}) %collective-permute-start.2) | collective-permute-done | bytes 135200 | tf_op jit(solution)/shard_map/ppermute | solution.py:315
  23.9 2.4 %collective-permute-start.3 = (f32[264,128]{1,0:T(8,128)S(1)}, f32[264,128]{1,0:T(8,128)S(1)}, u32[]{:S(2)}, u32[]{:S(2)}) collective-permute-start(f32[264,128]{1,0:T(8,128)S(1)} %get-tuple-element.65), channel_id=1, source_target_pairs={{0,4},{4,0},{8,12},{12,8},{16,20},{20,16},{24,28},{28,24},{32,36},... | collective-permute-start | bytes 405512 | tf_op jit(solution)/shard_map/ppermute | solution.py:312
  26.4 1.2 %collective-permute-done.5.refs_0_ = f32[264,128]{1,0:T(8,128)S(1)} collective-permute-done((f32[264,128]{1,0:T(8,128)S(1)}, f32[264,128]{1,0:T(8,128)S(1)}, u32[]{:S(2)}, u32[]{:S(2)}) %collective-permute-start.5) | collective-permute-done | bytes 135200 | tf_op jit(solution)/shard_map/ppermute | solution.py:315
  27.6 1.6 %collective-permute-start.6 = (f32[264,128]{1,0:T(8,128)S(1)}, f32[264,128]{1,0:T(8,128)S(1)}, u32[]{:S(2)}, u32[]{:S(2)}) collective-permute-start(f32[264,128]{1,0:T(8,128)S(1)} %get-tuple-element.69), channel_id=1, source_target_pairs={{0,4},{4,0},{8,12},{12,8},{16,20},{20,16},{24,28},{28,24},{32,36},... | collective-permute-start | bytes 405512 | tf_op jit(solution)/shard_map/ppermute | solution.py:312
  29.2 0.0 collective-permute-done.3.refs_5_
  29.2 0.8 %attend.2 = (bf16[256,256]{1,0:T(8,128)(2,1)S(1)}, bf16[256,256]{1,0:T(8,128)(2,1)S(1)}, bf16[256,256]{1,0:T(8,128)(2,1)S(1)}, bf16[256,128]{1,0:T(8,128)(2,1)S(...) custom-call(s32[1,256]{1,0:T(1,128)S(1)} %get-tuple-element.51.refs_0_, ...), custom_call_target="tpu_custom_call" | custom-call | tf_op jit(solution)/shard_map/attend/pallas_call | solution.py:295
  29.9 0.2 collective-permute-done.6.refs_4_
  30.2 0.6 attend.3
  30.7 1.3 %collective-permute-start.7 = (f32[8,256]{1,0:T(8,128)S(1)}, f32[8,256]{1,0:T(8,128)S(1)}, u32[]{:S(2)}, u32[]{:S(2)}) collective-permute-start(f32[8,256]{1,0:T(8,128)S(1)} %get-tuple-element.71.refs_5_), channel_id=1, source_target_pairs={{0,1},{1,2},{2,3},{3,0},{4,5},{5,6},{6,7},{7,4},{8,9},{9,10},{10,1... | collective-permute-start | bytes 24584 | tf_op jit(solution)/shard_map/ppermute | solution.py:398
  32.1 2.6 %collective-permute-start.8 = (f32[8,256]{1,0:T(8,128)S(1)}, f32[8,256]{1,0:T(8,128)S(1)}, u32[]{:S(2)}, u32[]{:S(2)}) collective-permute-start(f32[8,256]{1,0:T(8,128)S(1)} %get-tuple-element.71.refs_5_), channel_id=1, source_target_pairs={{0,2},{1,3},{2,0},{3,1},{4,6},{5,7},{6,4},{7,5},{8,10},{9,11},{10,... | collective-permute-start | bytes 24584 | tf_op jit(solution)/shard_map/ppermute | solution.py:398
  34.7 1.1 %collective-permute-start.9 = (f32[8,256]{1,0:T(8,128)S(1)}, f32[8,256]{1,0:T(8,128)S(1)}, u32[]{:S(2)}, u32[]{:S(2)}) collective-permute-start(f32[8,256]{1,0:T(8,128)S(1)} %get-tuple-element.71.refs_5_), channel_id=1, source_target_pairs={{0,3},{1,0},{2,1},{3,2},{4,7},{5,4},{6,5},{7,6},{8,11},{9,8},{10,9... | collective-permute-start | bytes 24584 | tf_op jit(solution)/shard_map/ppermute | solution.py:398
  35.7 0.0 collective-permute-done.7.refs_6_
  35.7 0.3 collective-permute-done.8.refs_7_
  36.1 1.4 %collective-permute-done.9.refs_8_ = f32[8,256]{1,0:T(8,128)S(1)} collective-permute-done((f32[8,256]{1,0:T(8,128)S(1)}, f32[8,256]{1,0:T(8,128)S(1)}, u32[]{:S(2)}, u32[]{:S(2)}) %collective-permute-start.9) | collective-permute-done | bytes 8224 | tf_op jit(solution)/shard_map/ppermute | solution.py:398
  37.5 0.4 grad.2
  37.9 1.9 %collective-permute-start.10 = (f32[520,128]{1,0:T(8,128)S(1)}, f32[520,128]{1,0:T(8,128)S(1)}, u32[]{:S(2)}, u32[]{:S(2)}) collective-permute-start(f32[520,128]{1,0:T(8,128)S(1)} %get-tuple-element.75.refs_12_), channel_id=1, source_target_pairs={{0,4},{4,0},{8,12},{12,8},{16,20},{20,16},{24,28},{28,24},{32,36},... | collective-permute-start | bytes 798728 | tf_op jit(solution)/shard_map/ppermute | solution.py:312
  39.8 0.5 grad.3
  40.3 0.6 %collective-permute-done.10.refs_1_.refs_2_ = f32[520,128]{1,0:T(8,128)S(1)} collective-permute-done((f32[520,128]{1,0:T(8,128)S(1)}, f32[520,128]{1,0:T(8,128)S(1)}, u32[]{:S(2)}, u32[]{:S(2)}) %collective-permute-start.10) | collective-permute-done | bytes 266272 | tf_op jit(solution)/shard_map/ppermute | solution.py:312
  41.0 0.1 collective-permute-start.14
  41.1 0.3 collective-permute-start.11
  41.3 3.3 %back.1 = (bf16[256,1024]{1,0:T(8,128)(2,1)}, bf16[256,1024]{1,0:T(8,128)(2,1)}, f32[256,1024]{1,0:T(8,128)S(1)}, f32[256,1024]{1,0:T(8,128)S(1)}) custom-call(s32[1,256]{1,0:T(1,128)S(1)} %get-tuple-element.51.refs_0_, bf16[256,1024]{1,0:T(8,128)(2,1)S(1)} %get-tuple-element.59.refs_1_, bf16[8,256,256]{2,1,0:T(8,128)(2,1)S(1)} %get-tuple-element.60.refs_2_, ...), custom_call_target="tpu_custom_call" | custom-call | tf_op jit(solution)/shard_map/back/pallas_call | solution.py:295
  44.7 1.1 %collective-permute-done.14.refs_1_ = f32[264,128]{1,0:T(8,128)S(1)} collective-permute-done((f32[264,128]{1,0:T(8,128)S(1)}, f32[264,128]{1,0:T(8,128)S(1)}, u32[]{:S(2)}, u32[]{:S(2)}) %collective-permute-start.14) | collective-permute-done | bytes 135200 | tf_op jit(solution)/shard_map/ppermute | solution.py:315
  45.8 3.7 %collective-permute-start.15 = (f32[264,128]{1,0:T(8,128)S(1)}, f32[264,128]{1,0:T(8,128)S(1)}, u32[]{:S(2)}, u32[]{:S(2)}) collective-permute-start(f32[264,128]{1,0:T(8,128)S(1)} %merge.7), channel_id=1, source_target_pairs={{0,248},{4,252},{8,0},{12,4},{16,8},{20,12},{24,16},{28,20},{32,24... | collective-permute-start | bytes 405512 | tf_op jit(solution)/shard_map/ppermute | solution.py:315
  49.5 0.0 collective-permute-done.11.refs_1_
  49.6 2.9 %collective-permute-start.12 = (f32[264,128]{1,0:T(8,128)S(1)}, f32[264,128]{1,0:T(8,128)S(1)}, u32[]{:S(2)}, u32[]{:S(2)}) collective-permute-start(f32[264,128]{1,0:T(8,128)S(1)} %merge.6), channel_id=1, source_target_pairs={{0,248},{4,252},{8,0},{12,4},{16,8},{20,12},{24,16},{28,20},{32,24... | collective-permute-start | bytes 405512 | tf_op jit(solution)/shard_map/ppermute | solution.py:315
  52.4 0.0 collective-permute-done.15.refs_0_
  52.5 2.0 %collective-permute-start.16 = (f32[264,128]{1,0:T(8,128)S(1)}, f32[264,128]{1,0:T(8,128)S(1)}, u32[]{:S(2)}, u32[]{:S(2)}) collective-permute-start(f32[264,128]{1,0:T(8,128)S(1)} %get-tuple-element.92), channel_id=1, source_target_pairs={{0,4},{4,0},{8,12},{12,8},{16,20},{20,16},{24,28},{28,24},{32,36},... | collective-permute-start | bytes 405512 | tf_op jit(solution)/shard_map/ppermute | solution.py:312
  54.5 1.0 %collective-permute-done.12.refs_0_ = f32[264,128]{1,0:T(8,128)S(1)} collective-permute-done((f32[264,128]{1,0:T(8,128)S(1)}, f32[264,128]{1,0:T(8,128)S(1)}, u32[]{:S(2)}, u32[]{:S(2)}) %collective-permute-start.12) | collective-permute-done | bytes 135200 | tf_op jit(solution)/shard_map/ppermute | solution.py:315
  55.5 1.4 %collective-permute-start.13 = (f32[264,128]{1,0:T(8,128)S(1)}, f32[264,128]{1,0:T(8,128)S(1)}, u32[]{:S(2)}, u32[]{:S(2)}) collective-permute-start(f32[264,128]{1,0:T(8,128)S(1)} %get-tuple-element.89), channel_id=1, source_target_pairs={{0,4},{4,0},{8,12},{12,8},{16,20},{20,16},{24,28},{28,24},{32,36},... | collective-permute-start | bytes 405512 | tf_op jit(solution)/shard_map/ppermute | solution.py:312
  56.9 0.0 collective-permute-done.16.refs_6_
  56.9 1.2 %last.2 = (bf16[256,1024]{1,0:T(8,128)(2,1)}, bf16[256,1024]{1,0:T(8,128)(2,1)}) custom-call(s32[1,256]{1,0:T(1,128)S(1)} %get-tuple-element.51.refs_0_, f32[256,1024]{1,0:T(8,128)S(1)} %get-tuple-element.87.refs_2_.refs_1_, f32[256,1024]{1,0:T(8,128)S(1)} %get-tuple-element.88.refs_2_, f32[264,128]{1,0:T(8,128)S(1)} %get-tuple-element.91.refs_3_, ...), custom_call_target="tpu_custom_call" | custom-call | tf_op jit(solution)/shard_map/last/pallas_call | solution.py:295
  58.1 0.0 collective-permute-done.13.refs_3_
  58.1 1.0 %last.3 = (bf16[256,1024]{1,0:T(8,128)(2,1)}, bf16[256,1024]{1,0:T(8,128)(2,1)}) custom-call(s32[1,256]{1,0:T(1,128)S(1)} %get-tuple-element.51.refs_0_, f32[256,1024]{1,0:T(8,128)S(1)} %get-tuple-element.87.refs_2_.refs_1_, f32[256,1024]{1,0:T(8,128)S(1)} %get-tuple-element.88.refs_2_, ...), custom_call_target="tpu_custom_call", output_to_operand_aliasing={{0}: (6, {}), {1}: (7, {})} | custom-call | tf_op jit(solution)/shard_map/last/pallas_call | solution.py:295
  (9 shorter events, 0.2 us)
Async XLA Ops:
  2.0 4.6 %collective-permute-start = (f32[520,128]{1,0:T(8,128)S(1)}, f32[520,128]{1,0:T(8,128)S(1)}, u32[]{:S(2)}, u32[]{:S(2)}) collective-permute-start(f32[520,128]{1,0:T(8,128)S(1)} %get-tuple-element.52.refs_3_), channel_id=1, source_target_pairs={{0,4},{4,0},{8,12},{12,8},{16,20},{20,16},{24,28},{28,24},{32,36},... | collective-permute-start | bytes 798728 | tf_op jit(solution)/shard_map/ppermute | solution.py:312
  6.7 9.9 %collective-permute-start.1 = (f32[264,128]{1,0:T(8,128)S(1)}, f32[264,128]{1,0:T(8,128)S(1)}, u32[]{:S(2)}, u32[]{:S(2)}) collective-permute-start(f32[264,128]{1,0:T(8,128)S(1)} %get-tuple-element.63.refs_0_), channel_id=1, source_target_pairs={{0,8},{4,12},{8,16},{12,20},{16,24},{20,28},{24,32},{28,36},{32,40... | collective-permute-start | bytes 405512 | tf_op jit(solution)/shard_map/ppermute | solution.py:315
  6.8 12.7 %collective-permute-start.4 = (f32[264,128]{1,0:T(8,128)S(1)}, f32[264,128]{1,0:T(8,128)S(1)}, u32[]{:S(2)}, u32[]{:S(2)}) collective-permute-start(f32[264,128]{1,0:T(8,128)S(1)} %get-tuple-element.58.refs_8_.refs_0_), channel_id=1, source_target_pairs={{0,8},{4,12},{8,16},{12,20},{16,24},{20,28},{24,32},{28,36},{32,40... | collective-permute-start | bytes 405512 | tf_op jit(solution)/shard_map/ppermute | solution.py:315
  16.7 7.3 %collective-permute-start.2 = (f32[264,128]{1,0:T(8,128)S(1)}, f32[264,128]{1,0:T(8,128)S(1)}, u32[]{:S(2)}, u32[]{:S(2)}) collective-permute-start(f32[264,128]{1,0:T(8,128)S(1)} %merge.4), channel_id=1, source_target_pairs={{0,8},{4,12},{8,16},{12,20},{16,24},{20,28},{24,32},{28,36},{32,40... | collective-permute-start | bytes 405512 | tf_op jit(solution)/shard_map/ppermute | solution.py:315
  19.6 8.0 %collective-permute-start.5 = (f32[264,128]{1,0:T(8,128)S(1)}, f32[264,128]{1,0:T(8,128)S(1)}, u32[]{:S(2)}, u32[]{:S(2)}) collective-permute-start(f32[264,128]{1,0:T(8,128)S(1)} %merge.5), channel_id=1, source_target_pairs={{0,8},{4,12},{8,16},{12,20},{16,24},{20,28},{24,32},{28,36},{32,40... | collective-permute-start | bytes 405512 | tf_op jit(solution)/shard_map/ppermute | solution.py:315
  23.9 5.2 %collective-permute-start.3 = (f32[264,128]{1,0:T(8,128)S(1)}, f32[264,128]{1,0:T(8,128)S(1)}, u32[]{:S(2)}, u32[]{:S(2)}) collective-permute-start(f32[264,128]{1,0:T(8,128)S(1)} %get-tuple-element.65), channel_id=1, source_target_pairs={{0,4},{4,0},{8,12},{12,8},{16,20},{20,16},{24,28},{28,24},{32,36},... | collective-permute-start | bytes 405512 | tf_op jit(solution)/shard_map/ppermute | solution.py:312
  27.6 2.6 %collective-permute-start.6 = (f32[264,128]{1,0:T(8,128)S(1)}, f32[264,128]{1,0:T(8,128)S(1)}, u32[]{:S(2)}, u32[]{:S(2)}) collective-permute-start(f32[264,128]{1,0:T(8,128)S(1)} %get-tuple-element.69), channel_id=1, source_target_pairs={{0,4},{4,0},{8,12},{12,8},{16,20},{20,16},{24,28},{28,24},{32,36},... | collective-permute-start | bytes 405512 | tf_op jit(solution)/shard_map/ppermute | solution.py:312
  30.7 5.0 %collective-permute-start.7 = (f32[8,256]{1,0:T(8,128)S(1)}, f32[8,256]{1,0:T(8,128)S(1)}, u32[]{:S(2)}, u32[]{:S(2)}) collective-permute-start(f32[8,256]{1,0:T(8,128)S(1)} %get-tuple-element.71.refs_5_), channel_id=1, source_target_pairs={{0,1},{1,2},{2,3},{3,0},{4,5},{5,6},{6,7},{7,4},{8,9},{9,10},{10,1... | collective-permute-start | bytes 24584 | tf_op jit(solution)/shard_map/ppermute | solution.py:398
  32.1 4.0 %collective-permute-start.8 = (f32[8,256]{1,0:T(8,128)S(1)}, f32[8,256]{1,0:T(8,128)S(1)}, u32[]{:S(2)}, u32[]{:S(2)}) collective-permute-start(f32[8,256]{1,0:T(8,128)S(1)} %get-tuple-element.71.refs_5_), channel_id=1, source_target_pairs={{0,2},{1,3},{2,0},{3,1},{4,6},{5,7},{6,4},{7,5},{8,10},{9,11},{10,... | collective-permute-start | bytes 24584 | tf_op jit(solution)/shard_map/ppermute | solution.py:398
  34.7 2.8 %collective-permute-start.9 = (f32[8,256]{1,0:T(8,128)S(1)}, f32[8,256]{1,0:T(8,128)S(1)}, u32[]{:S(2)}, u32[]{:S(2)}) collective-permute-start(f32[8,256]{1,0:T(8,128)S(1)} %get-tuple-element.71.refs_5_), channel_id=1, source_target_pairs={{0,3},{1,0},{2,1},{3,2},{4,7},{5,4},{6,5},{7,6},{8,11},{9,8},{10,9... | collective-permute-start | bytes 24584 | tf_op jit(solution)/shard_map/ppermute | solution.py:398
  37.9 3.0 %collective-permute-start.10 = (f32[520,128]{1,0:T(8,128)S(1)}, f32[520,128]{1,0:T(8,128)S(1)}, u32[]{:S(2)}, u32[]{:S(2)}) collective-permute-start(f32[520,128]{1,0:T(8,128)S(1)} %get-tuple-element.75.refs_12_), channel_id=1, source_target_pairs={{0,4},{4,0},{8,12},{12,8},{16,20},{20,16},{24,28},{28,24},{32,36},... | collective-permute-start | bytes 798728 | tf_op jit(solution)/shard_map/ppermute | solution.py:312
  41.0 4.8 %collective-permute-start.14 = (f32[264,128]{1,0:T(8,128)S(1)}, f32[264,128]{1,0:T(8,128)S(1)}, u32[]{:S(2)}, u32[]{:S(2)}) collective-permute-start(f32[264,128]{1,0:T(8,128)S(1)} %get-tuple-element.90.refs_0_), channel_id=1, source_target_pairs={{0,248},{4,252},{8,0},{12,4},{16,8},{20,12},{24,16},{28,20},{32,24... | collective-permute-start | bytes 405512 | tf_op jit(solution)/shard_map/ppermute | solution.py:315
  41.1 8.5 %collective-permute-start.11 = (f32[264,128]{1,0:T(8,128)S(1)}, f32[264,128]{1,0:T(8,128)S(1)}, u32[]{:S(2)}, u32[]{:S(2)}) collective-permute-start(f32[264,128]{1,0:T(8,128)S(1)} %get-tuple-element.84.refs_14_.refs_0_), channel_id=1, source_target_pairs={{0,248},{4,252},{8,0},{12,4},{16,8},{20,12},{24,16},{28,20},{32,24... | collective-permute-start | bytes 405512 | tf_op jit(solution)/shard_map/ppermute | solution.py:315
  45.8 6.6 %collective-permute-start.15 = (f32[264,128]{1,0:T(8,128)S(1)}, f32[264,128]{1,0:T(8,128)S(1)}, u32[]{:S(2)}, u32[]{:S(2)}) collective-permute-start(f32[264,128]{1,0:T(8,128)S(1)} %merge.7), channel_id=1, source_target_pairs={{0,248},{4,252},{8,0},{12,4},{16,8},{20,12},{24,16},{28,20},{32,24... | collective-permute-start | bytes 405512 | tf_op jit(solution)/shard_map/ppermute | solution.py:315
  49.6 5.9 %collective-permute-start.12 = (f32[264,128]{1,0:T(8,128)S(1)}, f32[264,128]{1,0:T(8,128)S(1)}, u32[]{:S(2)}, u32[]{:S(2)}) collective-permute-start(f32[264,128]{1,0:T(8,128)S(1)} %merge.6), channel_id=1, source_target_pairs={{0,248},{4,252},{8,0},{12,4},{16,8},{20,12},{24,16},{28,20},{32,24... | collective-permute-start | bytes 405512 | tf_op jit(solution)/shard_map/ppermute | solution.py:315
  52.5 4.4 %collective-permute-start.16 = (f32[264,128]{1,0:T(8,128)S(1)}, f32[264,128]{1,0:T(8,128)S(1)}, u32[]{:S(2)}, u32[]{:S(2)}) collective-permute-start(f32[264,128]{1,0:T(8,128)S(1)} %get-tuple-element.92), channel_id=1, source_target_pairs={{0,4},{4,0},{8,12},{12,8},{16,20},{20,16},{24,28},{28,24},{32,36},... | collective-permute-start | bytes 405512 | tf_op jit(solution)/shard_map/ppermute | solution.py:312
  55.5 2.6 %collective-permute-start.13 = (f32[264,128]{1,0:T(8,128)S(1)}, f32[264,128]{1,0:T(8,128)S(1)}, u32[]{:S(2)}, u32[]{:S(2)}) collective-permute-start(f32[264,128]{1,0:T(8,128)S(1)} %get-tuple-element.89), channel_id=1, source_target_pairs={{0,4},{4,0},{8,12},{12,8},{16,20},{20,16},{24,28},{28,24},{32,36},... | collective-permute-start | bytes 405512 | tf_op jit(solution)/shard_map/ppermute | solution.py:312
